TPU v7x, 32 devices: a whole 2x2x4 slice. The times are simulated.
32 devices in a mesh: dp: 8 (over z, x), mp: 4 (over y, core).
Axes of the slice: x: 2, y: 2, z: 4, core: 2. Of those that a mesh axis runs over, the one named last changes fastest.
Arguments:
- tokens: float32 [32, 196, 512], P('dp'), may hold values from -6 to 6
- cotangent: float32 [32, 196, 512], P('dp'), may hold values from -6 to 6
- counts: int32 [8], P('dp'), may hold values from 2 to 4, as said below
- inwards: float32 [2, 3, 512, 512], P(None, None, 'dp', 'mp'), may hold values from -0.25 to 0.25
- inbias: float32 [2, 2, 512], P(None, None, 'mp'), may hold values from -3 to 3
- relative: float32 [2, 169, 16], P(None, None, 'mp'), may hold values from -3 to 322
- outwards: float32 [2, 512, 512], P(None, 'mp', 'dp'), may hold values from -0.75 to 0.75
- widening: float32 [2, 512, 2048], P(None, 'dp', 'mp'), may hold values from -0.25 to 0.25
- widebias: float32 [2, 2048], P(None, 'mp'), may hold values from -3 to 3
- narrowing: float32 [2, 2048, 512], P(None, 'mp', 'dp'), may hold values from -0.125 to 0.125
- norm_gains: float32 [2, 2, 512], replicated, may hold values from 0.1 to 1.9
- offsets: float32 [2, 4, 512], replicated, may hold values from -3 to 3
- mean_inwards: float32 [2, 3, 512, 512], P(None, None, 'dp', 'mp'), may hold values from -6 to 6
- mean_inbias: float32 [2, 2, 512], P(None, None, 'mp'), may hold values from -6 to 6
- mean_relative: float32 [2, 169, 16], P(None, None, 'mp'), may hold values from -6 to 6
- mean_outwards: float32 [2, 512, 512], P(None, 'mp', 'dp'), may hold values from -6 to 6
- mean_widening: float32 [2, 512, 2048], P(None, 'dp', 'mp'), may hold values from -6 to 6
- mean_widebias: float32 [2, 2048], P(None, 'mp'), may hold values from -6 to 6
- mean_narrowing: float32 [2, 2048, 512], P(None, 'mp', 'dp'), may hold values from -6 to 6
- mean_gains: float32 [2, 2, 512], replicated, may hold values from -6 to 6
- mean_offsets: float32 [2, 4, 512], replicated, may hold values from -6 to 6
- square_inwards: float32 [2, 3, 512, 512], P(None, None, 'dp', 'mp'), may hold values from 0.6272 to 62.72
- square_inbias: float32 [2, 2, 512], P(None, None, 'mp'), may hold values from 0.6272 to 62.72
- square_relative: float32 [2, 169, 16], P(None, None, 'mp'), may hold values from 0.6272 to 6.272
- square_outwards: float32 [2, 512, 512], P(None, 'mp', 'dp'), may hold values from 0.6272 to 6.272
- square_widening: float32 [2, 512, 2048], P(None, 'dp', 'mp'), may hold values from 0.6272 to 6.272
- square_widebias: float32 [2, 2048], P(None, 'mp'), may hold values from 0.6272 to 6.272
- square_narrowing: float32 [2, 2048, 512], P(None, 'mp', 'dp'), may hold values from 0.6272 to 6.272
- square_gains: float32 [2, 2, 512], replicated, may hold values from 0.6272 to 62.72
- square_offsets: float32 [2, 4, 512], replicated, may hold values from 0.6272 to 62.72
Outputs:
- output: float32 [32, 196, 512], P('dp')
- grad_tokens: float32 [32, 196, 512], P('dp')
- grad_inwards: float32 [2, 3, 512, 512], P(None, None, 'dp', 'mp')
- grad_inbias: float32 [2, 2, 512], P(None, None, 'mp')
- grad_relative: float32 [2, 169, 16], P(None, None, 'mp')
- grad_outwards: float32 [2, 512, 512], P(None, 'mp', 'dp')
- grad_widening: float32 [2, 512, 2048], P(None, 'dp', 'mp')
- grad_widebias: float32 [2, 2048], P(None, 'mp')
- grad_narrowing: float32 [2, 2048, 512], P(None, 'mp', 'dp')
- grad_gains: float32 [2, 2, 512], replicated
- grad_offsets: float32 [2, 4, 512], replicated
- next_inwards: float32 [2, 3, 512, 512], P(None, None, 'dp', 'mp')
- next_inbias: float32 [2, 2, 512], P(None, None, 'mp')
- next_relative: float32 [2, 169, 16], P(None, None, 'mp')
- next_outwards: float32 [2, 512, 512], P(None, 'mp', 'dp')
- next_widening: float32 [2, 512, 2048], P(None, 'dp', 'mp')
- next_widebias: float32 [2, 2048], P(None, 'mp')
- next_narrowing: float32 [2, 2048, 512], P(None, 'mp', 'dp')
- next_gains: float32 [2, 2, 512], replicated
- next_offsets: float32 [2, 4, 512], replicated
- nextmean_inwards: float32 [2, 3, 512, 512], P(None, None, 'dp', 'mp')
- nextmean_inbias: float32 [2, 2, 512], P(None, None, 'mp')
- nextmean_relative: float32 [2, 169, 16], P(None, None, 'mp')
- nextmean_outwards: float32 [2, 512, 512], P(None, 'mp', 'dp')
- nextmean_widening: float32 [2, 512, 2048], P(None, 'dp', 'mp')
- nextmean_widebias: float32 [2, 2048], P(None, 'mp')
- nextmean_narrowing: float32 [2, 2048, 512], P(None, 'mp', 'dp')
- nextmean_gains: float32 [2, 2, 512], replicated
- nextmean_offsets: float32 [2, 4, 512], replicated
- nextsquare_inwards: float32 [2, 3, 512, 512], P(None, None, 'dp', 'mp')
- nextsquare_inbias: float32 [2, 2, 512], P(None, None, 'mp')
- nextsquare_relative: float32 [2, 169, 16], P(None, None, 'mp')
- nextsquare_outwards: float32 [2, 512, 512], P(None, 'mp', 'dp')
- nextsquare_widening: float32 [2, 512, 2048], P(None, 'dp', 'mp')
- nextsquare_widebias: float32 [2, 2048], P(None, 'mp')
- nextsquare_narrowing: float32 [2, 2048, 512], P(None, 'mp', 'dp')
- nextsquare_gains: float32 [2, 2, 512], replicated
- nextsquare_offsets: float32 [2, 4, 512], replicated
Inputs may be any that keep to these rules, and one draw needn't show every extreme that they name: Each dp index holds counts real images in its first slots; some index holds 4.
All inputs are finite; a program needn't handle non-finite values.
Results may differ from a plain program's by a relative error of at most 0.025.
Values may be sent and summed in bfloat16 or wider, within the bound.
No kernel may reach another device: no remote copies, remote signals or barrier semaphores. Data moves between devices by JAX's collectives and lax.ppermute only.
A program may use at most 128 MiB of HBM per device.

v0:
```python
import jax
import jax.numpy as jnp
import numpy as np
from jax import lax
from jax.experimental import pallas as pl
from jax.experimental.pallas import tpu as pltpu
from jax.sharding import Mesh
from jax.sharding import PartitionSpec as P


HEAD_DIM = 32
WIN = 7
SIDE = 14
SHIFT = 3
STEP = 3

norm_eps = 1e-05
beta_one = 0.9
beta_two = 0.999
learn_rate = 0.02
decay_rate = 0.05
adam_eps = 1e-08

CELLS = WIN * WIN
PANES = (SIDE // WIN) ** 2
SLOT = 64
GROUPS = 2
DIRECT_MAX = 8
UNROLL = 2
ROWS = -(-SIDE * SIDE // 8) * 8
VMEM_BYTES = 60 * 1024 * 1024
f32 = jnp.float32
bf16 = jnp.bfloat16


def window_order(shifted):
    grid = np.arange(SIDE * SIDE).reshape(SIDE, SIDE)
    if shifted:
        grid = np.roll(grid, (-SHIFT, -SHIFT), axis=(0, 1))
    side_panes = SIDE // WIN
    return grid.reshape(side_panes, WIN, side_panes, WIN).transpose(0, 2, 1, 3).reshape(-1, CELLS)


def selection(shifted, images):
    source = np.full((images, PANES, SLOT), -1, np.int32)
    for i in range(images):
        source[i, :, :CELLS] = window_order(shifted) + i * ROWS
    wanted = jnp.asarray(source.reshape(-1, 1))
    return (wanted == jnp.arange(images * ROWS, dtype=jnp.int32)[None, :]).astype(bf16)


def lookup_onehot():
    places = np.arange(CELLS)
    rowpos, colpos = places // WIN, places % WIN
    lookup = (rowpos[:, None] - rowpos[None, :] + WIN - 1) * (2 * WIN - 1) + (
        colpos[:, None] - colpos[None, :] + WIN - 1
    )
    full = np.full((SLOT, SLOT), -1, np.int32)
    full[:CELLS, :CELLS] = lookup
    entries = jnp.arange((2 * WIN - 1) ** 2, dtype=jnp.int32)
    return (entries[:, None] == jnp.asarray(full.reshape(1, -1))).astype(f32)


def pane_mask(shifted):
    pad = np.zeros((SLOT, SLOT), np.float32)
    pad[:, CELLS:] = -1e30
    if not shifted:
        return pad[None]
    coords = np.arange(SIDE)
    stripe = (coords >= SIDE - WIN).astype(int) + (coords >= SIDE - SHIFT).astype(int)
    region = (stripe[:, None] * 3 + stripe[None, :]).reshape(-1)
    side_panes = SIDE // WIN
    per = region.reshape(side_panes, WIN, side_panes, WIN).transpose(0, 2, 1, 3).reshape(-1, CELLS)
    out = np.repeat(pad[None], PANES, axis=0)
    out[:, :CELLS, :CELLS] = np.where(per[:, :, None] != per[:, None, :], -100.0, 0.0)
    return out


def dot(left, right, lc, rc):
    return lax.dot_general(left, right, (((lc,), (rc,)), ((), ())), preferred_element_type=f32)


def unit_norm(hidden):
    centered = hidden - jnp.mean(hidden, axis=-1, keepdims=True)
    inverse = lax.rsqrt(jnp.mean(centered * centered, axis=-1, keepdims=True) + norm_eps)
    return centered * inverse, inverse


def norm_back(upstream, normed, inverse, gain):
    d_normed = upstream * gain
    source = inverse * (
        d_normed
        - jnp.mean(d_normed, axis=-1, keepdims=True)
        - normed * jnp.mean(d_normed * normed, axis=-1, keepdims=True)
    )
    return source, jnp.sum(upstream * normed, axis=0, keepdims=True), jnp.sum(
        upstream, axis=0, keepdims=True
    )


def head_masks(width):
    lane = lax.broadcasted_iota(jnp.int32, (1, width), 1) // HEAD_DIM
    return [lane == head for head in range(width // HEAD_DIM)]


def spread(value, masks):
    zero = jnp.zeros_like(value)
    return jnp.concatenate([jnp.where(mask, value, zero) for mask in masks], axis=0)


def gather_heads(stacked, masks):
    total = None
    for head, mask in enumerate(masks):
        part = jnp.where(mask, stacked[head * SLOT : (head + 1) * SLOT], 0.0)
        total = part if total is None else total + part
    return total


def call(kernel, outs, *args, scratch=(), scalars=0):
    specs = [pl.BlockSpec(memory_space=pltpu.SMEM)] * scalars
    specs += [pl.BlockSpec(memory_space=pltpu.VMEM)] * (len(args) - scalars)
    return pl.pallas_call(
        kernel,
        in_specs=specs,
        out_shape=[jax.ShapeDtypeStruct(shape, dtype) for shape, dtype in outs],
        scratch_shapes=[pltpu.VMEM(shape, dtype) for shape, dtype in scratch],
        compiler_params=pltpu.CompilerParams(vmem_limit_bytes=VMEM_BYTES),
    )(*args)


def load_images(place_ref, images_ref, buffer, images):
    cells, width = images_ref.shape[1:]
    for i in range(images):
        buffer[i * ROWS : i * ROWS + cells, :] = images_ref[place_ref[0] * images + i]
        buffer[i * ROWS + cells : (i + 1) * ROWS, :] = jnp.zeros((ROWS - cells, width), f32)


def store_images(value, out, images):
    cells = out.shape[1]
    for i in range(images):
        out[i] = value[i * ROWS : i * ROWS + cells, :]


def attn_fwd(layer, gains, offsets, source, weights, bias_qv, pos, pick):
    first = layer == 0
    win_rows, rows = pick.shape
    width = weights[0].shape[0]
    panes = win_rows // SLOT
    local = weights[0].shape[1] // 4
    heads = local // HEAD_DIM
    masks_n = pos.shape[0]
    factor = HEAD_DIM ** (-0.5)
    n_src = len(source)

    def kernel(*refs):
        src = refs[:n_src]
        gain_ref, off_ref, w0, w1, bias_ref, pos_ref, pick_ref = refs[n_src : n_src + 7]
        h_ref, a_ref, q_ref, k_ref, v_ref, prob_ref, mixed_ref, part_ref, mw_ref = refs[n_src + 7 :]
        if first:
            load_images(src[0], src[1], h_ref, rows // ROWS)
            hidden = h_ref[...]
        else:
            hidden = src[0][...] + (
                src[1][...].astype(f32) + src[2][...].astype(f32) + off_ref[layer - 1, 3:4]
            )
            h_ref[...] = hidden
        normed, _ = unit_norm(hidden)
        a = (normed * gain_ref[layer, 0:1] + off_ref[layer, 0:1]).astype(bf16)
        a_ref[...] = a
        a_win = dot(pick_ref[...], a, 1, 0).astype(bf16)
        for g, w in enumerate((w0, w1)):
            proj = dot(a_win, w[:, : 3 * local], 1, 0)
            q = ((proj[:, :local] + bias_ref[0:1, g * local : (g + 1) * local]) * factor).astype(bf16)
            k = proj[:, local : 2 * local].astype(bf16)
            v = (proj[:, 2 * local :] + bias_ref[1:2, g * local : (g + 1) * local]).astype(bf16)
            q_ref[g] = q.reshape(panes, SLOT, local)
            k_ref[g] = k.reshape(panes, SLOT, local)
            v_ref[g] = v.reshape(panes, SLOT, local)
        masks = head_masks(local)

        def step(w, carry):
            for g in range(GROUPS):
                q, k, v = q_ref[g, w], k_ref[g, w], v_ref[g, w]
                score = dot(spread(q, masks), k, 1, 1) + pos_ref[w % masks_n if masks_n > 1 else 0, g]
                top = jnp.max(score, axis=-1, keepdims=True)
                grown = jnp.exp(score - top)
                prob = grown * (1.0 / jnp.sum(grown, axis=-1, keepdims=True))
                prob_ref[w, g] = prob
                mixed = gather_heads(dot(prob.astype(bf16), v, 1, 0), masks)
                mw_ref[w, :, g * local : (g + 1) * local] = mixed.astype(bf16)
            return carry

        lax.fori_loop(0, panes, step, 0, unroll=UNROLL)
        mixed = dot(pick_ref[...], mw_ref[...].reshape(win_rows, GROUPS * local), 0, 0).astype(bf16)
        mixed_ref[...] = mixed
        part = None
        for g, w in enumerate((w0, w1)):
            term = dot(mixed[:, g * local : (g + 1) * local], w[:, 3 * local :], 1, 1)
            part = term if part is None else part + term
        part_ref[...] = part.astype(bf16)

    outs = [
        ((rows, width), f32),
        ((rows, width), bf16),
        ((GROUPS, panes, SLOT, local), bf16),
        ((GROUPS, panes, SLOT, local), bf16),
        ((GROUPS, panes, SLOT, local), bf16),
        ((panes, GROUPS, heads * SLOT, SLOT), f32),
        ((rows, GROUPS * local), bf16),
        ((rows, width), bf16),
    ]
    return call(
        kernel,
        outs,
        *source,
        gains,
        offsets,
        *weights,
        bias_qv,
        pos,
        pick,
        scratch=[((panes, SLOT, GROUPS * local), bf16)],
        scalars=1 if first else 0,
    )


def mlp_fwd(layer, hidden, own, recv, gains, offsets, weights, wide_bias):
    rows, width = hidden.shape
    local = weights[0].shape[1] // 2

    def kernel(
        h_ref, own_ref, recv_ref, gain_ref, off_ref, w0, w1, wb_ref, h1_ref, c_ref, z_ref, s_ref, p_ref
    ):
        h1 = h_ref[...] + (own_ref[...].astype(f32) + recv_ref[...].astype(f32) + off_ref[layer, 2:3])
        h1_ref[...] = h1
        normed, _ = unit_norm(h1)
        c = (normed * gain_ref[layer, 1:2] + off_ref[layer, 1:2]).astype(bf16)
        c_ref[...] = c
        part = None
        for g, w in enumerate((w0, w1)):
            u = dot(c, w[:, :local], 1, 0) + wb_ref[g : g + 1, :]
            cdf = 0.5 * (1.0 + lax.erf(u * 0.7071067811865476))
            density = jnp.exp(-0.5 * u * u) * 0.3989422804014327
            z = (u * cdf).astype(bf16)
            z_ref[:, g * local : (g + 1) * local] = z
            s_ref[:, g * local : (g + 1) * local] = (cdf + u * density).astype(bf16)
            term = dot(z, w[:, local:], 1, 1)
            part = term if part is None else part + term
        p_ref[...] = part.astype(bf16)

    outs = [
        ((rows, width), f32),
        ((rows, width), bf16),
        ((rows, GROUPS * local), bf16),
        ((rows, GROUPS * local), bf16),
        ((rows, width), bf16),
    ]
    return call(kernel, outs, hidden, own, recv, gains, offsets, *weights, wide_bias)


def mlp_bwd(layer, last, source, gains, offsets, slope, weights):
    rows, width = source[3].shape
    local = weights[0].shape[1] // 2
    n_src = len(source)

    def kernel(*refs):
        src = refs[:n_src]
        gain_ref, off_ref, s_ref, w0, w1 = refs[n_src : n_src + 5]
        g_ref, gb_ref, du_ref, p_ref, sum_ref = refs[n_src + 5 : n_src + 10]
        sum_ref[...] = jnp.zeros_like(sum_ref)
        if last:
            place_ref, count_ref = src[:2]
            images = rows // ROWS
            load_images(place_ref, src[2], g_ref, images)
            result = src[3][...] + (src[4][...].astype(f32) + src[5][...].astype(f32) + off_ref[layer, 3:4])
            out_ref = refs[n_src + 10]
            cells = out_ref.shape[1]
            for i in range(images):
                keep = jnp.where(place_ref[0] * images + i < count_ref[0], 1.0, 0.0)
                out_ref[i] = result[i * ROWS : i * ROWS + cells, :] * keep
                g_ref[i * ROWS : (i + 1) * ROWS, :] = g_ref[i * ROWS : (i + 1) * ROWS, :] * keep
            grad = g_ref[...]
        else:
            normed, inverse = unit_norm(src[3][...])
            upstream = src[1][...].astype(f32) + src[2][...].astype(f32)
            first_grad, d_gain, d_off = norm_back(
                upstream, normed, inverse, gain_ref[layer + 1, 0:1]
            )
            grad = src[0][...] + first_grad
            sum_ref[1:2, :] = d_gain
            sum_ref[2:3, :] = d_off
            g_ref[...] = grad
        sum_ref[0:1, :] = jnp.sum(grad, axis=0, keepdims=True)
        grad_b = grad.astype(bf16)
        gb_ref[...] = grad_b
        part = None
        for g, w in enumerate((w0, w1)):
            du = dot(grad_b, w[:, local:], 1, 0) * s_ref[:, g * local : (g + 1) * local].astype(f32)
            sum_ref[3 + g : 4 + g, :local] = jnp.sum(du, axis=0, keepdims=True)
            du_b = du.astype(bf16)
            du_ref[:, g * local : (g + 1) * local] = du_b
            term = dot(du_b, w[:, :local], 1, 1)
            part = term if part is None else part + term
        p_ref[...] = part.astype(bf16)

    outs = [
        ((rows, width), f32),
        ((rows, width), bf16),
        ((rows, GROUPS * local), bf16),
        ((rows, width), bf16),
        ((8, width), f32),
    ]
    if last:
        outs.append(((rows // ROWS, source[2].shape[1], width), f32))
    return call(kernel, outs, *source, gains, offsets, slope, *weights, scalars=2 if last else 0)


def grad_outs(width, cols, halves):
    if not halves:
        return [((width, cols), bf16)] * 2
    half = width // halves
    return [((half, cols), bf16), ((half, cols), bf16), ((halves, half, cols), bf16)]


def cut(full, outs, place_ref, halves, slab):
    if not halves:
        outs[0][...] = full[...]
        return
    deep = full.shape[0] // (halves * slab)
    for x in range(halves):
        for z in range(deep):
            block = (z ^ place_ref[1]) * halves + (x ^ place_ref[2])
            start = pl.multiple_of(block * slab, slab)
            target = outs[x] if len(outs) > 1 else outs[0].at[x]
            target[z * slab : (z + 1) * slab, :] = full[pl.ds(start, slab), :]


def mlp_grads(place, c, du_b, z, grad_b, halves, slab):
    width = c.shape[1]
    local = z.shape[1] // GROUPS

    def kernel(place_ref, c_ref, du_ref, z_ref, g_ref, *outs):
        full = outs[-1]
        for g, out in enumerate((outs[:-2], outs[-2:-1])):
            cols = slice(g * local, (g + 1) * local)
            full[:, :local] = dot(c_ref[...], du_ref[:, cols], 0, 0).astype(bf16)
            full[:, local:] = dot(g_ref[...], z_ref[:, cols], 0, 0).astype(bf16)
            cut(full, out, place_ref, halves, slab)

    return call(
        kernel,
        grad_outs(width, 2 * local, halves),
        place,
        c,
        du_b,
        z,
        grad_b,
        scratch=[((width, 2 * local), bf16)],
        scalars=1,
    )


def attn_bwd(layer, grad, own, recv, h1, gains, weights, q, k, v, prob, pick):
    rows, width = grad.shape
    win_rows = pick.shape[0]
    panes = win_rows // SLOT
    local = weights[0].shape[1] // 4
    heads = local // HEAD_DIM
    factor = HEAD_DIM ** (-0.5)

    def kernel(
        g_ref, own_ref, recv_ref, h1_ref, gain_ref, w0, w1, q_ref, k_ref, v_ref, prob_ref, pick_ref,
        dh_ref, dhb_ref, dp_ref, part_ref, sum_ref, ds_ref, dm_ref, dw_ref, bias_ref,
    ):
        normed, inverse = unit_norm(h1_ref[...])
        upstream = own_ref[...].astype(f32) + recv_ref[...].astype(f32)
        d_mid, d_gain, d_off = norm_back(upstream, normed, inverse, gain_ref[layer, 1:2])
        dh1 = g_ref[...] + d_mid
        dh_ref[...] = dh1
        sum_ref[...] = jnp.zeros_like(sum_ref)
        sum_ref[0:1, :] = d_gain
        sum_ref[1:2, :] = d_off
        sum_ref[2:3, :] = jnp.sum(dh1, axis=0, keepdims=True)
        dh_b = dh1.astype(bf16)
        dhb_ref[...] = dh_b
        for g, w in enumerate((w0, w1)):
            d_mixed = dot(dh_b, w[:, 3 * local :], 1, 0).astype(bf16)
            d_win = dot(pick_ref[...], d_mixed, 1, 0).astype(bf16)
            dm_ref[g] = d_win.reshape(panes, SLOT, local)
        ds_ref[...] = jnp.zeros_like(ds_ref)
        bias_ref[...] = jnp.zeros_like(bias_ref)
        masks = head_masks(local)

        def step(w, carry):
            for g in range(GROUPS):
                keys, values = k_ref[g, w], v_ref[g, w]
                d_out = spread(dm_ref[g, w], masks)
                queries = spread(q_ref[g, w], masks)
                probs = prob_ref[w, g]
                d_prob = dot(d_out, values, 1, 1)
                d_value = dot(probs.astype(bf16), d_out, 0, 0)
                d_score = probs * (d_prob - jnp.sum(probs * d_prob, axis=-1, keepdims=True))
                ds_ref[g] += d_score
                d_score_b = d_score.astype(bf16)
                d_query = gather_heads(dot(d_score_b, keys, 1, 0), masks) * factor
                d_key = dot(d_score_b, queries, 0, 0)
                base = g * 3 * local
                dw_ref[w, :, base : base + local] = d_query.astype(bf16)
                dw_ref[w, :, base + local : base + 2 * local] = d_key.astype(bf16)
                dw_ref[w, :, base + 2 * local : base + 3 * local] = d_value.astype(bf16)
                bias_ref[0:1, g * local : (g + 1) * local] += jnp.sum(d_query, axis=0, keepdims=True)
                bias_ref[1:2, g * local : (g + 1) * local] += jnp.sum(d_value, axis=0, keepdims=True)
            return carry

        lax.fori_loop(0, panes, step, 0, unroll=UNROLL)
        sum_ref[3:4, : GROUPS * local] = bias_ref[0:1, :]
        sum_ref[4:5, : GROUPS * local] = bias_ref[1:2, :]
        d_proj = dot(
            pick_ref[...], dw_ref[...].reshape(win_rows, GROUPS * 3 * local), 0, 0
        ).astype(bf16)
        dp_ref[...] = d_proj
        part = None
        for g, w in enumerate((w0, w1)):
            term = dot(d_proj[:, g * 3 * local : (g + 1) * 3 * local], w[:, : 3 * local], 1, 1)
            part = term if part is None else part + term
        part_ref[...] = part.astype(bf16)

    outs = [
        ((rows, width), f32),
        ((rows, width), bf16),
        ((rows, GROUPS * 3 * local), bf16),
        ((rows, width), bf16),
        ((8, width), f32),
        ((GROUPS, heads * SLOT, SLOT), f32),
    ]
    return call(
        kernel,
        outs,
        grad,
        own,
        recv,
        h1,
        gains,
        *weights,
        q,
        k,
        v,
        prob,
        pick,
        scratch=[
            ((GROUPS, panes, SLOT, local), bf16),
            ((panes, SLOT, GROUPS * 3 * local), bf16),
            ((8, GROUPS * local), f32),
        ],
    )


def attn_grads(place, a, d_proj, mixed, dh_b, halves, slab):
    width = a.shape[1]
    local = mixed.shape[1] // GROUPS

    def kernel(place_ref, a_ref, dp_ref, m_ref, g_ref, *outs):
        full = outs[-1]
        for g, out in enumerate((outs[:-2], outs[-2:-1])):
            full[:, : 3 * local] = dot(
                a_ref[...], dp_ref[:, g * 3 * local : (g + 1) * 3 * local], 0, 0
            ).astype(bf16)
            full[:, 3 * local :] = dot(
                g_ref[...], m_ref[:, g * local : (g + 1) * local], 0, 0
            ).astype(bf16)
            cut(full, out, place_ref, halves, slab)

    return call(
        kernel,
        grad_outs(width, 4 * local, halves),
        place,
        a,
        d_proj,
        mixed,
        dh_b,
        scratch=[((width, 4 * local), bf16)],
        scalars=1,
    )


def tail(dh1, own, recv, hidden, gains, cells):
    rows, width = dh1.shape
    images = rows // ROWS

    def kernel(d_ref, own_ref, recv_ref, h_ref, gain_ref, o_ref, sum_ref):
        normed, inverse = unit_norm(h_ref[...])
        upstream = own_ref[...].astype(f32) + recv_ref[...].astype(f32)
        first_grad, d_gain, d_off = norm_back(upstream, normed, inverse, gain_ref[0, 0:1])
        store_images(d_ref[...] + first_grad, o_ref, images)
        sum_ref[...] = jnp.zeros_like(sum_ref)
        sum_ref[1:2, :] = d_gain
        sum_ref[2:3, :] = d_off

    outs = [((images, cells, width), f32), ((8, width), f32)]
    return call(kernel, outs, dh1, own, recv, hidden, gains)


def order(blocks, place, member):
    rows, cols = blocks[0].shape

    def kernel(place_ref, *refs):
        out = refs[-1]
        for s in range(len(blocks)):
            start = pl.multiple_of((place_ref[member] ^ s) * rows, rows)
            out[pl.ds(start, rows), :] = refs[s][...]

    outs = [((rows * len(blocks), cols), blocks[0].dtype)]
    return call(kernel, outs, place, *blocks, scalars=1)[0]


def pack(inwards, outwards, widening, narrowing):
    layers, _, slab, local = inwards.shape
    hidden = widening.shape[2]

    def kernel(in_ref, out_ref, wide_ref, narrow_ref, *packed):
        for l in range(layers):
            part_a, part_b = packed[2 * l : 2 * l + 2]
            for j in range(3):
                part_a[:, j * local : (j + 1) * local] = in_ref[l, j].astype(bf16)
            part_a[:, 3 * local :] = out_ref[l].astype(bf16)
            part_b[:, :hidden] = wide_ref[l].astype(bf16)
            part_b[:, hidden:] = narrow_ref[l].astype(bf16)

    outs = [((slab, 4 * local), bf16), ((slab, 2 * hidden), bf16)] * layers
    return call(kernel, outs, inwards, outwards, widening, narrowing)


def adam_pair(parts, first, second, turned):
    layers = len(parts)
    counts = [len(p) for p in parts]
    flat = [p for layer in parts for p in layer]
    stacked = first[0].ndim == 4

    def kernel(*refs):
        blocks, rest = refs[: len(flat)], refs[len(flat) :]
        one, two, out_one, out_two = rest[:3], rest[3:6], rest[6:10], rest[10:14]
        at = 0

        def update(index, gradient, ins, outs):
            weight, mean, square = (r[index] for r in ins)
            new = adam_update(weight, gradient, mean, square, decay_rate)
            outs[0][index] = gradient
            for ref, value in zip(outs[1:], new):
                ref[index] = value

        for l in range(layers):
            terms = [blocks[at + i][...].astype(f32) for i in range(counts[l])]
            at += counts[l]
            total = tree(terms)
            split = total.shape[1] - turned
            if stacked:
                piece = split // one[0].shape[1]
                for j in range(one[0].shape[1]):
                    update((l, j), total[:, j * piece : (j + 1) * piece], one, out_one)
            else:
                update((l,), total[:, :split], one, out_one)
            update((l,), total[:, split:], two, out_two)

    outs = [(first[0].shape, f32)] * 4 + [(second[0].shape, f32)] * 4
    res = call(kernel, outs, *flat, *first, *second)
    return res[:4], res[4:]


def small_rows(layers, heads):
    per = 8 + heads
    return per, -(-layers * per // 8) * 8


def small_pack(sums_mlp, sums_attn, sums_tail, tables, local):
    layers = len(tables)
    heads = tables[0].shape[0] // GROUPS
    entries = tables[0].shape[1]
    width = sums_mlp[0].shape[1]
    per, rows = small_rows(layers, heads)

    def kernel(*refs):
        ins, outs = refs[:-GROUPS], refs[-GROUPS:]
        for g, out in enumerate(outs):
            out[...] = jnp.zeros_like(out)
            for l in range(layers):
                mlp, attn, late, table = ins[4 * l : 4 * l + 4]
                base = l * per
                out[base : base + 1, :] = late[1:2, :]
                out[base + 1 : base + 2, :] = attn[0:1, :]
                out[base + 2 : base + 3, :] = late[2:3, :]
                out[base + 3 : base + 4, :] = attn[1:2, :]
                out[base + 4 : base + 5, :] = attn[2:3, :]
                out[base + 5 : base + 6, :] = mlp[0:1, :]
                out[base + 6 : base + 7, :] = mlp[3 + g : 4 + g, :]
                out[base + 7 : base + 8, :local] = attn[3:4, g * local : (g + 1) * local]
                out[base + 7 : base + 8, local : 2 * local] = attn[4:5, g * local : (g + 1) * local]
                out[base + 8 : base + 8 + heads, :entries] = table[g * heads : (g + 1) * heads, :]

    flat = [v for quad in zip(sums_mlp, sums_attn, sums_tail, tables) for v in quad]
    return call(kernel, [((rows, width), f32)] * GROUPS, *flat)


def small_adam(total, states):
    layers, _, local = states[0][0].shape
    heads, entries = states[1][0].shape[1:]
    hidden = states[2][0].shape[1]
    width = states[3][0].shape[2]
    per, _ = small_rows(layers, heads)

    def kernel(total_ref, *refs):
        ins, outs = refs[:15], refs[15:]

        def update(member, index, gradient):
            weight, mean, square = (r[index] for r in ins[3 * member : 3 * member + 3])
            new = (gradient,) + adam_update(weight, gradient, mean, square, 0.0)
            for ref, value in zip(outs[4 * member : 4 * member + 4], new):
                ref[index] = value

        for l in range(layers):
            base = l * per
            for row in range(2):
                update(
                    0,
                    (l, slice(row, row + 1)),
                    total_ref[base + 7 : base + 8, row * local : (row + 1) * local],
                )
            update(1, (l,), total_ref[base + 8 : base + 8 + heads, :entries])
            update(2, (slice(l, l + 1),), total_ref[base + 6 : base + 7, :hidden])
            update(3, (l,), total_ref[base : base + 2, :width])
            update(4, (l,), total_ref[base + 2 : base + 6, :width])

    outs = [(state[0].shape, f32) for state in states for _ in range(4)]
    res = call(kernel, outs, total, *[v for state in states for v in state])
    return [res[4 * m : 4 * m + 4] for m in range(5)]


def adam_update(weight, gradient, moment_one, second, decay_on):
    first_new = beta_one * moment_one + (1.0 - beta_one) * gradient
    second_new = beta_two * second + (1.0 - beta_two) * gradient * gradient
    first_hat = first_new / (1.0 - beta_one**STEP)
    second_hat = second_new / (1.0 - beta_two**STEP)
    updated = weight - learn_rate * (
        first_hat / (jnp.sqrt(second_hat) + adam_eps) + decay_on * weight
    )
    return (updated, first_new, second_new)


def turn(x):
    return jnp.swapaxes(x, 1, 2)


def tree(parts):
    while len(parts) > 1:
        parts = [parts[i] + parts[i + 1] for i in range(0, len(parts), 2)]
    return parts[0]


def step(*args):
    (tokens, cotangent, counts), params = args[:3], list(args[3:12])
    first_moments, second_moments = list(args[12:21]), list(args[21:30])
    inwards, inbias, relative, outwards, widening, widebias, narrowing, gains, offsets = params
    layer_total = inwards.shape[0]
    slots, cells, _ = tokens.shape
    images = slots // 2
    local = inwards.shape[3]
    hidden_local = widening.shape[2]
    heads = local // HEAD_DIM
    slab = inwards.shape[2]
    n_x = lax.axis_size("x")
    n_z = lax.axis_size("z")
    direct = n_x == 2 and n_x * n_z <= DIRECT_MAX and n_z & (n_z - 1) == 0
    halves = n_x if direct else 0
    c_index = lax.axis_index("c")
    place = jnp.stack(
        [
            c_index,
            lax.axis_index("z"),
            lax.axis_index("x"),
            lax.axis_index("z") * n_x + lax.axis_index("x"),
        ]
    ).astype(jnp.int32)
    dp = ("z", "x")

    def swap(x, axis):
        return lax.ppermute(x, axis, [(0, 1), (1, 0)])

    def xor_z(x, s):
        return lax.ppermute(x, "z", [(i, i ^ s) for i in range(n_z)])

    def xor_dp(x, s):
        return lax.ppermute(x, dp, [(i, i ^ s) for i in range(n_x * n_z)])

    def gather_now(p):
        if not direct:
            return lax.all_gather(p, dp, axis=0, tiled=True)
        blocks = [p] + [xor_dp(p, s) for s in range(1, n_x * n_z)]
        return order(blocks, place, 3)

    def gather_staged(p):
        if not direct:
            return lax.all_gather(p, dp, axis=0, tiled=True)
        away = swap(p, "x")
        pair = order([p, away], place, 2)
        blocks = [pair] + [xor_z(pair, s) for s in range(1, n_z)]
        return order(blocks, place, 1)

    def scatter_terms(own, other):
        recv = swap(other, "c")
        if not direct:
            total = (own[0].astype(f32) + recv.astype(f32)).astype(bf16)
            return [lax.psum_scatter(total, dp, scatter_dimension=0, tiled=True)]
        away = (own[1].astype(f32) + recv[1].astype(f32)).astype(bf16)
        back = swap(away, "x")
        near = (own[0].astype(f32) + recv[0].astype(f32) + back.astype(f32)).astype(bf16)
        return [near[:slab]] + [xor_z(near[s * slab : (s + 1) * slab], s) for s in range(1, n_z)]

    def sum_dp(x):
        if not direct:
            return lax.psum(x, dp)
        x = x + swap(x, "x")
        return tree([x if s == 0 else xor_z(x, s) for s in range(n_z)])

    shards = pack(inwards, turn(outwards), widening, turn(narrowing))
    whole = []
    for i, shard in enumerate(shards):
        full = gather_staged(shard) if i else gather_now(shard)
        whole.append((full, swap(full, "c")))
    weights_a, weights_b = whole[0::2], whole[1::2]

    sizes = [inbias[0].size, relative[0].size, widebias[0].size]
    packed = jnp.concatenate(
        [v for l in range(layer_total) for v in (inbias[l].ravel(), relative[l].ravel(), widebias[l])]
    ).reshape(-1, 4)
    other = swap(packed, "c").reshape(-1)
    packed = packed.reshape(-1)
    lookup = lookup_onehot()
    bias_qv, pos, wide_bias = [], [], []
    for l in range(layer_total):
        mask = pane_mask(l % 2 == 1)
        qv, tables, wides = [], [], []
        for source in (packed, other):
            at = l * sum(sizes)
            qv.append(source[at : at + sizes[0]].reshape(2, local))
            tables.append(source[at + sizes[0] : at + sizes[0] + sizes[1]].reshape(-1, heads))
            wides.append(source[at + sizes[0] + sizes[1] : at + sum(sizes)])
        bias_qv.append(jnp.concatenate(qv, axis=1))
        wide_bias.append(jnp.stack(wides))
        table = jnp.concatenate(tables, axis=1)
        spread_bias = jnp.dot(table.T, lookup, precision=lax.Precision.HIGHEST).reshape(
            GROUPS, heads, SLOT, SLOT
        )
        full = spread_bias[None] + jnp.asarray(mask)[:, None, None]
        pos.append(full.reshape(mask.shape[0], GROUPS, heads * SLOT, SLOT))
    picks = [
        selection(l % 2 == 1, images) for l in range(min(layer_total, 2))
    ]

    saved = []
    source = (place, tokens)
    for l in range(layer_total):
        hidden, a, q, k, v, prob, mixed, part = attn_fwd(
            l, gains, offsets, source, weights_a[l], bias_qv[l], pos[l], picks[l % 2]
        )
        recv = swap(part, "y")
        h1, c, z, slope, part_mlp = mlp_fwd(
            l, hidden, part, recv, gains, offsets, weights_b[l], wide_bias[l]
        )
        source = (h1, part_mlp, swap(part_mlp, "y"))
        saved.append((hidden, a, q, k, v, prob, mixed, h1, c, z, slope))

    back = (place, counts, cotangent) + source
    sums_mlp, sums_attn, score_sums = [None] * layer_total, [None] * layer_total, [None] * layer_total
    grads_a, grads_b = [None] * layer_total, [None] * layer_total
    sums_tail = [None] * layer_total
    for l in reversed(range(layer_total)):
        hidden, a, q, k, v, prob, mixed, h1, c, z, slope = saved[l]
        last = l == layer_total - 1
        res = mlp_bwd(l, last, back, gains, offsets, slope, weights_b[l])
        grad, grad_b, du_b, part, sums_mlp[l] = res[:5]
        if last:
            out_mine = res[5]
        else:
            sums_tail[l + 1] = sums_mlp[l]
        recv = swap(part, "y")
        pair = mlp_grads(place, c, du_b, z, grad_b, halves, slab)
        grads_b[l] = scatter_terms(pair[:-1], pair[-1])
        dh1, dh_b, d_proj, part_in, sums_attn[l], score_sums[l] = attn_bwd(
            l, grad, part, recv, h1, gains, weights_a[l], q, k, v, prob, picks[l % 2]
        )
        back = (dh1, part_in, swap(part_in, "y"), hidden)
        pair = attn_grads(place, a, d_proj, mixed, dh_b, halves, slab)
        grads_a[l] = scatter_terms(pair[:-1], pair[-1])
    grad_mine, sums_tail[0] = tail(*back, gains, cells)

    def both_halves(x):
        recv = swap(x, "c")
        lower = c_index == 0
        return jnp.concatenate([jnp.where(lower, x, recv), jnp.where(lower, recv, x)], axis=0)

    output = both_halves(out_mine)
    grad_tokens = both_halves(grad_mine)

    tables = []
    for l in range(layer_total):
        tables.append(
            lax.dot_general(
                score_sums[l].reshape(GROUPS * heads, SLOT * SLOT),
                lookup,
                (((1,), (1,)), ((), ())),
                precision=lax.Precision.HIGHEST,
            )
        )
    own_rows, other_rows = small_pack(sums_mlp, sums_attn, sums_tail, tables, local)
    other_rows = swap(other_rows, "c")
    total = sum_dp(own_rows + other_rows)

    def states(m):
        return params[m], first_moments[m], second_moments[m]

    results = [None] * len(params)
    results[4], results[6] = adam_pair(
        grads_b, states(4), [turn(v) for v in states(6)], hidden_local
    )
    results[0], results[3] = adam_pair(grads_a, states(0), [turn(v) for v in states(3)], local)
    results[3], results[6] = [turn(v) for v in results[3]], [turn(v) for v in results[6]]
    small = [states(1), [turn(v) for v in states(2)], states(5), states(7), states(8)]
    for m, result in zip((1, 2, 5, 7, 8), small_adam(total, small)):
        results[m] = [turn(v) for v in result] if m == 2 else result
    return (output, grad_tokens) + tuple(r[kind] for kind in range(4) for r in results)


def solution(mesh):
    n_dp, n_mp = mesh.shape["dp"], mesh.shape["mp"]
    inner = Mesh(
        mesh.devices.reshape(n_dp // 2, 2, n_mp // 2, 2), ("z", "x", "y", "c")
    )
    dp = ("z", "x")
    mp = ("y", "c")
    batch = P(dp, None, None)
    member_specs = (
        P(None, None, dp, mp),
        P(None, None, mp),
        P(None, None, mp),
        P(None, mp, dp),
        P(None, dp, mp),
        P(None, mp),
        P(None, mp, dp),
        P(),
        P(),
    )
    in_specs = (batch, batch, P(dp)) + member_specs * 3
    out_specs = (batch, batch) + member_specs * 4
    return jax.shard_map(step, mesh=inner, in_specs=in_specs, out_specs=out_specs, check_vma=False)
```

profile of v0, /device:TPU:0, one launch (start us, length us, event | category | flops | bytes accessed | tf_op | source)
XLA Modules:
  0.0 314.4 jit_solution(8523308495386924469)
XLA Ops:
  2.7 6.0 %collective-permute-start.6 = (bf16[64,512]{1,0:T(8,128)(2,1)}, bf16[64,512]{1,0:T(8,128)(2,1)S(1)}, u32[]{:S(2)}, u32[]{:S(2)}) collective-permute-start(bf16[64,512]{1,0:T(8,128)(2,1)} %get-tuple-element.143.refs_0_), channel_id=1, source_target_pairs={{0,28},{4,24},{8,20},{12,16},{16,12},{20,8},{24,4},{28,0},{1,29},{... | collective-permute-start | bytes 196616 | tf_op jit(solution)/shard_map/ppermute | solution.py:691
  39.0 12.6 %collective-permute-done.12.refs_2_ = bf16[128,1024]{1,0:T(8,128)(2,1)S(1)} collective-permute-done((bf16[128,1024]{1,0:T(8,128)(2,1)}, bf16[128,1024]{1,0:T(8,128)(2,1)S(1)}, u32[]{:S(2)}, u32[]{:S(2)}) %collective-permute-start.12) | collective-permute-done | bytes 262176 | tf_op jit(solution)/shard_map/ppermute | solution.py:688
  64.5 8.4 %shard_map.628 = (f32[400,512]{1,0:T(8,128)}, bf16[400,512]{1,0:T(8,128)(2,1)}, bf16[2,8,64,128]{3,2,1,0:T(8,128)(2,1)}, bf16[2,8,64,128]{3,2,1,0:T(8,128)(2,1)}...) custom-call(s32[4]{0:T(128)} %pad_add_fusion.place_ref.refs_0_, ...), custom_call_target="tpu_custom_call" | custom-call | tf_op jit(solution)/shard_map/pallas_call | solution.py:122
  78.3 8.2 %collective-permute-done.24.refs_2_ = bf16[128,1024]{1,0:T(8,128)(2,1)S(1)} collective-permute-done((bf16[128,1024]{1,0:T(8,128)(2,1)}, bf16[128,1024]{1,0:T(8,128)(2,1)S(1)}, u32[]{:S(2)}, u32[]{:S(2)}) %collective-permute-start.24) | collective-permute-done | bytes 262176 | tf_op jit(solution)/shard_map/ppermute | solution.py:688
  98.5 5.0 %shard_map.631 = (f32[400,512]{1,0:T(8,128)}, bf16[400,512]{1,0:T(8,128)(2,1)}, bf16[400,1024]{1,0:T(8,128)(2,1)}, bf16[400,1024]{1,0:T(8,128)(2,1)}, bf16[400,512]{1,0:T(8,128)(2,1)}) custom-call(f32[400,512]{1,0:T(8,128)} %get-tuple-element.144.h_ref, bf16[400,512]{1,0:T(8,128)(2,1)} %get-tuple-element.145.own_ref, bf16[400,512]{1,0:T(8,128)(2,1)} %copy-done.13, ...), custom_call_target="tpu_custom_call" | custom-call | tf_op jit(solution)/shard_map/pallas_call | solution.py:122
  108.0 7.7 %collective-permute-done.15.refs_2_ = bf16[400,512]{1,0:T(8,128)(2,1)S(1)} collective-permute-done((bf16[400,512]{1,0:T(8,128)(2,1)}, bf16[400,512]{1,0:T(8,128)(2,1)S(1)}, u32[]{:S(2)}, u32[]{:S(2)}) %collective-permute-start.15) | collective-permute-done | bytes 409632 | tf_op jit(solution)/shard_map/ppermute | solution.py:685
  116.4 9.0 %shard_map.634 = (f32[400,512]{1,0:T(8,128)}, bf16[400,512]{1,0:T(8,128)(2,1)}, bf16[2,8,64,128]{3,2,1,0:T(8,128)(2,1)}, bf16[2,8,64,128]{3,2,1,0:T(8,128)(2,1)}...) custom-call(f32[400,512]{1,0:T(8,128)} %get-tuple-element.147.refs_0, ...), custom_call_target="tpu_custom_call" | custom-call | tf_op jit(solution)/shard_map/pallas_call | solution.py:122
  127.6 9.0 %collective-permute-done.21.recv_ref = bf16[400,512]{1,0:T(8,128)(2,1)S(1)} collective-permute-done((bf16[400,512]{1,0:T(8,128)(2,1)}, bf16[400,512]{1,0:T(8,128)(2,1)S(1)}, u32[]{:S(2)}, u32[]{:S(2)}) %collective-permute-start.21) | collective-permute-done | bytes 409632 | tf_op jit(solution)/shard_map/ppermute | solution.py:685
  137.4 5.1 %shard_map.637 = (f32[400,512]{1,0:T(8,128)}, bf16[400,512]{1,0:T(8,128)(2,1)}, bf16[400,1024]{1,0:T(8,128)(2,1)}, bf16[400,1024]{1,0:T(8,128)(2,1)}, bf16[400,512]{1,0:T(8,128)(2,1)}) custom-call(f32[400,512]{1,0:T(8,128)} %get-tuple-element.150.h_ref.refs_3_, bf16[400,512]{1,0:T(8,128)(2,1)} %get-tuple-element.151.own_ref, bf16[400,512]{1,0:T(8,128)(2,1)} %copy-done.14, ...), custom_call_target="tpu_custom_call" | custom-call | tf_op jit(solution)/shard_map/pallas_call | solution.py:122
  146.3 6.5 %collective-permute-done.27.refs_5_ = bf16[400,512]{1,0:T(8,128)(2,1)S(1)} collective-permute-done((bf16[400,512]{1,0:T(8,128)(2,1)}, bf16[400,512]{1,0:T(8,128)(2,1)S(1)}, u32[]{:S(2)}, u32[]{:S(2)}) %collective-permute-start.27) | collective-permute-done | bytes 409632 | tf_op jit(solution)/shard_map/ppermute | solution.py:685
  153.6 5.1 %shard_map.638 = (f32[400,512]{1,0:T(8,128)}, bf16[400,512]{1,0:T(8,128)(2,1)}, bf16[400,1024]{1,0:T(8,128)(2,1)}, bf16[400,512]{1,0:T(8,128)(2,1)}, f32[8,512]{1,0:T(8,128)}, /*index=5*/f32[2,196,512]{2,1,0:T(8,128)}) custom-call(s32[4]{0:T(128)} %pad_add_fusion.place_ref.refs_0_, s32[1]{0:T(128)S(6)} %copy.105.refs_1_, f32[4,196,512]{2,1,0:T(8,128)} %copy.92.refs_2_, ...), custom_call_target="tpu_custom_call" | custom-call | tf_op jit(solution)/shard_map/pallas_call | solution.py:122
  162.9 4.0 %shard_map.649 = (bf16[256,1024]{1,0:T(8,128)(2,1)}, bf16[256,1024]{1,0:T(8,128)(2,1)}, bf16[2,256,1024]{2,1,0:T(8,128)(2,1)}) custom-call(s32[4]{0:T(128)} %pad_add_fusion.place_ref.refs_0_, bf16[400,512]{1,0:T(8,128)(2,1)} %get-tuple-element.209.c_ref, bf16[400,1024]{1,0:T(8,128)(2,1)} %get-tuple-element.210.du_ref, ...), custom_call_target="tpu_custom_call" | custom-call | tf_op jit(solution)/shard_map/pallas_call | solution.py:122
  167.1 6.4 %collective-permute-done.29.recv_ref = bf16[400,512]{1,0:T(8,128)(2,1)S(1)} collective-permute-done((bf16[400,512]{1,0:T(8,128)(2,1)}, bf16[400,512]{1,0:T(8,128)(2,1)S(1)}, u32[]{:S(2)}, u32[]{:S(2)}) %collective-permute-start.29) | collective-permute-done | bytes 409632 | tf_op jit(solution)/shard_map/ppermute | solution.py:685
  174.2 11.7 %shard_map.639 = (f32[400,512]{1,0:T(8,128)}, bf16[400,512]{1,0:T(8,128)(2,1)}, bf16[400,768]{1,0:T(8,128)(2,1)}, bf16[400,512]{1,0:T(8,128)(2,1)}, f32[8,512]{1,0:T(8,128)}, /*index=5*/f32[2,256,64]{2,1,0:T(8,128)}) custom-call(f32[400,512]{1,0:T(8,128)} %get-tuple-element.157.g_ref, bf16[400,512]{1,0:T(8,128)(2,1)} %get-tuple-element.158.own_ref, ...), custom_call_target="tpu_custom_call" | custom-call | tf_op jit(solution)/shard_map/pallas_call | solution.py:122
  187.1 3.3 %shard_map.644 = (bf16[256,512]{1,0:T(8,128)(2,1)}, bf16[256,512]{1,0:T(8,128)(2,1)}, bf16[2,256,512]{2,1,0:T(8,128)(2,1)}) custom-call(s32[4]{0:T(128)} %pad_add_fusion.place_ref.refs_0_, bf16[400,512]{1,0:T(8,128)(2,1)} %get-tuple-element.182.a_ref, bf16[400,768]{1,0:T(8,128)(2,1)} %get-tuple-element.183.dp_ref, ...), custom_call_target="tpu_custom_call" | custom-call | tf_op jit(solution)/shard_map/pallas_call | solution.py:122
  196.5 7.8 %collective-permute-done.30.refs_2_ = bf16[400,512]{1,0:T(8,128)(2,1)S(1)} collective-permute-done((bf16[400,512]{1,0:T(8,128)(2,1)S(1)}, bf16[400,512]{1,0:T(8,128)(2,1)S(1)}, u32[]{:S(2)}, u32[]{:S(2)}) %collective-permute-start.30) | collective-permute-done | bytes 409632 | tf_op jit(solution)/shard_map/ppermute | solution.py:685
  205.0 5.0 %shard_map.640 = (f32[400,512]{1,0:T(8,128)}, bf16[400,512]{1,0:T(8,128)(2,1)}, bf16[400,1024]{1,0:T(8,128)(2,1)}, bf16[400,512]{1,0:T(8,128)(2,1)}, f32[8,512]{1,0:T(8,128)}) custom-call(f32[400,512]{1,0:T(8,128)} %get-tuple-element.163.refs_0_, bf16[400,512]{1,0:T(8,128)(2,1)} %get-tuple-element.164.refs_1_, bf16[400,512]{1,0:T(8,128)(2,1)} %copy-done.19, ...), custom_call_target="tpu_custom_call" | custom-call | tf_op jit(solution)/shard_map/pallas_call | solution.py:122
  211.5 4.0 %shard_map.648 = (bf16[256,1024]{1,0:T(8,128)(2,1)}, bf16[256,1024]{1,0:T(8,128)(2,1)}, bf16[2,256,1024]{2,1,0:T(8,128)(2,1)}) custom-call(s32[4]{0:T(128)} %pad_add_fusion.place_ref.refs_0_, bf16[400,512]{1,0:T(8,128)(2,1)} %get-tuple-element.202.c_ref, bf16[400,1024]{1,0:T(8,128)(2,1)} %get-tuple-element.203.du_ref, ...), custom_call_target="tpu_custom_call" | custom-call | tf_op jit(solution)/shard_map/pallas_call | solution.py:122
  218.9 6.9 %collective-permute-done.40 = bf16[256,512]{1,0:T(8,128)(2,1)S(1)} collective-permute-done((bf16[256,512]{1,0:T(8,128)(2,1)S(1)}, bf16[256,512]{1,0:T(8,128)(2,1)S(1)}, u32[]{:S(2)}, u32[]{:S(2)}) %collective-permute-start.40) | collective-permute-done | bytes 262176 | tf_op jit(solution)/shard_map/ppermute | solution.py:685
  227.6 11.7 %shard_map.641 = (f32[400,512]{1,0:T(8,128)}, bf16[400,512]{1,0:T(8,128)(2,1)}, bf16[400,768]{1,0:T(8,128)(2,1)}, bf16[400,512]{1,0:T(8,128)(2,1)}, f32[8,512]{1,0:T(8,128)}, /*index=5*/f32[2,256,64]{2,1,0:T(8,128)}) custom-call(f32[400,512]{1,0:T(8,128)} %get-tuple-element.166.g_ref, bf16[400,512]{1,0:T(8,128)(2,1)} %get-tuple-element.167.own_ref, ...), custom_call_target="tpu_custom_call" | custom-call | tf_op jit(solution)/shard_map/pallas_call | solution.py:122
  243.5 3.3 %shard_map.643 = (bf16[256,512]{1,0:T(8,128)(2,1)}, bf16[256,512]{1,0:T(8,128)(2,1)}, bf16[2,256,512]{2,1,0:T(8,128)(2,1)}) custom-call(s32[4]{0:T(128)} %pad_add_fusion.place_ref.refs_0_, bf16[400,512]{1,0:T(8,128)(2,1)} %get-tuple-element.175.a_ref, bf16[400,768]{1,0:T(8,128)(2,1)} %get-tuple-element.176.dp_ref, ...), custom_call_target="tpu_custom_call" | custom-call | tf_op jit(solution)/shard_map/pallas_call | solution.py:122
  265.1 7.0 %collective-permute-done.35 = bf16[256,512]{1,0:T(8,128)(2,1)S(1)} collective-permute-done((bf16[256,512]{1,0:T(8,128)(2,1)S(1)}, bf16[256,512]{1,0:T(8,128)(2,1)S(1)}, u32[]{:S(2)}, u32[]{:S(2)}) %collective-permute-start.35) | collective-permute-done | bytes 262176 | tf_op jit(solution)/shard_map/ppermute | solution.py:685
  305.8 4.3 %collective-permute-done.52.refs_2_ = bf16[64,1024]{1,0:T(8,128)(2,1)S(1)} collective-permute-done((bf16[64,1024]{1,0:T(8,128)(2,1)S(1)}, bf16[64,1024]{1,0:T(8,128)(2,1)S(1)}, u32[]{:S(2)}, u32[]{:S(2)}) %collective-permute-start.52) | collective-permute-done | bytes 131104 | tf_op jit(solution)/shard_map/ppermute | solution.py:688
  310.8 3.4 %shard_map.650 = (f32[2,64,512]{2,1,0:T(8,128)}, f32[2,64,512]{2,1,0:T(8,128)}, f32[2,64,512]{2,1,0:T(8,128)}, f32[2,64,512]{2,1,0:T(8,128)}, f32[2,64,512]{2,1,...) custom-call(bf16[64,1024]{1,0:T(8,128)(2,1)} %get-tuple-element.373.refs_0_, ...), custom_call_target="tpu_custom_call" | custom-call | tf_op jit(solution)/shard_map/pallas_call | solution.py:122
  (297 shorter events, 150.9 us)
Async XLA Ops:
  2.7 22.9 %collective-permute-start.6 = (bf16[64,512]{1,0:T(8,128)(2,1)}, bf16[64,512]{1,0:T(8,128)(2,1)S(1)}, u32[]{:S(2)}, u32[]{:S(2)}) collective-permute-start(bf16[64,512]{1,0:T(8,128)(2,1)} %get-tuple-element.143.refs_0_), channel_id=1, source_target_pairs={{0,28},{4,24},{8,20},{12,16},{16,12},{20,8},{24,4},{28,0},{1,29},{... | collective-permute-start | bytes 196616 | tf_op jit(solution)/shard_map/ppermute | solution.py:691
  9.0 17.3 %collective-permute-start.4 = (bf16[64,512]{1,0:T(8,128)(2,1)}, bf16[64,512]{1,0:T(8,128)(2,1)S(1)}, u32[]{:S(2)}, u32[]{:S(2)}) collective-permute-start(bf16[64,512]{1,0:T(8,128)(2,1)} %get-tuple-element.143.refs_0_), channel_id=1, source_target_pairs={{0,20},{4,16},{8,28},{12,24},{16,4},{20,0},{24,12},{28,8},{1,21},{... | collective-permute-start | bytes 196616 | tf_op jit(solution)/shard_map/ppermute | solution.py:691
  28.8 22.9 %collective-permute-start.12 = (bf16[128,1024]{1,0:T(8,128)(2,1)}, bf16[128,1024]{1,0:T(8,128)(2,1)S(1)}, u32[]{:S(2)}, u32[]{:S(2)}) collective-permute-start(bf16[128,1024]{1,0:T(8,128)(2,1)} %shard_map.629.refs_0_), channel_id=1, source_target_pairs={{0,16},{8,24},{16,0},{24,8},{1,17},{9,25},{17,1},{25,9},{2,18},{10... | collective-permute-start | bytes 786440 | tf_op jit(solution)/shard_map/ppermute | solution.py:688
  29.7 22.0 %collective-permute-start.11 = (bf16[128,1024]{1,0:T(8,128)(2,1)}, bf16[128,1024]{1,0:T(8,128)(2,1)S(1)}, u32[]{:S(2)}, u32[]{:S(2)}) collective-permute-start(bf16[128,1024]{1,0:T(8,128)(2,1)} %shard_map.629.refs_0_), channel_id=1, source_target_pairs={{0,8},{8,0},{16,24},{24,16},{1,9},{9,1},{17,25},{25,17},{2,10},{10... | collective-permute-start | bytes 786440 | tf_op jit(solution)/shard_map/ppermute | solution.py:688
  30.7 42.2 %collective-permute-start.16 = (bf16[64,512]{1,0:T(8,128)(2,1)S(1)}, bf16[64,512]{1,0:T(8,128)(2,1)S(1)}, u32[]{:S(2)}, u32[]{:S(2)}) collective-permute-start(bf16[64,512]{1,0:T(8,128)(2,1)S(1)} %copy-done.42), channel_id=1, source_target_pairs={{0,4},{4,0},{1,5},{5,1},{2,6},{6,2},{3,7},{7,3},{8,12},{12,8},{9,1... | collective-permute-start | bytes 196616 | tf_op jit(solution)/shard_map/ppermute | solution.py:685
  34.9 25.9 %collective-permute-start.7 = (bf16[512,512]{1,0:T(8,128)(2,1)}, bf16[512,512]{1,0:T(8,128)(2,1)S(1)}, u32[]{:S(2)}, u32[]{:S(2)}) collective-permute-start(bf16[512,512]{1,0:T(8,128)(2,1)} %shard_map.627.refs_4_.w0), channel_id=1, source_target_pairs={{0,1},{1,0},{2,3},{3,2},{4,5},{5,4},{6,7},{7,6},{8,9},{9,8},{10,11... | collective-permute-start | bytes 1572872 | tf_op jit(solution)/shard_map/ppermute | solution.py:685
  37.5 19.6 %collective-permute-start.22 = (bf16[64,1024]{1,0:T(8,128)(2,1)S(1)}, bf16[64,1024]{1,0:T(8,128)(2,1)S(1)}, u32[]{:S(2)}, u32[]{:S(2)}) collective-permute-start(bf16[64,1024]{1,0:T(8,128)(2,1)S(1)} %copy-done.31), channel_id=1, source_target_pairs={{0,4},{4,0},{1,5},{5,1},{2,6},{6,2},{3,7},{7,3},{8,12},{12,8},{9,1... | collective-permute-start | bytes 393224 | tf_op jit(solution)/shard_map/ppermute | solution.py:685
  55.3 42.1 %collective-permute-start.14 = (bf16[512,1024]{1,0:T(8,128)(2,1)}, bf16[512,1024]{1,0:T(8,128)(2,1)S(1)}, u32[]{:S(2)}, u32[]{:S(2)}) collective-permute-start(bf16[512,1024]{1,0:T(8,128)(2,1)} %shard_map.630.w0.refs_7_), channel_id=1, source_target_pairs={{0,1},{1,0},{2,3},{3,2},{4,5},{5,4},{6,7},{7,6},{8,9},{9,8},{10,11... | collective-permute-start | bytes 3145736 | tf_op jit(solution)/shard_map/ppermute | solution.py:685
  59.5 17.5 %collective-permute-start.25 = (bf16[128,1024]{1,0:T(8,128)(2,1)}, bf16[128,1024]{1,0:T(8,128)(2,1)S(1)}, u32[]{:S(2)}, u32[]{:S(2)}) collective-permute-start(bf16[128,1024]{1,0:T(8,128)(2,1)} %shard_map.635.refs_0_), channel_id=1, source_target_pairs={{0,24},{8,16},{16,8},{24,0},{1,25},{9,17},{17,9},{25,1},{2,26},{10... | collective-permute-start | bytes 786440 | tf_op jit(solution)/shard_map/ppermute | solution.py:688
  60.8 25.8 %collective-permute-start.24 = (bf16[128,1024]{1,0:T(8,128)(2,1)}, bf16[128,1024]{1,0:T(8,128)(2,1)S(1)}, u32[]{:S(2)}, u32[]{:S(2)}) collective-permute-start(bf16[128,1024]{1,0:T(8,128)(2,1)} %shard_map.635.refs_0_), channel_id=1, source_target_pairs={{0,16},{8,24},{16,0},{24,8},{1,17},{9,25},{17,1},{25,9},{2,18},{10... | collective-permute-start | bytes 786440 | tf_op jit(solution)/shard_map/ppermute | solution.py:688
  60.8 25.8 %collective-permute-start.23 = (bf16[128,1024]{1,0:T(8,128)(2,1)}, bf16[128,1024]{1,0:T(8,128)(2,1)S(1)}, u32[]{:S(2)}, u32[]{:S(2)}) collective-permute-start(bf16[128,1024]{1,0:T(8,128)(2,1)} %shard_map.635.refs_0_), channel_id=1, source_target_pairs={{0,8},{8,0},{16,24},{24,16},{1,9},{9,1},{17,25},{25,17},{2,10},{10... | collective-permute-start | bytes 786440 | tf_op jit(solution)/shard_map/ppermute | solution.py:688
  73.0 24.4 %collective-permute-start.9 = (bf16[400,512]{1,0:T(8,128)(2,1)}, bf16[400,512]{1,0:T(8,128)(2,1)S(1)}, u32[]{:S(2)}, u32[]{:S(2)}) collective-permute-start(bf16[400,512]{1,0:T(8,128)(2,1)} %get-tuple-element.145.own_ref), channel_id=1, source_target_pairs={{0,2},{2,0},{1,3},{3,1},{4,6},{6,4},{5,7},{7,5},{8,10},{10,8},{9,1... | collective-permute-start | bytes 1228808 | tf_op jit(solution)/shard_map/ppermute | solution.py:685
  92.1 35.6 %collective-permute-start.26 = (bf16[512,1024]{1,0:T(8,128)(2,1)}, bf16[512,1024]{1,0:T(8,128)(2,1)S(1)}, u32[]{:S(2)}, u32[]{:S(2)}) collective-permute-start(bf16[512,1024]{1,0:T(8,128)(2,1)} %shard_map.636.w0.refs_9_), channel_id=1, source_target_pairs={{0,1},{1,0},{2,3},{3,2},{4,5},{5,4},{6,7},{7,6},{8,9},{9,8},{10,11... | collective-permute-start | bytes 3145736 | tf_op jit(solution)/shard_map/ppermute | solution.py:685
  161.4 32.5 %collective-permute-start.28 = (f32[2,196,512]{2,0,1:T(2,128)}, f32[2,196,512]{2,0,1:T(2,128)S(1)}, u32[]{:S(2)}, u32[]{:S(2)}) collective-permute-start(f32[2,196,512]{2,0,1:T(2,128)} %copy.93), channel_id=1, source_target_pairs={{0,1},{1,0},{2,3},{3,2},{4,5},{5,4},{6,7},{7,6},{8,9},{9,8},{10,11... | collective-permute-start | bytes 2408456 | tf_op jit(solution)/shard_map/ppermute | solution.py:685
  166.9 51.3 %collective-permute-start.54 = (bf16[2,256,1024]{2,1,0:T(8,128)(2,1)}, bf16[2,256,1024]{2,1,0:T(8,128)(2,1)S(1)}, u32[]{:S(2)}, u32[]{:S(2)}) collective-permute-start(bf16[2,256,1024]{2,1,0:T(8,128)(2,1)} %get-tuple-element.214), channel_id=1, source_target_pairs={{0,1},{1,0},{2,3},{3,2},{4,5},{5,4},{6,7},{7,6},{8,9},{9,8},{10,11... | collective-permute-start | bytes 3145736 | tf_op jit(solution)/shard_map/ppermute | solution.py:685
  190.4 25.1 %collective-permute-start.39 = (bf16[2,256,512]{2,1,0:T(8,128)(2,1)}, bf16[2,256,512]{2,1,0:T(8,128)(2,1)}, u32[]{:S(2)}, u32[]{:S(2)}) collective-permute-start(bf16[2,256,512]{2,1,0:T(8,128)(2,1)} %get-tuple-element.187), channel_id=1, source_target_pairs={{0,1},{1,0},{2,3},{3,2},{4,5},{5,4},{6,7},{7,6},{8,9},{9,8},{10,11... | collective-permute-start | bytes 1572872 | tf_op jit(solution)/shard_map/ppermute | solution.py:685
  215.5 47.8 %collective-permute-start.49 = (bf16[2,256,1024]{2,1,0:T(8,128)(2,1)}, bf16[2,256,1024]{2,1,0:T(8,128)(2,1)S(1)}, u32[]{:S(2)}, u32[]{:S(2)}) collective-permute-start(bf16[2,256,1024]{2,1,0:T(8,128)(2,1)} %get-tuple-element.207), channel_id=1, source_target_pairs={{0,1},{1,0},{2,3},{3,2},{4,5},{5,4},{6,7},{7,6},{8,9},{9,8},{10,11... | collective-permute-start | bytes 3145736 | tf_op jit(solution)/shard_map/ppermute | solution.py:685
  218.3 36.7 %collective-permute-start.55 = (bf16[256,1024]{1,0:T(8,128)(2,1)S(1)}, bf16[256,1024]{1,0:T(8,128)(2,1)}, u32[]{:S(2)}, u32[]{:S(2)}) collective-permute-start(bf16[256,1024]{1,0:T(8,128)(2,1)S(1)} %fusion.8), channel_id=1, source_target_pairs={{0,4},{4,0},{1,5},{5,1},{2,6},{6,2},{3,7},{7,3},{8,12},{12,8},{9,1... | collective-permute-start | bytes 1572872 | tf_op jit(solution)/shard_map/ppermute | solution.py:685
  240.5 33.2 %collective-permute-start.43 = (bf16[64,512]{1,0:T(8,128)(2,1)}, bf16[64,512]{1,0:T(8,128)(2,1)S(1)}, u32[]{:S(2)}, u32[]{:S(2)}) collective-permute-start(bf16[64,512]{1,0:T(8,128)(2,1)} %get-tuple-element.380), channel_id=1, source_target_pairs={{0,24},{8,16},{16,8},{24,0},{1,25},{9,17},{17,9},{25,1},{2,26},{10... | collective-permute-start | bytes 196616 | tf_op jit(solution)/shard_map/ppermute | solution.py:688
  250.1 25.6 %collective-permute-start.42 = (bf16[64,512]{1,0:T(8,128)(2,1)}, bf16[64,512]{1,0:T(8,128)(2,1)S(1)}, u32[]{:S(2)}, u32[]{:S(2)}) collective-permute-start(bf16[64,512]{1,0:T(8,128)(2,1)} %get-tuple-element.381), channel_id=1, source_target_pairs={{0,16},{8,24},{16,0},{24,8},{1,17},{9,25},{17,1},{25,9},{2,18},{10... | collective-permute-start | bytes 196616 | tf_op jit(solution)/shard_map/ppermute | solution.py:688
  263.2 34.5 %collective-permute-start.33 = (f32[2,196,512]{2,0,1:T(2,128)S(1)}, f32[2,196,512]{2,0,1:T(2,128)S(1)}, u32[]{:S(2)}, u32[]{:S(2)}) collective-permute-start(f32[2,196,512]{2,0,1:T(2,128)S(1)} %copy.96), channel_id=1, source_target_pairs={{0,1},{1,0},{2,3},{3,2},{4,5},{5,4},{6,7},{7,6},{8,9},{9,8},{10,11... | collective-permute-start | bytes 2408456 | tf_op jit(solution)/shard_map/ppermute | solution.py:685
  272.1 21.5 %collective-permute-start.50 = (bf16[256,1024]{1,0:T(8,128)(2,1)S(1)}, bf16[256,1024]{1,0:T(8,128)(2,1)}, u32[]{:S(2)}, u32[]{:S(2)}) collective-permute-start(bf16[256,1024]{1,0:T(8,128)(2,1)S(1)} %fusion.11), channel_id=1, source_target_pairs={{0,4},{4,0},{1,5},{5,1},{2,6},{6,2},{3,7},{7,3},{8,12},{12,8},{9,1... | collective-permute-start | bytes 1572872 | tf_op jit(solution)/shard_map/ppermute | solution.py:685
  288.6 17.1 %collective-permute-start.57 = (bf16[64,1024]{1,0:T(8,128)(2,1)}, bf16[64,1024]{1,0:T(8,128)(2,1)}, u32[]{:S(2)}, u32[]{:S(2)}) collective-permute-start(bf16[64,1024]{1,0:T(8,128)(2,1)} %get-tuple-element.367), channel_id=1, source_target_pairs={{0,16},{8,24},{16,0},{24,8},{1,17},{9,25},{17,1},{25,9},{2,18},{10... | collective-permute-start | bytes 393224 | tf_op jit(solution)/shard_map/ppermute | solution.py:688
  288.6 17.1 %collective-permute-start.56 = (bf16[64,1024]{1,0:T(8,128)(2,1)}, bf16[64,1024]{1,0:T(8,128)(2,1)}, u32[]{:S(2)}, u32[]{:S(2)}) collective-permute-start(bf16[64,1024]{1,0:T(8,128)(2,1)} %get-tuple-element.368), channel_id=1, source_target_pairs={{0,8},{8,0},{16,24},{24,16},{1,9},{9,1},{17,25},{25,17},{2,10},{10... | collective-permute-start | bytes 393224 | tf_op jit(solution)/shard_map/ppermute | solution.py:688
  (93 other events, 706.4 us)
where the time goes:
time: 320 us; the launch traced here: 314 us
  Pallas kernels  103 us (32%)
  waiting for transfers between devices  88.7 us (28%)
  starting transfers between devices  71.2 us (22%)
  local copies, waits for them, and re-layouts  29.3 us (9%)
  other arithmetic  13.8 us (4%)
  matrix products  5.97 us (2%)
    pallas_call x25, Pallas kernels, call(): pl.pallas_call(kernel, in_specs=specs, out_shape=[jax.ShapeDtypeStruct(sh...  103 us
    ppermute x28, waiting for transfers between devices, swap(): return lax.ppermute(x, axis, [(0, 1), (1, 0)])  54.6 us
    ppermute x24, starting transfers between devices, xor_z(): return lax.ppermute(x, 'z', [(i, i ^ s) for i in range(n_z)])  35.2 us
    ppermute x24, waiting for transfers between devices, xor_z(): return lax.ppermute(x, 'z', [(i, i ^ s) for i in range(n_z)])  34.1 us
    ppermute x28, starting transfers between devices, swap(): return lax.ppermute(x, axis, [(0, 1), (1, 0)])  23 us
    unnamed x120, local copies, waits for them, and re-layouts  17.1 us
    ppermute x7, starting transfers between devices, xor_dp(): return lax.ppermute(x, dp, [(i, i ^ s) for i in range(n_x * n_z)])  12.9 us
  transfers between devices with their start and end apart: 59, of which 18 were waited for; matrix products, arithmetic and copies ran while one was open for 12% of the time, Pallas kernels for 28%

commit v1 on v0

--- a/solution.py
+++ b/solution.py
@@ -58,7 +58,7 @@
     full = np.full((SLOT, SLOT), -1, np.int32)
     full[:CELLS, :CELLS] = lookup
     entries = jnp.arange((2 * WIN - 1) ** 2, dtype=jnp.int32)
-    return (entries[:, None] == jnp.asarray(full.reshape(1, -1))).astype(f32)
+    return (entries[:, None] == jnp.asarray(full.reshape(1, -1))).astype(bf16)
 
 
 def pane_mask(shifted):
@@ -128,10 +128,10 @@
     )(*args)
 
 
-def load_images(place_ref, images_ref, buffer, images):
+def load_images(images_ref, buffer, images):
     cells, width = images_ref.shape[1:]
     for i in range(images):
-        buffer[i * ROWS : i * ROWS + cells, :] = images_ref[place_ref[0] * images + i]
+        buffer[i * ROWS : i * ROWS + cells, :] = images_ref[i]
         buffer[i * ROWS + cells : (i + 1) * ROWS, :] = jnp.zeros((ROWS - cells, width), f32)
 
 
@@ -141,12 +141,13 @@
         out[i] = value[i * ROWS : i * ROWS + cells, :]
 
 
-def attn_fwd(layer, gains, offsets, source, weights, bias_qv, pos, pick):
+def attn_fwd(layer, gains, offsets, source, weights, biases, pos, pick):
     first = layer == 0
     win_rows, rows = pick.shape
+    *weights, at = weights
     width = weights[0].shape[0]
     panes = win_rows // SLOT
-    local = weights[0].shape[1] // 4
+    local = biases[0].shape[2]
     heads = local // HEAD_DIM
     masks_n = pos.shape[0]
     factor = HEAD_DIM ** (-0.5)
@@ -154,10 +155,10 @@
 
     def kernel(*refs):
         src = refs[:n_src]
-        gain_ref, off_ref, w0, w1, bias_ref, pos_ref, pick_ref = refs[n_src : n_src + 7]
-        h_ref, a_ref, q_ref, k_ref, v_ref, prob_ref, mixed_ref, part_ref, mw_ref = refs[n_src + 7 :]
+        gain_ref, off_ref, w0, w1, b0, b1, pos_ref, pick_ref = refs[n_src : n_src + 8]
+        h_ref, a_ref, q_ref, k_ref, v_ref, prob_ref, mixed_ref, part_ref, mw_ref = refs[n_src + 8 :]
         if first:
-            load_images(src[0], src[1], h_ref, rows // ROWS)
+            load_images(src[0], h_ref, rows // ROWS)
             hidden = h_ref[...]
         else:
             hidden = src[0][...] + (
@@ -168,11 +169,11 @@
         a = (normed * gain_ref[layer, 0:1] + off_ref[layer, 0:1]).astype(bf16)
         a_ref[...] = a
         a_win = dot(pick_ref[...], a, 1, 0).astype(bf16)
-        for g, w in enumerate((w0, w1)):
-            proj = dot(a_win, w[:, : 3 * local], 1, 0)
-            q = ((proj[:, :local] + bias_ref[0:1, g * local : (g + 1) * local]) * factor).astype(bf16)
+        for g, (w, bias_ref) in enumerate(((w0, b0), (w1, b1))):
+            proj = dot(a_win, w[:, at : at + 3 * local], 1, 0)
+            q = ((proj[:, :local] + bias_ref[layer, 0:1]) * factor).astype(bf16)
             k = proj[:, local : 2 * local].astype(bf16)
-            v = (proj[:, 2 * local :] + bias_ref[1:2, g * local : (g + 1) * local]).astype(bf16)
+            v = (proj[:, 2 * local :] + bias_ref[layer, 1:2]).astype(bf16)
             q_ref[g] = q.reshape(panes, SLOT, local)
             k_ref[g] = k.reshape(panes, SLOT, local)
             v_ref[g] = v.reshape(panes, SLOT, local)
@@ -195,7 +196,7 @@
         mixed_ref[...] = mixed
         part = None
         for g, w in enumerate((w0, w1)):
-            term = dot(mixed[:, g * local : (g + 1) * local], w[:, 3 * local :], 1, 1)
+            term = dot(mixed[:, g * local : (g + 1) * local], w[:, at + 3 * local : at + 4 * local], 1, 1)
             part = term if part is None else part + term
         part_ref[...] = part.astype(bf16)
 
@@ -216,20 +217,20 @@
         gains,
         offsets,
         *weights,
-        bias_qv,
+        *biases,
         pos,
         pick,
         scratch=[((panes, SLOT, GROUPS * local), bf16)],
-        scalars=1 if first else 0,
-    )
-
-
-def mlp_fwd(layer, hidden, own, recv, gains, offsets, weights, wide_bias):
+    )
+
+
+def mlp_fwd(layer, hidden, own, recv, gains, offsets, weights, wide_biases):
+    *weights, at = weights
     rows, width = hidden.shape
-    local = weights[0].shape[1] // 2
+    local = wide_biases[0].shape[1]
 
     def kernel(
-        h_ref, own_ref, recv_ref, gain_ref, off_ref, w0, w1, wb_ref, h1_ref, c_ref, z_ref, s_ref, p_ref
+        h_ref, own_ref, recv_ref, gain_ref, off_ref, w0, w1, b0, b1, h1_ref, c_ref, z_ref, s_ref, p_ref
     ):
         h1 = h_ref[...] + (own_ref[...].astype(f32) + recv_ref[...].astype(f32) + off_ref[layer, 2:3])
         h1_ref[...] = h1
@@ -237,14 +238,14 @@
         c = (normed * gain_ref[layer, 1:2] + off_ref[layer, 1:2]).astype(bf16)
         c_ref[...] = c
         part = None
-        for g, w in enumerate((w0, w1)):
-            u = dot(c, w[:, :local], 1, 0) + wb_ref[g : g + 1, :]
+        for g, (w, bias_ref) in enumerate(((w0, b0), (w1, b1))):
+            u = dot(c, w[:, at : at + local], 1, 0) + bias_ref[layer : layer + 1, :]
             cdf = 0.5 * (1.0 + lax.erf(u * 0.7071067811865476))
             density = jnp.exp(-0.5 * u * u) * 0.3989422804014327
             z = (u * cdf).astype(bf16)
             z_ref[:, g * local : (g + 1) * local] = z
             s_ref[:, g * local : (g + 1) * local] = (cdf + u * density).astype(bf16)
-            term = dot(z, w[:, local:], 1, 1)
+            term = dot(z, w[:, at + local : at + 2 * local], 1, 1)
             part = term if part is None else part + term
         p_ref[...] = part.astype(bf16)
 
@@ -255,12 +256,13 @@
         ((rows, GROUPS * local), bf16),
         ((rows, width), bf16),
     ]
-    return call(kernel, outs, hidden, own, recv, gains, offsets, *weights, wide_bias)
+    return call(kernel, outs, hidden, own, recv, gains, offsets, *weights, *wide_biases)
 
 
 def mlp_bwd(layer, last, source, gains, offsets, slope, weights):
+    *weights, at = weights
     rows, width = source[3].shape
-    local = weights[0].shape[1] // 2
+    local = slope.shape[1] // GROUPS
     n_src = len(source)
 
     def kernel(*refs):
@@ -271,7 +273,7 @@
         if last:
             place_ref, count_ref = src[:2]
             images = rows // ROWS
-            load_images(place_ref, src[2], g_ref, images)
+            load_images(src[2], g_ref, images)
             result = src[3][...] + (src[4][...].astype(f32) + src[5][...].astype(f32) + off_ref[layer, 3:4])
             out_ref = refs[n_src + 10]
             cells = out_ref.shape[1]
@@ -295,11 +297,11 @@
         gb_ref[...] = grad_b
         part = None
         for g, w in enumerate((w0, w1)):
-            du = dot(grad_b, w[:, local:], 1, 0) * s_ref[:, g * local : (g + 1) * local].astype(f32)
+            du = dot(grad_b, w[:, at + local : at + 2 * local], 1, 0) * s_ref[:, g * local : (g + 1) * local].astype(f32)
             sum_ref[3 + g : 4 + g, :local] = jnp.sum(du, axis=0, keepdims=True)
             du_b = du.astype(bf16)
             du_ref[:, g * local : (g + 1) * local] = du_b
-            term = dot(du_b, w[:, :local], 1, 1)
+            term = dot(du_b, w[:, at : at + local], 1, 1)
             part = term if part is None else part + term
         p_ref[...] = part.astype(bf16)
 
@@ -364,7 +366,8 @@
     rows, width = grad.shape
     win_rows = pick.shape[0]
     panes = win_rows // SLOT
-    local = weights[0].shape[1] // 4
+    *weights, at = weights
+    local = q.shape[3]
     heads = local // HEAD_DIM
     factor = HEAD_DIM ** (-0.5)
 
@@ -384,7 +387,7 @@
         dh_b = dh1.astype(bf16)
         dhb_ref[...] = dh_b
         for g, w in enumerate((w0, w1)):
-            d_mixed = dot(dh_b, w[:, 3 * local :], 1, 0).astype(bf16)
+            d_mixed = dot(dh_b, w[:, at + 3 * local : at + 4 * local], 1, 0).astype(bf16)
             d_win = dot(pick_ref[...], d_mixed, 1, 0).astype(bf16)
             dm_ref[g] = d_win.reshape(panes, SLOT, local)
         ds_ref[...] = jnp.zeros_like(ds_ref)
@@ -412,7 +415,7 @@
                 bias_ref[1:2, g * local : (g + 1) * local] += jnp.sum(d_value, axis=0, keepdims=True)
             return carry
 
-        lax.fori_loop(0, panes, step, 0, unroll=UNROLL)
+        lax.fori_loop(0, panes, step, 0)
         sum_ref[3:4, : GROUPS * local] = bias_ref[0:1, :]
         sum_ref[4:5, : GROUPS * local] = bias_ref[1:2, :]
         d_proj = dot(
@@ -421,7 +424,7 @@
         dp_ref[...] = d_proj
         part = None
         for g, w in enumerate((w0, w1)):
-            term = dot(d_proj[:, g * 3 * local : (g + 1) * 3 * local], w[:, : 3 * local], 1, 1)
+            term = dot(d_proj[:, g * 3 * local : (g + 1) * 3 * local], w[:, at : at + 3 * local], 1, 1)
             part = term if part is None else part + term
         part_ref[...] = part.astype(bf16)
 
@@ -530,40 +533,48 @@
     return call(kernel, outs, inwards, outwards, widening, narrowing)
 
 
-def adam_pair(parts, first, second, turned):
+def adam_all(parts, states):
     layers = len(parts)
-    counts = [len(p) for p in parts]
-    flat = [p for layer in parts for p in layer]
-    stacked = first[0].ndim == 4
+    count = len(parts[0])
+    flat = [p for terms in parts for p in terms]
 
     def kernel(*refs):
-        blocks, rest = refs[: len(flat)], refs[len(flat) :]
-        one, two, out_one, out_two = rest[:3], rest[3:6], rest[6:10], rest[10:14]
-        at = 0
-
-        def update(index, gradient, ins, outs):
-            weight, mean, square = (r[index] for r in ins)
-            new = adam_update(weight, gradient, mean, square, decay_rate)
-            outs[0][index] = gradient
-            for ref, value in zip(outs[1:], new):
+        blocks, refs = refs[: len(flat)], refs[len(flat) :]
+        ins, outs = refs[:12], refs[12:]
+
+        def update(member, index, gradient):
+            weight, mean, square = (r[index] for r in ins[3 * member : 3 * member + 3])
+            new = (gradient,) + adam_update(weight, gradient, mean, square, decay_rate)
+            for ref, value in zip(outs[4 * member : 4 * member + 4], new):
                 ref[index] = value
 
         for l in range(layers):
-            terms = [blocks[at + i][...].astype(f32) for i in range(counts[l])]
-            at += counts[l]
-            total = tree(terms)
-            split = total.shape[1] - turned
-            if stacked:
-                piece = split // one[0].shape[1]
-                for j in range(one[0].shape[1]):
-                    update((l, j), total[:, j * piece : (j + 1) * piece], one, out_one)
-            else:
-                update((l,), total[:, :split], one, out_one)
-            update((l,), total[:, split:], two, out_two)
-
-    outs = [(first[0].shape, f32)] * 4 + [(second[0].shape, f32)] * 4
-    res = call(kernel, outs, *flat, *first, *second)
-    return res[:4], res[4:]
+            total = tree([blocks[l * count + i][...].astype(f32) for i in range(count)])
+            at = 0
+            for member in range(4):
+                shape = ins[3 * member].shape
+                for j in range(shape[1] if len(shape) == 4 else 1):
+                    index = (l, j) if len(shape) == 4 else (l,)
+                    update(member, index, total[:, at : at + shape[-1]])
+                    at += shape[-1]
+
+    outs = [(state[0].shape, f32) for state in states for _ in range(4)]
+    res = call(kernel, outs, *flat, *[v for state in states for v in state])
+    return [res[4 * m : 4 * m + 4] for m in range(4)]
+
+
+def join(place, own, recv):
+    images, cells, width = own.shape
+
+    def kernel(place_ref, own_ref, recv_ref, out_ref):
+        lower = place_ref[0] == 0
+        for i in range(images):
+            mine, theirs = own_ref[i], recv_ref[i]
+            out_ref[:, i, :] = jnp.where(lower, mine, theirs)
+            out_ref[:, images + i, :] = jnp.where(lower, theirs, mine)
+
+    outs = [((cells, 2 * images, width), f32)]
+    return call(kernel, outs, place, own, recv, scalars=1)[0]
 
 
 def small_rows(layers, heads):
@@ -663,7 +674,6 @@
     slots, cells, _ = tokens.shape
     images = slots // 2
     local = inwards.shape[3]
-    hidden_local = widening.shape[2]
     heads = local // HEAD_DIM
     slab = inwards.shape[2]
     n_x = lax.axis_size("x")
@@ -704,14 +714,18 @@
         blocks = [pair] + [xor_z(pair, s) for s in range(1, n_z)]
         return order(blocks, place, 1)
 
-    def scatter_terms(own, other):
+    def scatter_half(own, other):
         recv = swap(other, "c")
         if not direct:
-            total = (own[0].astype(f32) + recv.astype(f32)).astype(bf16)
-            return [lax.psum_scatter(total, dp, scatter_dimension=0, tiled=True)]
+            return (own[0].astype(f32) + recv.astype(f32)).astype(bf16)
         away = (own[1].astype(f32) + recv[1].astype(f32)).astype(bf16)
         back = swap(away, "x")
-        near = (own[0].astype(f32) + recv[0].astype(f32) + back.astype(f32)).astype(bf16)
+        return own[0].astype(f32) + recv[0].astype(f32) + back.astype(f32)
+
+    def scatter_rest(halves_of):
+        near = jnp.concatenate(halves_of, axis=1).astype(bf16)
+        if not direct:
+            return [lax.psum_scatter(near, dp, scatter_dimension=0, tiled=True)]
         return [near[:slab]] + [xor_z(near[s * slab : (s + 1) * slab], s) for s in range(1, n_z)]
 
     def sum_dp(x):
@@ -724,31 +738,22 @@
     whole = []
     for i, shard in enumerate(shards):
         full = gather_staged(shard) if i else gather_now(shard)
-        whole.append((full, swap(full, "c")))
+        whole.append((full, swap(full, "c"), 0))
     weights_a, weights_b = whole[0::2], whole[1::2]
 
-    sizes = [inbias[0].size, relative[0].size, widebias[0].size]
-    packed = jnp.concatenate(
-        [v for l in range(layer_total) for v in (inbias[l].ravel(), relative[l].ravel(), widebias[l])]
-    ).reshape(-1, 4)
-    other = swap(packed, "c").reshape(-1)
-    packed = packed.reshape(-1)
+    tables = turn(relative)
+    biases = (inbias, swap(inbias, "c"))
+    wide_biases = (widebias, swap(widebias, "c"))
+    tables = jnp.concatenate([tables, swap(tables, "c")], axis=1)
     lookup = lookup_onehot()
-    bias_qv, pos, wide_bias = [], [], []
+    pos = []
     for l in range(layer_total):
         mask = pane_mask(l % 2 == 1)
-        qv, tables, wides = [], [], []
-        for source in (packed, other):
-            at = l * sum(sizes)
-            qv.append(source[at : at + sizes[0]].reshape(2, local))
-            tables.append(source[at + sizes[0] : at + sizes[0] + sizes[1]].reshape(-1, heads))
-            wides.append(source[at + sizes[0] + sizes[1] : at + sum(sizes)])
-        bias_qv.append(jnp.concatenate(qv, axis=1))
-        wide_bias.append(jnp.stack(wides))
-        table = jnp.concatenate(tables, axis=1)
-        spread_bias = jnp.dot(table.T, lookup, precision=lax.Precision.HIGHEST).reshape(
-            GROUPS, heads, SLOT, SLOT
-        )
+        upper = lax.reduce_precision(tables[l], 8, 7)
+        middle = lax.reduce_precision(tables[l] - upper, 8, 7)
+        terms = jnp.concatenate([upper, middle, tables[l] - upper - middle], axis=0)
+        terms = dot(terms.astype(bf16), lookup, 1, 0).reshape(3, -1, SLOT * SLOT)
+        spread_bias = (terms[0] + terms[1] + terms[2]).reshape(GROUPS, heads, SLOT, SLOT)
         full = spread_bias[None] + jnp.asarray(mask)[:, None, None]
         pos.append(full.reshape(mask.shape[0], GROUPS, heads * SLOT, SLOT))
     picks = [
@@ -756,21 +761,22 @@
     ]
 
     saved = []
-    source = (place, tokens)
+    source = (lax.dynamic_slice_in_dim(tokens, c_index * images, images, 0),)
     for l in range(layer_total):
         hidden, a, q, k, v, prob, mixed, part = attn_fwd(
-            l, gains, offsets, source, weights_a[l], bias_qv[l], pos[l], picks[l % 2]
+            l, gains, offsets, source, weights_a[l], biases, pos[l], picks[l % 2]
         )
         recv = swap(part, "y")
         h1, c, z, slope, part_mlp = mlp_fwd(
-            l, hidden, part, recv, gains, offsets, weights_b[l], wide_bias[l]
+            l, hidden, part, recv, gains, offsets, weights_b[l], wide_biases
         )
         source = (h1, part_mlp, swap(part_mlp, "y"))
         saved.append((hidden, a, q, k, v, prob, mixed, h1, c, z, slope))
 
-    back = (place, counts, cotangent) + source
+    cot_mine = lax.dynamic_slice_in_dim(cotangent, c_index * images, images, 0)
+    back = (place, counts, cot_mine) + source
     sums_mlp, sums_attn, score_sums = [None] * layer_total, [None] * layer_total, [None] * layer_total
-    grads_a, grads_b = [None] * layer_total, [None] * layer_total
+    grads = [None] * layer_total
     sums_tail = [None] * layer_total
     for l in reversed(range(layer_total)):
         hidden, a, q, k, v, prob, mixed, h1, c, z, slope = saved[l]
@@ -783,33 +789,30 @@
             sums_tail[l + 1] = sums_mlp[l]
         recv = swap(part, "y")
         pair = mlp_grads(place, c, du_b, z, grad_b, halves, slab)
-        grads_b[l] = scatter_terms(pair[:-1], pair[-1])
+        half_b = scatter_half(pair[:-1], pair[-1])
         dh1, dh_b, d_proj, part_in, sums_attn[l], score_sums[l] = attn_bwd(
             l, grad, part, recv, h1, gains, weights_a[l], q, k, v, prob, picks[l % 2]
         )
         back = (dh1, part_in, swap(part_in, "y"), hidden)
         pair = attn_grads(place, a, d_proj, mixed, dh_b, halves, slab)
-        grads_a[l] = scatter_terms(pair[:-1], pair[-1])
+        half_a = scatter_half(pair[:-1], pair[-1])
+        grads[l] = scatter_rest([half_a, half_b])
     grad_mine, sums_tail[0] = tail(*back, gains, cells)
 
     def both_halves(x):
         recv = swap(x, "c")
-        lower = c_index == 0
-        return jnp.concatenate([jnp.where(lower, x, recv), jnp.where(lower, recv, x)], axis=0)
+        return jnp.swapaxes(join(place, x, recv), 0, 1)
 
     output = both_halves(out_mine)
     grad_tokens = both_halves(grad_mine)
 
     tables = []
     for l in range(layer_total):
-        tables.append(
-            lax.dot_general(
-                score_sums[l].reshape(GROUPS * heads, SLOT * SLOT),
-                lookup,
-                (((1,), (1,)), ((), ())),
-                precision=lax.Precision.HIGHEST,
-            )
-        )
+        flat = score_sums[l].reshape(GROUPS * heads, SLOT * SLOT)
+        upper = lax.reduce_precision(flat, 8, 7)
+        both = jnp.concatenate([upper, flat - upper], axis=0).astype(bf16)
+        both = dot(both, lookup, 1, 1)
+        tables.append(both[: GROUPS * heads] + both[GROUPS * heads :])
     own_rows, other_rows = small_pack(sums_mlp, sums_attn, sums_tail, tables, local)
     other_rows = swap(other_rows, "c")
     total = sum_dp(own_rows + other_rows)
@@ -818,13 +821,13 @@
         return params[m], first_moments[m], second_moments[m]
 
     results = [None] * len(params)
-    results[4], results[6] = adam_pair(
-        grads_b, states(4), [turn(v) for v in states(6)], hidden_local
-    )
-    results[0], results[3] = adam_pair(grads_a, states(0), [turn(v) for v in states(3)], local)
-    results[3], results[6] = [turn(v) for v in results[3]], [turn(v) for v in results[6]]
+    matrices = [states(0), [turn(v) for v in states(3)], states(4), [turn(v) for v in states(6)]]
+    updated = adam_all(grads, matrices)
+    for m, result in zip((0, 3, 4, 6), updated):
+        results[m] = [turn(v) for v in result] if m in (3, 6) else result
     small = [states(1), [turn(v) for v in states(2)], states(5), states(7), states(8)]
-    for m, result in zip((1, 2, 5, 7, 8), small_adam(total, small)):
+    updated = small_adam(total, small)
+    for m, result in zip((1, 2, 5, 7, 8), updated):
         results[m] = [turn(v) for v in result] if m == 2 else result
     return (output, grad_tokens) + tuple(r[kind] for kind in range(4) for r in results)
 

time: 320 us -> 311 us (0.972); the launches traced: 314 us -> 310 us
  waiting for transfers between devices: 88.7 us -> 109 us
  starting transfers between devices: 71.2 us -> 58.1 us
  local copies, waits for them, and re-layouts: 29.3 us -> 19.7 us
  Pallas kernels: 103 us -> 107 us
    ppermute x7, waiting for transfers between devices: 0.02 us -> 13.5 us  [xor_dp(): return lax.ppermute(x, dp, [(i, i ^ s) for i in range(n_x * n_z)])]
    ppermute x24 -> x18, starting transfers between devices: 35.2 us -> 23.6 us  [xor_z(): return lax.ppermute(x, 'z', [(i, i ^ s) for i in range(n_z)])]
    ppermute x28 -> x30, waiting for transfers between devices: 54.6 us -> 62.4 us  [swap(): return lax.ppermute(x, axis, [(0, 1), (1, 0)])]
    unnamed x120 -> x124, local copies, waits for them, and re-layouts: 17.1 us -> 10.6 us
    convert_element_type x8 -> x4, other arithmetic: 5.67 us -> 1.33 us  [scatter_half(): away = (own[1].astype(f32) + recv[1].astype(f32)).astype(bf16)]
    pallas_call x25 -> x26, Pallas kernels: 103 us -> 107 us  [call(): pl.pallas_call(kernel, in_specs=specs, out_shape=[jax.ShapeDtypeStruct(sh...]
    slice x12 -> x0, local copies, waits for them, and re-layouts: 4.05 us -> none  [the longest x4 2.88 us: scatter_terms(): near[s * slab:(s + 1) * slab]]
    ppermute x28 -> x30, starting transfers between devices: 23 us -> 21.2 us  [swap(): return lax.ppermute(x, axis, [(0, 1), (1, 0)])]
  transfers between devices with their start and end apart: 59 -> 55, of which waited for: 18 -> 18; matrix products, arithmetic and copies ran while one was open for 12% -> 8% of each run, Pallas kernels for 28% -> 29%
where the time goes in v1:
time: 311 us; the launch traced here: 310 us
  waiting for transfers between devices  109 us (35%)
  Pallas kernels  107 us (34%)
  starting transfers between devices  58.1 us (19%)
  local copies, waits for them, and re-layouts  19.7 us (6%)
  other arithmetic  11.7 us (4%)
    pallas_call x26, Pallas kernels, call(): pl.pallas_call(kernel, in_specs=specs, out_shape=[jax.ShapeDtypeStruct(sh...  107 us
    ppermute x30, waiting for transfers between devices, swap(): return lax.ppermute(x, axis, [(0, 1), (1, 0)])  62.4 us
    ppermute x18, waiting for transfers between devices, xor_z(): return lax.ppermute(x, 'z', [(i, i ^ s) for i in range(n_z)])  32.6 us
    ppermute x18, starting transfers between devices, xor_z(): return lax.ppermute(x, 'z', [(i, i ^ s) for i in range(n_z)])  23.6 us
    ppermute x30, starting transfers between devices, swap(): return lax.ppermute(x, axis, [(0, 1), (1, 0)])  21.2 us
    ppermute x7, waiting for transfers between devices, xor_dp(): return lax.ppermute(x, dp, [(i, i ^ s) for i in range(n_x * n_z)])  13.5 us
    ppermute x7, starting transfers between devices, xor_dp(): return lax.ppermute(x, dp, [(i, i ^ s) for i in range(n_x * n_z)])  13.4 us
    unnamed x124, local copies, waits for them, and re-layouts  10.6 us
  transfers between devices with their start and end apart: 55, of which 18 were waited for; matrix products, arithmetic and copies ran while one was open for 8% of the time, Pallas kernels for 29%

profile of v1, /device:TPU:0, one launch (start us, length us, event | category | flops | bytes accessed | tf_op | source)
XLA Modules:
  0.0 310.4 jit_solution(1305441026719901403)
XLA Ops:
  2.7 6.0 %collective-permute-start.6 = (bf16[64,512]{1,0:T(8,128)(2,1)}, bf16[64,512]{1,0:T(8,128)(2,1)S(1)}, u32[]{:S(2)}, u32[]{:S(2)}) collective-permute-start(bf16[64,512]{1,0:T(8,128)(2,1)} %get-tuple-element.143.refs_0_), channel_id=1, source_target_pairs={{0,28},{4,24},{8,20},{12,16},{16,12},{20,8},{24,4},{28,0},{1,29},{... | collective-permute-start | bytes 196616 | tf_op jit(solution)/shard_map/ppermute | solution.py:701
  29.0 13.5 %collective-permute-done.1.refs_2_ = bf16[64,512]{1,0:T(8,128)(2,1)S(1)} collective-permute-done((bf16[64,512]{1,0:T(8,128)(2,1)S(1)}, bf16[64,512]{1,0:T(8,128)(2,1)S(1)}, u32[]{:S(2)}, u32[]{:S(2)}) %collective-permute-start.1) | collective-permute-done | bytes 65568 | tf_op jit(solution)/shard_map/ppermute | solution.py:701
  63.0 7.9 %shard_map.628 = (f32[400,512]{1,0:T(8,128)}, bf16[400,512]{1,0:T(8,128)(2,1)}, bf16[2,8,64,128]{3,2,1,0:T(8,128)(2,1)}, bf16[2,8,64,128]{3,2,1,0:T(8,128)(2,1)}...) custom-call(f32[2,196,512]{2,1,0:T(8,128)} %copy.84.refs_0_, ...), custom_call_target="tpu_custom_call" | custom-call | tf_op jit(solution)/shard_map/pallas_call | solution.py:122
  71.0 9.8 %collective-permute-done.20.refs_2_ = bf16[128,512]{1,0:T(8,128)(2,1)S(1)} collective-permute-done((bf16[128,512]{1,0:T(8,128)(2,1)}, bf16[128,512]{1,0:T(8,128)(2,1)S(1)}, u32[]{:S(2)}, u32[]{:S(2)}) %collective-permute-start.20) | collective-permute-done | bytes 131104 | tf_op jit(solution)/shard_map/ppermute | solution.py:698
  86.7 5.0 %collective-permute-done.26.refs_2_ = bf16[128,1024]{1,0:T(8,128)(2,1)S(1)} collective-permute-done((bf16[128,1024]{1,0:T(8,128)(2,1)S(1)}, bf16[128,1024]{1,0:T(8,128)(2,1)S(1)}, u32[]{:S(2)}, u32[]{:S(2)}) %collective-permute-start.26) | collective-permute-done | bytes 262176 | tf_op jit(solution)/shard_map/ppermute | solution.py:698
  98.0 4.9 %shard_map.631 = (f32[400,512]{1,0:T(8,128)}, bf16[400,512]{1,0:T(8,128)(2,1)}, bf16[400,1024]{1,0:T(8,128)(2,1)}, bf16[400,1024]{1,0:T(8,128)(2,1)}, bf16[400,512]{1,0:T(8,128)(2,1)}) custom-call(f32[400,512]{1,0:T(8,128)} %get-tuple-element.144.h_ref, bf16[400,512]{1,0:T(8,128)(2,1)} %get-tuple-element.145.own_ref, bf16[400,512]{1,0:T(8,128)(2,1)} %copy-done.11, ...), custom_call_target="tpu_custom_call" | custom-call | tf_op jit(solution)/shard_map/pallas_call | solution.py:122
  105.7 9.3 %collective-permute-done.17.refs_2_ = bf16[400,512]{1,0:T(8,128)(2,1)S(1)} collective-permute-done((bf16[400,512]{1,0:T(8,128)(2,1)}, bf16[400,512]{1,0:T(8,128)(2,1)S(1)}, u32[]{:S(2)}, u32[]{:S(2)}) %collective-permute-start.17) | collective-permute-done | bytes 409632 | tf_op jit(solution)/shard_map/ppermute | solution.py:695
  115.8 8.6 %shard_map.634 = (f32[400,512]{1,0:T(8,128)}, bf16[400,512]{1,0:T(8,128)(2,1)}, bf16[2,8,64,128]{3,2,1,0:T(8,128)(2,1)}, bf16[2,8,64,128]{3,2,1,0:T(8,128)(2,1)}...) custom-call(f32[400,512]{1,0:T(8,128)} %get-tuple-element.147.refs_0, ...), custom_call_target="tpu_custom_call" | custom-call | tf_op jit(solution)/shard_map/pallas_call | solution.py:122
  125.9 9.7 %collective-permute-done.23.recv_ref = bf16[400,512]{1,0:T(8,128)(2,1)S(1)} collective-permute-done((bf16[400,512]{1,0:T(8,128)(2,1)}, bf16[400,512]{1,0:T(8,128)(2,1)S(1)}, u32[]{:S(2)}, u32[]{:S(2)}) %collective-permute-start.23) | collective-permute-done | bytes 409632 | tf_op jit(solution)/shard_map/ppermute | solution.py:695
  136.4 5.0 %shard_map.637 = (f32[400,512]{1,0:T(8,128)}, bf16[400,512]{1,0:T(8,128)(2,1)}, bf16[400,1024]{1,0:T(8,128)(2,1)}, bf16[400,1024]{1,0:T(8,128)(2,1)}, bf16[400,512]{1,0:T(8,128)(2,1)}) custom-call(f32[400,512]{1,0:T(8,128)} %get-tuple-element.150.h_ref.refs_3_, bf16[400,512]{1,0:T(8,128)(2,1)} %get-tuple-element.151.own_ref, bf16[400,512]{1,0:T(8,128)(2,1)} %copy-done.14, ...), custom_call_target="tpu_custom_call" | custom-call | tf_op jit(solution)/shard_map/pallas_call | solution.py:122
  146.4 5.4 %collective-permute-done.29.refs_5_ = bf16[400,512]{1,0:T(8,128)(2,1)S(1)} collective-permute-done((bf16[400,512]{1,0:T(8,128)(2,1)}, bf16[400,512]{1,0:T(8,128)(2,1)S(1)}, u32[]{:S(2)}, u32[]{:S(2)}) %collective-permute-start.29) | collective-permute-done | bytes 409632 | tf_op jit(solution)/shard_map/ppermute | solution.py:695
  152.5 4.9 %shard_map.638 = (f32[400,512]{1,0:T(8,128)}, bf16[400,512]{1,0:T(8,128)(2,1)}, bf16[400,1024]{1,0:T(8,128)(2,1)}, bf16[400,512]{1,0:T(8,128)(2,1)}, f32[8,512]{1,0:T(8,128)}, /*index=5*/f32[2,196,512]{2,1,0:T(8,128)}) custom-call(s32[4]{0:T(128)} %pad_add_fusion.place_ref.refs_0_, s32[1]{0:T(128)S(6)} %copy.85.refs_1_, f32[2,196,512]{2,1,0:T(8,128)} %copy.83.refs_2_, ...), custom_call_target="tpu_custom_call" | custom-call | tf_op jit(solution)/shard_map/pallas_call | solution.py:122
  160.7 4.0 %shard_map.648 = (bf16[256,1024]{1,0:T(8,128)(2,1)}, bf16[256,1024]{1,0:T(8,128)(2,1)}, bf16[2,256,1024]{2,1,0:T(8,128)(2,1)}) custom-call(s32[4]{0:T(128)} %pad_add_fusion.place_ref.refs_0_, bf16[400,512]{1,0:T(8,128)(2,1)} %get-tuple-element.196.c_ref, bf16[400,1024]{1,0:T(8,128)(2,1)} %get-tuple-element.197.du_ref, ...), custom_call_target="tpu_custom_call" | custom-call | tf_op jit(solution)/shard_map/pallas_call | solution.py:122
  167.6 12.2 %shard_map.640 = (f32[400,512]{1,0:T(8,128)}, bf16[400,512]{1,0:T(8,128)(2,1)}, bf16[400,768]{1,0:T(8,128)(2,1)}, bf16[400,512]{1,0:T(8,128)(2,1)}, f32[8,512]{1,0:T(8,128)}, /*index=5*/f32[2,256,64]{2,1,0:T(8,128)}) custom-call(f32[400,512]{1,0:T(8,128)} %get-tuple-element.157.g_ref, bf16[400,512]{1,0:T(8,128)(2,1)} %get-tuple-element.158.own_ref, ...), custom_call_target="tpu_custom_call" | custom-call | tf_op jit(solution)/shard_map/pallas_call | solution.py:122
  191.0 5.4 %collective-permute-done.32.refs_2_ = bf16[400,512]{1,0:T(8,128)(2,1)} collective-permute-done((bf16[400,512]{1,0:T(8,128)(2,1)S(1)}, bf16[400,512]{1,0:T(8,128)(2,1)}, u32[]{:S(2)}, u32[]{:S(2)}) %collective-permute-start.32) | collective-permute-done | bytes 409632 | tf_op jit(solution)/shard_map/ppermute | solution.py:695
  196.4 5.0 %shard_map.641 = (f32[400,512]{1,0:T(8,128)}, bf16[400,512]{1,0:T(8,128)(2,1)}, bf16[400,1024]{1,0:T(8,128)(2,1)}, bf16[400,512]{1,0:T(8,128)(2,1)}, f32[8,512]{1,0:T(8,128)}) custom-call(f32[400,512]{1,0:T(8,128)} %get-tuple-element.163.refs_0_, bf16[400,512]{1,0:T(8,128)(2,1)} %get-tuple-element.164.refs_1_, ...), custom_call_target="tpu_custom_call" | custom-call | tf_op jit(solution)/shard_map/pallas_call | solution.py:122
  202.9 4.0 %shard_map.646 = (bf16[256,1024]{1,0:T(8,128)(2,1)}, bf16[256,1024]{1,0:T(8,128)(2,1)}, bf16[2,256,1024]{2,1,0:T(8,128)(2,1)}) custom-call(s32[4]{0:T(128)} %pad_add_fusion.place_ref.refs_0_, bf16[400,512]{1,0:T(8,128)(2,1)} %get-tuple-element.182.c_ref, bf16[400,1024]{1,0:T(8,128)(2,1)} %get-tuple-element.183.du_ref, ...), custom_call_target="tpu_custom_call" | custom-call | tf_op jit(solution)/shard_map/pallas_call | solution.py:122
  210.1 6.1 %collective-permute-done.44 = bf16[256,512]{1,0:T(8,128)(2,1)S(1)} collective-permute-done((bf16[256,512]{1,0:T(8,128)(2,1)S(1)}, bf16[256,512]{1,0:T(8,128)(2,1)S(1)}, u32[]{:S(2)}, u32[]{:S(2)}) %collective-permute-start.44) | collective-permute-done | bytes 262176 | tf_op jit(solution)/shard_map/ppermute | solution.py:695
  217.1 12.3 %shard_map.642 = (f32[400,512]{1,0:T(8,128)}, bf16[400,512]{1,0:T(8,128)(2,1)}, bf16[400,768]{1,0:T(8,128)(2,1)}, bf16[400,512]{1,0:T(8,128)(2,1)}, f32[8,512]{1,0:T(8,128)}, /*index=5*/f32[2,256,64]{2,1,0:T(8,128)}) custom-call(f32[400,512]{1,0:T(8,128)} %get-tuple-element.166.g_ref, bf16[400,512]{1,0:T(8,128)(2,1)} %get-tuple-element.167.own_ref, ...), custom_call_target="tpu_custom_call" | custom-call | tf_op jit(solution)/shard_map/pallas_call | solution.py:122
  235.5 10.5 %collective-permute-done.34.recv_ref = bf16[400,512]{1,0:T(8,128)(2,1)} collective-permute-done((bf16[400,512]{1,0:T(8,128)(2,1)}, bf16[400,512]{1,0:T(8,128)(2,1)}, u32[]{:S(2)}, u32[]{:S(2)}) %collective-permute-start.34) | collective-permute-done | bytes 409632 | tf_op jit(solution)/shard_map/ppermute | solution.py:695
  258.5 13.3 %collective-permute-done.51 = f32[24,512]{1,0:T(8,128)S(1)} collective-permute-done((f32[24,512]{1,0:T(8,128)S(1)}, f32[24,512]{1,0:T(8,128)S(1)}, u32[]{:S(2)}, u32[]{:S(2)}) %collective-permute-start.51) | collective-permute-done | bytes 49184 | tf_op jit(solution)/shard_map/ppermute | solution.py:695
  290.8 4.2 %collective-permute-done.48.refs_6_ = bf16[64,1536]{1,0:T(8,128)(2,1)S(1)} collective-permute-done((bf16[64,1536]{1,0:T(8,128)(2,1)S(1)}, bf16[64,1536]{1,0:T(8,128)(2,1)S(1)}, u32[]{:S(2)}, u32[]{:S(2)}) %collective-permute-start.48) | collective-permute-done | bytes 196640 | tf_op jit(solution)/shard_map/ppermute | solution.py:698
  297.0 8.2 %collective-permute-done.41.refs_2_ = bf16[64,1536]{1,0:T(8,128)(2,1)S(1)} collective-permute-done((bf16[64,1536]{1,0:T(8,128)(2,1)S(1)}, bf16[64,1536]{1,0:T(8,128)(2,1)S(1)}, u32[]{:S(2)}, u32[]{:S(2)}) %collective-permute-start.41) | collective-permute-done | bytes 196640 | tf_op jit(solution)/shard_map/ppermute | solution.py:698
  305.9 4.3 %shard_map.649 = (f32[2,3,64,128]{3,2,1,0:T(8,128)}, f32[2,3,64,128]{3,2,1,0:T(8,128)}, f32[2,3,64,128]{3,2,1,0:T(8,128)}, f32[2,3,64,128]{3,2,1,0:T(8,128)}, f3...) custom-call(bf16[64,1536]{1,0:T(8,128)(2,1)} %get-tuple-element.253., ...), custom_call_target="tpu_custom_call" | custom-call | tf_op jit(solution)/shard_map/pallas_call | solution.py:122
  (277 shorter events, 128.7 us)
Async XLA Ops:
  2.7 19.8 %collective-permute-start.6 = (bf16[64,512]{1,0:T(8,128)(2,1)}, bf16[64,512]{1,0:T(8,128)(2,1)S(1)}, u32[]{:S(2)}, u32[]{:S(2)}) collective-permute-start(bf16[64,512]{1,0:T(8,128)(2,1)} %get-tuple-element.143.refs_0_), channel_id=1, source_target_pairs={{0,28},{4,24},{8,20},{12,16},{16,12},{20,8},{24,4},{28,0},{1,29},{... | collective-permute-start | bytes 196616 | tf_op jit(solution)/shard_map/ppermute | solution.py:701
  22.5 23.1 %collective-permute-start.14 = (bf16[128,1024]{1,0:T(8,128)(2,1)}, bf16[128,1024]{1,0:T(8,128)(2,1)S(1)}, u32[]{:S(2)}, u32[]{:S(2)}) collective-permute-start(bf16[128,1024]{1,0:T(8,128)(2,1)} %shard_map.629.refs_0_), channel_id=1, source_target_pairs={{0,24},{8,16},{16,8},{24,0},{1,25},{9,17},{17,9},{25,1},{2,26},{10... | collective-permute-start | bytes 786440 | tf_op jit(solution)/shard_map/ppermute | solution.py:698
  23.7 23.9 %collective-permute-start.13 = (bf16[128,1024]{1,0:T(8,128)(2,1)}, bf16[128,1024]{1,0:T(8,128)(2,1)S(1)}, u32[]{:S(2)}, u32[]{:S(2)}) collective-permute-start(bf16[128,1024]{1,0:T(8,128)(2,1)} %shard_map.629.refs_0_), channel_id=1, source_target_pairs={{0,16},{8,24},{16,0},{24,8},{1,17},{9,25},{17,1},{25,9},{2,18},{10... | collective-permute-start | bytes 786440 | tf_op jit(solution)/shard_map/ppermute | solution.py:698
  25.1 22.5 %collective-permute-start.12 = (bf16[128,1024]{1,0:T(8,128)(2,1)}, bf16[128,1024]{1,0:T(8,128)(2,1)S(1)}, u32[]{:S(2)}, u32[]{:S(2)}) collective-permute-start(bf16[128,1024]{1,0:T(8,128)(2,1)} %shard_map.629.refs_0_), channel_id=1, source_target_pairs={{0,8},{8,0},{16,24},{24,16},{1,9},{9,1},{17,25},{25,17},{2,10},{10... | collective-permute-start | bytes 786440 | tf_op jit(solution)/shard_map/ppermute | solution.py:698
  51.2 45.7 %collective-permute-start.15 = (bf16[512,1024]{1,0:T(8,128)(2,1)}, bf16[512,1024]{1,0:T(8,128)(2,1)S(1)}, u32[]{:S(2)}, u32[]{:S(2)}) collective-permute-start(bf16[512,1024]{1,0:T(8,128)(2,1)} %shard_map.630.w0.refs_7_), channel_id=1, source_target_pairs={{0,1},{1,0},{2,3},{3,2},{4,5},{5,4},{6,7},{7,6},{8,9},{9,8},{10,11... | collective-permute-start | bytes 3145736 | tf_op jit(solution)/shard_map/ppermute | solution.py:695
  53.5 17.4 %collective-permute-start.21 = (bf16[128,512]{1,0:T(8,128)(2,1)}, bf16[128,512]{1,0:T(8,128)(2,1)S(1)}, u32[]{:S(2)}, u32[]{:S(2)}) collective-permute-start(bf16[128,512]{1,0:T(8,128)(2,1)} %shard_map.632.refs_0_), channel_id=1, source_target_pairs={{0,24},{8,16},{16,8},{24,0},{1,25},{9,17},{17,9},{25,1},{2,26},{10... | collective-permute-start | bytes 393224 | tf_op jit(solution)/shard_map/ppermute | solution.py:698
  56.0 24.8 %collective-permute-start.20 = (bf16[128,512]{1,0:T(8,128)(2,1)}, bf16[128,512]{1,0:T(8,128)(2,1)S(1)}, u32[]{:S(2)}, u32[]{:S(2)}) collective-permute-start(bf16[128,512]{1,0:T(8,128)(2,1)} %shard_map.632.refs_0_), channel_id=1, source_target_pairs={{0,16},{8,24},{16,0},{24,8},{1,17},{9,25},{17,1},{25,9},{2,18},{10... | collective-permute-start | bytes 393224 | tf_op jit(solution)/shard_map/ppermute | solution.py:698
  58.4 22.4 %collective-permute-start.19 = (bf16[128,512]{1,0:T(8,128)(2,1)}, bf16[128,512]{1,0:T(8,128)(2,1)S(1)}, u32[]{:S(2)}, u32[]{:S(2)}) collective-permute-start(bf16[128,512]{1,0:T(8,128)(2,1)} %shard_map.632.refs_0_), channel_id=1, source_target_pairs={{0,8},{8,0},{16,24},{24,16},{1,9},{9,1},{17,25},{25,17},{2,10},{10... | collective-permute-start | bytes 393224 | tf_op jit(solution)/shard_map/ppermute | solution.py:698
  59.7 23.6 %collective-permute-start.27 = (bf16[128,1024]{1,0:T(8,128)(2,1)}, bf16[128,1024]{1,0:T(8,128)(2,1)S(1)}, u32[]{:S(2)}, u32[]{:S(2)}) collective-permute-start(bf16[128,1024]{1,0:T(8,128)(2,1)} %shard_map.635.refs_0_), channel_id=1, source_target_pairs={{0,24},{8,16},{16,8},{24,0},{1,25},{9,17},{17,9},{25,1},{2,26},{10... | collective-permute-start | bytes 786440 | tf_op jit(solution)/shard_map/ppermute | solution.py:698
  70.9 20.8 %collective-permute-start.26 = (bf16[128,1024]{1,0:T(8,128)(2,1)S(1)}, bf16[128,1024]{1,0:T(8,128)(2,1)S(1)}, u32[]{:S(2)}, u32[]{:S(2)}) collective-permute-start(bf16[128,1024]{1,0:T(8,128)(2,1)S(1)} %copy-done.7), channel_id=1, source_target_pairs={{0,16},{8,24},{16,0},{24,8},{1,17},{9,25},{17,1},{25,9},{2,18},{10... | collective-permute-start | bytes 786440 | tf_op jit(solution)/shard_map/ppermute | solution.py:698
  96.8 29.1 %collective-permute-start.28 = (bf16[512,1024]{1,0:T(8,128)(2,1)}, bf16[512,1024]{1,0:T(8,128)(2,1)S(1)}, u32[]{:S(2)}, u32[]{:S(2)}) collective-permute-start(bf16[512,1024]{1,0:T(8,128)(2,1)} %shard_map.636.w0.refs_9_), channel_id=1, source_target_pairs={{0,1},{1,0},{2,3},{3,2},{4,5},{5,4},{6,7},{7,6},{8,9},{9,8},{10,11... | collective-permute-start | bytes 3145736 | tf_op jit(solution)/shard_map/ppermute | solution.py:695
  160.7 26.4 %collective-permute-start.30 = (f32[2,196,512]{2,0,1:T(2,128)S(1)}, f32[2,196,512]{2,0,1:T(2,128)S(1)}, u32[]{:S(2)}, u32[]{:S(2)}) collective-permute-start(f32[2,196,512]{2,0,1:T(2,128)S(1)} %copy.79), channel_id=1, source_target_pairs={{0,1},{1,0},{2,3},{3,2},{4,5},{5,4},{6,7},{7,6},{8,9},{9,8},{10,11... | collective-permute-start | bytes 2408456 | tf_op jit(solution)/shard_map/ppermute | solution.py:695
  164.7 43.4 %collective-permute-start.45 = (bf16[2,256,1024]{2,1,0:T(8,128)(2,1)}, bf16[2,256,1024]{2,1,0:T(8,128)(2,1)S(1)}, u32[]{:S(2)}, u32[]{:S(2)}) collective-permute-start(bf16[2,256,1024]{2,1,0:T(8,128)(2,1)} %get-tuple-element.201), channel_id=1, source_target_pairs={{0,1},{1,0},{2,3},{3,2},{4,5},{5,4},{6,7},{7,6},{8,9},{9,8},{10,11... | collective-permute-start | bytes 3145736 | tf_op jit(solution)/shard_map/ppermute | solution.py:695
  184.3 22.6 %collective-permute-start.43 = (bf16[2,256,512]{2,1,0:T(8,128)(2,1)}, bf16[2,256,512]{2,1,0:T(8,128)(2,1)S(1)}, u32[]{:S(2)}, u32[]{:S(2)}) collective-permute-start(bf16[2,256,512]{2,1,0:T(8,128)(2,1)} %get-tuple-element.194), channel_id=1, source_target_pairs={{0,1},{1,0},{2,3},{3,2},{4,5},{5,4},{6,7},{7,6},{8,9},{9,8},{10,11... | collective-permute-start | bytes 1572872 | tf_op jit(solution)/shard_map/ppermute | solution.py:695
  206.9 45.1 %collective-permute-start.38 = (bf16[2,256,1024]{2,1,0:T(8,128)(2,1)}, bf16[2,256,1024]{2,1,0:T(8,128)(2,1)S(1)}, u32[]{:S(2)}, u32[]{:S(2)}) collective-permute-start(bf16[2,256,1024]{2,1,0:T(8,128)(2,1)} %get-tuple-element.187), channel_id=1, source_target_pairs={{0,1},{1,0},{2,3},{3,2},{4,5},{5,4},{6,7},{7,6},{8,9},{9,8},{10,11... | collective-permute-start | bytes 3145736 | tf_op jit(solution)/shard_map/ppermute | solution.py:695
  209.2 44.0 %collective-permute-start.46 = (bf16[256,1024]{1,0:T(8,128)(2,1)}, bf16[256,1024]{1,0:T(8,128)(2,1)}, u32[]{:S(2)}, u32[]{:S(2)}) collective-permute-start(bf16[256,1024]{1,0:T(8,128)(2,1)} %fusion.8), channel_id=1, source_target_pairs={{0,4},{4,0},{1,5},{5,1},{2,6},{6,2},{3,7},{7,3},{8,12},{12,8},{9,1... | collective-permute-start | bytes 1572872 | tf_op jit(solution)/shard_map/ppermute | solution.py:695
  233.7 17.0 %collective-permute-start.36 = (bf16[2,256,512]{2,1,0:T(8,128)(2,1)}, bf16[2,256,512]{2,1,0:T(8,128)(2,1)S(1)}, u32[]{:S(2)}, u32[]{:S(2)}) collective-permute-start(bf16[2,256,512]{2,1,0:T(8,128)(2,1)} %get-tuple-element.180), channel_id=1, source_target_pairs={{0,1},{1,0},{2,3},{3,2},{4,5},{5,4},{6,7},{7,6},{8,9},{9,8},{10,11... | collective-permute-start | bytes 1572872 | tf_op jit(solution)/shard_map/ppermute | solution.py:695
  250.8 23.0 %collective-permute-start.37 = (bf16[256,512]{1,0:T(8,128)(2,1)S(1)}, bf16[256,512]{1,0:T(8,128)(2,1)S(1)}, u32[]{:S(2)}, u32[]{:S(2)}) collective-permute-start(bf16[256,512]{1,0:T(8,128)(2,1)S(1)} %fusion.19), channel_id=1, source_target_pairs={{0,4},{4,0},{1,5},{5,1},{2,6},{6,2},{3,7},{7,3},{8,12},{12,8},{9,1... | collective-permute-start | bytes 786440 | tf_op jit(solution)/shard_map/ppermute | solution.py:695
  252.2 21.8 %collective-permute-start.39 = (bf16[256,1024]{1,0:T(8,128)(2,1)S(1)}, bf16[256,1024]{1,0:T(8,128)(2,1)S(1)}, u32[]{:S(2)}, u32[]{:S(2)}) collective-permute-start(bf16[256,1024]{1,0:T(8,128)(2,1)S(1)} %fusion.11), channel_id=1, source_target_pairs={{0,4},{4,0},{1,5},{5,1},{2,6},{6,2},{3,7},{7,3},{8,12},{12,8},{9,1... | collective-permute-start | bytes 1572872 | tf_op jit(solution)/shard_map/ppermute | solution.py:695
  255.3 26.6 %collective-permute-start.35 = (f32[2,196,512]{2,0,1:T(2,128)S(1)}, f32[2,196,512]{2,0,1:T(2,128)S(1)}, u32[]{:S(2)}, u32[]{:S(2)}) collective-permute-start(f32[2,196,512]{2,0,1:T(2,128)S(1)} %copy.81), channel_id=1, source_target_pairs={{0,1},{1,0},{2,3},{3,2},{4,5},{5,4},{6,7},{7,6},{8,9},{9,8},{10,11... | collective-permute-start | bytes 2408456 | tf_op jit(solution)/shard_map/ppermute | solution.py:695
  255.4 16.4 %collective-permute-start.51 = (f32[24,512]{1,0:T(8,128)S(1)}, f32[24,512]{1,0:T(8,128)S(1)}, u32[]{:S(2)}, u32[]{:S(2)}) collective-permute-start(f32[24,512]{1,0:T(8,128)S(1)} %add.183), channel_id=1, source_target_pairs={{0,4},{4,0},{1,5},{5,1},{2,6},{6,2},{3,7},{7,3},{8,12},{12,8},{9,1... | collective-permute-start | bytes 147464 | tf_op jit(solution)/shard_map/ppermute | solution.py:695
  257.3 20.1 %collective-permute-start.49 = (bf16[64,1536]{1,0:T(8,128)(2,1)S(1)}, bf16[64,1536]{1,0:T(8,128)(2,1)S(1)}, u32[]{:S(2)}, u32[]{:S(2)}) collective-permute-start(bf16[64,1536]{1,0:T(8,128)(2,1)S(1)} %get-tuple-element.248), channel_id=1, source_target_pairs={{0,24},{8,16},{16,8},{24,0},{1,25},{9,17},{17,9},{25,1},{2,26},{10... | collective-permute-start | bytes 589832 | tf_op jit(solution)/shard_map/ppermute | solution.py:698
  277.8 17.1 %collective-permute-start.48 = (bf16[64,1536]{1,0:T(8,128)(2,1)S(1)}, bf16[64,1536]{1,0:T(8,128)(2,1)S(1)}, u32[]{:S(2)}, u32[]{:S(2)}) collective-permute-start(bf16[64,1536]{1,0:T(8,128)(2,1)S(1)} %get-tuple-element.251), channel_id=1, source_target_pairs={{0,16},{8,24},{16,0},{24,8},{1,17},{9,25},{17,1},{25,9},{2,18},{10... | collective-permute-start | bytes 589832 | tf_op jit(solution)/shard_map/ppermute | solution.py:698
  281.9 23.3 %collective-permute-start.41 = (bf16[64,1536]{1,0:T(8,128)(2,1)S(1)}, bf16[64,1536]{1,0:T(8,128)(2,1)S(1)}, u32[]{:S(2)}, u32[]{:S(2)}) collective-permute-start(bf16[64,1536]{1,0:T(8,128)(2,1)S(1)} %get-tuple-element.255), channel_id=1, source_target_pairs={{0,16},{8,24},{16,0},{24,8},{1,17},{9,25},{17,1},{25,9},{2,18},{10... | collective-permute-start | bytes 589832 | tf_op jit(solution)/shard_map/ppermute | solution.py:698
  (92 other events, 969.0 us)

commit v2 on v1

--- a/solution.py
+++ b/solution.py
@@ -128,10 +128,10 @@
     )(*args)
 
 
-def load_images(images_ref, buffer, images):
+def load_images(images_ref, buffer, images, first=0):
     cells, width = images_ref.shape[1:]
     for i in range(images):
-        buffer[i * ROWS : i * ROWS + cells, :] = images_ref[i]
+        buffer[i * ROWS : i * ROWS + cells, :] = images_ref[first + i]
         buffer[i * ROWS + cells : (i + 1) * ROWS, :] = jnp.zeros((ROWS - cells, width), f32)
 
 
@@ -141,7 +141,7 @@
         out[i] = value[i * ROWS : i * ROWS + cells, :]
 
 
-def attn_fwd(layer, gains, offsets, source, weights, biases, pos, pick):
+def attn_fwd(layer, gains, offsets, source, weights, biases, pos, pick, cuts):
     first = layer == 0
     win_rows, rows = pick.shape
     *weights, at = weights
@@ -156,7 +156,8 @@
     def kernel(*refs):
         src = refs[:n_src]
         gain_ref, off_ref, w0, w1, b0, b1, pos_ref, pick_ref = refs[n_src : n_src + 8]
-        h_ref, a_ref, q_ref, k_ref, v_ref, prob_ref, mixed_ref, part_ref, mw_ref = refs[n_src + 8 :]
+        h_ref, a_ref, q_ref, k_ref, v_ref, prob_ref, mixed_ref = refs[n_src + 8 : n_src + 15]
+        part_refs, mw_ref = refs[n_src + 15 : -1], refs[-1]
         if first:
             load_images(src[0], h_ref, rows // ROWS)
             hidden = h_ref[...]
@@ -198,7 +199,8 @@
         for g, w in enumerate((w0, w1)):
             term = dot(mixed[:, g * local : (g + 1) * local], w[:, at + 3 * local : at + 4 * local], 1, 1)
             part = term if part is None else part + term
-        part_ref[...] = part.astype(bf16)
+        for i, part_ref in enumerate(part_refs):
+            part_ref[...] = part[i * rows // cuts : (i + 1) * rows // cuts].astype(bf16)
 
     outs = [
         ((rows, width), f32),
@@ -208,8 +210,7 @@
         ((GROUPS, panes, SLOT, local), bf16),
         ((panes, GROUPS, heads * SLOT, SLOT), f32),
         ((rows, GROUPS * local), bf16),
-        ((rows, width), bf16),
-    ]
+    ] + [((rows // cuts, width), bf16)] * cuts
     return call(
         kernel,
         outs,
@@ -224,15 +225,16 @@
     )
 
 
-def mlp_fwd(layer, hidden, own, recv, gains, offsets, weights, wide_biases):
+def mlp_fwd(layer, cut_index, hidden, own, recv, gains, offsets, weights, wide_biases):
     *weights, at = weights
-    rows, width = hidden.shape
+    rows, width = own.shape
+    first = cut_index * rows
     local = wide_biases[0].shape[1]
 
     def kernel(
         h_ref, own_ref, recv_ref, gain_ref, off_ref, w0, w1, b0, b1, h1_ref, c_ref, z_ref, s_ref, p_ref
     ):
-        h1 = h_ref[...] + (own_ref[...].astype(f32) + recv_ref[...].astype(f32) + off_ref[layer, 2:3])
+        h1 = h_ref[first : first + rows] + (own_ref[...].astype(f32) + recv_ref[...].astype(f32) + off_ref[layer, 2:3])
         h1_ref[...] = h1
         normed, _ = unit_norm(h1)
         c = (normed * gain_ref[layer, 1:2] + off_ref[layer, 1:2]).astype(bf16)
@@ -259,7 +261,7 @@
     return call(kernel, outs, hidden, own, recv, gains, offsets, *weights, *wide_biases)
 
 
-def mlp_bwd(layer, last, source, gains, offsets, slope, weights):
+def mlp_bwd(layer, last, cut_index, source, gains, offsets, slope, weights):
     *weights, at = weights
     rows, width = source[3].shape
     local = slope.shape[1] // GROUPS
@@ -273,12 +275,13 @@
         if last:
             place_ref, count_ref = src[:2]
             images = rows // ROWS
-            load_images(src[2], g_ref, images)
+            load_images(src[2], g_ref, images, cut_index * images)
             result = src[3][...] + (src[4][...].astype(f32) + src[5][...].astype(f32) + off_ref[layer, 3:4])
             out_ref = refs[n_src + 10]
             cells = out_ref.shape[1]
             for i in range(images):
-                keep = jnp.where(place_ref[0] * images + i < count_ref[0], 1.0, 0.0)
+                slot = place_ref[0] * src[2].shape[0] + cut_index * images + i
+                keep = jnp.where(slot < count_ref[0], 1.0, 0.0)
                 out_ref[i] = result[i * ROWS : i * ROWS + cells, :] * keep
                 g_ref[i * ROWS : (i + 1) * ROWS, :] = g_ref[i * ROWS : (i + 1) * ROWS, :] * keep
             grad = g_ref[...]
@@ -338,47 +341,64 @@
 
 
 def mlp_grads(place, c, du_b, z, grad_b, halves, slab):
-    width = c.shape[1]
-    local = z.shape[1] // GROUPS
-
-    def kernel(place_ref, c_ref, du_ref, z_ref, g_ref, *outs):
+    width = c[0].shape[1]
+    local = z[0].shape[1] // GROUPS
+    cuts = len(c)
+
+    def kernel(place_ref, *refs):
+        c_refs, du_refs = refs[:cuts], refs[cuts : 2 * cuts]
+        z_refs, g_refs = refs[2 * cuts : 3 * cuts], refs[3 * cuts : 4 * cuts]
+        outs = refs[4 * cuts :]
         full = outs[-1]
+
+        def over_rows(lefts, rights, cols):
+            return sum(dot(a[...], b[:, cols], 0, 0) for a, b in zip(lefts, rights))
+
         for g, out in enumerate((outs[:-2], outs[-2:-1])):
             cols = slice(g * local, (g + 1) * local)
-            full[:, :local] = dot(c_ref[...], du_ref[:, cols], 0, 0).astype(bf16)
-            full[:, local:] = dot(g_ref[...], z_ref[:, cols], 0, 0).astype(bf16)
+            full[:, :local] = over_rows(c_refs, du_refs, cols).astype(bf16)
+            full[:, local:] = over_rows(g_refs, z_refs, cols).astype(bf16)
             cut(full, out, place_ref, halves, slab)
 
     return call(
         kernel,
         grad_outs(width, 2 * local, halves),
         place,
-        c,
-        du_b,
-        z,
-        grad_b,
+        *c,
+        *du_b,
+        *z,
+        *grad_b,
         scratch=[((width, 2 * local), bf16)],
         scalars=1,
     )
 
 
 def attn_bwd(layer, grad, own, recv, h1, gains, weights, q, k, v, prob, pick):
-    rows, width = grad.shape
-    win_rows = pick.shape[0]
+    win_rows, rows = pick.shape
+    width = grad[0].shape[1]
+    cuts = len(grad)
     panes = win_rows // SLOT
     *weights, at = weights
     local = q.shape[3]
     heads = local // HEAD_DIM
     factor = HEAD_DIM ** (-0.5)
 
-    def kernel(
-        g_ref, own_ref, recv_ref, h1_ref, gain_ref, w0, w1, q_ref, k_ref, v_ref, prob_ref, pick_ref,
-        dh_ref, dhb_ref, dp_ref, part_ref, sum_ref, ds_ref, dm_ref, dw_ref, bias_ref,
-    ):
-        normed, inverse = unit_norm(h1_ref[...])
-        upstream = own_ref[...].astype(f32) + recv_ref[...].astype(f32)
+    def kernel(*refs):
+        g_refs, own_refs = refs[:cuts], refs[cuts : 2 * cuts]
+        recv_refs, h1_refs = refs[2 * cuts : 3 * cuts], refs[3 * cuts : 4 * cuts]
+        gain_ref, w0, w1, q_ref, k_ref, v_ref, prob_ref, pick_ref = refs[4 * cuts : 4 * cuts + 8]
+        dh_ref, dhb_ref, dp_ref, part_ref, sum_ref, ds_ref = refs[4 * cuts + 8 : 4 * cuts + 14]
+        dm_ref, dw_ref, bias_ref = refs[4 * cuts + 14 :]
+
+        def whole(parts):
+            return jnp.concatenate(parts, axis=0) if cuts > 1 else parts[0]
+
+        normed, inverse = unit_norm(whole([r[...] for r in h1_refs]))
+        upstream = whole(
+            [a[...].astype(f32) + b[...].astype(f32) for a, b in zip(own_refs, recv_refs)]
+        )
         d_mid, d_gain, d_off = norm_back(upstream, normed, inverse, gain_ref[layer, 1:2])
-        dh1 = g_ref[...] + d_mid
+        dh1 = whole([r[...] for r in g_refs]) + d_mid
         dh_ref[...] = dh1
         sum_ref[...] = jnp.zeros_like(sum_ref)
         sum_ref[0:1, :] = d_gain
@@ -439,10 +459,10 @@
     return call(
         kernel,
         outs,
-        grad,
-        own,
-        recv,
-        h1,
+        *grad,
+        *own,
+        *recv,
+        *h1,
         gains,
         *weights,
         q,
@@ -535,8 +555,7 @@
 
 def adam_all(parts, states):
     layers = len(parts)
-    count = len(parts[0])
-    flat = [p for terms in parts for p in terms]
+    flat = [p for groups in parts for terms in groups for p in terms]
 
     def kernel(*refs):
         blocks, refs = refs[: len(flat)], refs[len(flat) :]
@@ -548,8 +567,13 @@
             for ref, value in zip(outs[4 * member : 4 * member + 4], new):
                 ref[index] = value
 
+        used = 0
         for l in range(layers):
-            total = tree([blocks[l * count + i][...].astype(f32) for i in range(count)])
+            sums = []
+            for terms in parts[l]:
+                sums.append(tree([r[...].astype(f32) for r in blocks[used : used + len(terms)]]))
+                used += len(terms)
+            total = jnp.concatenate(sums, axis=1) if len(sums) > 1 else sums[0]
             at = 0
             for member in range(4):
                 shape = ins[3 * member].shape
@@ -564,17 +588,22 @@
 
 
 def join(place, own, recv):
-    images, cells, width = own.shape
-
-    def kernel(place_ref, own_ref, recv_ref, out_ref):
+    count = len(own)
+    _, cells, width = own[0].shape
+    each = own[0].shape[0]
+    images = count * each
+
+    def kernel(place_ref, *refs):
+        out_ref = refs[-1]
         lower = place_ref[0] == 0
         for i in range(images):
-            mine, theirs = own_ref[i], recv_ref[i]
+            mine = refs[i // each][i % each]
+            theirs = refs[count + i // each][i % each]
             out_ref[:, i, :] = jnp.where(lower, mine, theirs)
             out_ref[:, images + i, :] = jnp.where(lower, theirs, mine)
 
     outs = [((cells, 2 * images, width), f32)]
-    return call(kernel, outs, place, own, recv, scalars=1)[0]
+    return call(kernel, outs, place, *own, *recv, scalars=1)[0]
 
 
 def small_rows(layers, heads):
@@ -694,6 +723,12 @@
     def swap(x, axis):
         return lax.ppermute(x, axis, [(0, 1), (1, 0)])
 
+    def swap_each(parts):
+        received = []
+        for x in parts:
+            received.append(swap(x, "y"))
+        return received
+
     def xor_z(x, s):
         return lax.ppermute(x, "z", [(i, i ^ s) for i in range(n_z)])
 
@@ -723,7 +758,8 @@
         return own[0].astype(f32) + recv[0].astype(f32) + back.astype(f32)
 
     def scatter_rest(halves_of):
-        near = jnp.concatenate(halves_of, axis=1).astype(bf16)
+        joined = jnp.concatenate(halves_of, axis=1) if len(halves_of) > 1 else halves_of[0]
+        near = joined.astype(bf16)
         if not direct:
             return [lax.psum_scatter(near, dp, scatter_dimension=0, tiled=True)]
         return [near[:slab]] + [xor_z(near[s * slab : (s + 1) * slab], s) for s in range(1, n_z)]
@@ -756,55 +792,66 @@
         spread_bias = (terms[0] + terms[1] + terms[2]).reshape(GROUPS, heads, SLOT, SLOT)
         full = spread_bias[None] + jnp.asarray(mask)[:, None, None]
         pos.append(full.reshape(mask.shape[0], GROUPS, heads * SLOT, SLOT))
-    picks = [
-        selection(l % 2 == 1, images) for l in range(min(layer_total, 2))
-    ]
+    picks = []
+    for l in range(min(layer_total, 2)):
+        picks.append(selection(l % 2 == 1, images))
 
     saved = []
     source = (lax.dynamic_slice_in_dim(tokens, c_index * images, images, 0),)
     for l in range(layer_total):
-        hidden, a, q, k, v, prob, mixed, part = attn_fwd(
-            l, gains, offsets, source, weights_a[l], biases, pos[l], picks[l % 2]
+        cuts = images if l == layer_total - 1 else 1
+        hidden, a, q, k, v, prob, mixed, *own = attn_fwd(
+            l, gains, offsets, source, weights_a[l], biases, pos[l], picks[l % 2], cuts
         )
-        recv = swap(part, "y")
-        h1, c, z, slope, part_mlp = mlp_fwd(
-            l, hidden, part, recv, gains, offsets, weights_b[l], wide_biases
-        )
-        source = (h1, part_mlp, swap(part_mlp, "y"))
+        recv = swap_each(own)
+        res = []
+        for i in range(cuts):
+            res.append(
+                mlp_fwd(l, i, hidden, own[i], recv[i], gains, offsets, weights_b[l], wide_biases)
+            )
+        h1, c, z, slope, own = ([r[m] for r in res] for m in range(5))
+        recv = swap_each(own)
+        source = (h1[0], own[0], recv[0])
         saved.append((hidden, a, q, k, v, prob, mixed, h1, c, z, slope))
 
     cot_mine = lax.dynamic_slice_in_dim(cotangent, c_index * images, images, 0)
-    back = (place, counts, cot_mine) + source
+    back = [(place, counts, cot_mine) + terms for terms in zip(h1, own, recv)]
     sums_mlp, sums_attn, score_sums = [None] * layer_total, [None] * layer_total, [None] * layer_total
     grads = [None] * layer_total
     sums_tail = [None] * layer_total
     for l in reversed(range(layer_total)):
         hidden, a, q, k, v, prob, mixed, h1, c, z, slope = saved[l]
         last = l == layer_total - 1
-        res = mlp_bwd(l, last, back, gains, offsets, slope, weights_b[l])
-        grad, grad_b, du_b, part, sums_mlp[l] = res[:5]
+        res = []
+        for i, terms in enumerate(back):
+            res.append(mlp_bwd(l, last, i, terms, gains, offsets, slope[i], weights_b[l]))
+        grad, grad_b, du_b, own, sums = ([r[m] for r in res] for m in range(5))
+        sums_mlp[l] = sum(sums[1:], sums[0])
         if last:
-            out_mine = res[5]
+            out_mine = [r[5] for r in res]
         else:
             sums_tail[l + 1] = sums_mlp[l]
-        recv = swap(part, "y")
+        recv = swap_each(own)
         pair = mlp_grads(place, c, du_b, z, grad_b, halves, slab)
         half_b = scatter_half(pair[:-1], pair[-1])
         dh1, dh_b, d_proj, part_in, sums_attn[l], score_sums[l] = attn_bwd(
-            l, grad, part, recv, h1, gains, weights_a[l], q, k, v, prob, picks[l % 2]
+            l, grad, own, recv, h1, gains, weights_a[l], q, k, v, prob, picks[l % 2]
         )
-        back = (dh1, part_in, swap(part_in, "y"), hidden)
+        back = [(dh1, part_in, swap(part_in, "y"), hidden)]
         pair = attn_grads(place, a, d_proj, mixed, dh_b, halves, slab)
         half_a = scatter_half(pair[:-1], pair[-1])
-        grads[l] = scatter_rest([half_a, half_b])
-    grad_mine, sums_tail[0] = tail(*back, gains, cells)
+        if l:
+            grads[l] = [scatter_rest([half_a, half_b])]
+        else:
+            grads[l] = [scatter_rest([half_a]), scatter_rest([half_b])]
+    grad_mine, sums_tail[0] = tail(*back[0], gains, cells)
 
     def both_halves(x):
-        recv = swap(x, "c")
+        recv = [swap(part, "c") for part in x]
         return jnp.swapaxes(join(place, x, recv), 0, 1)
 
     output = both_halves(out_mine)
-    grad_tokens = both_halves(grad_mine)
+    grad_tokens = both_halves([grad_mine])
 
     tables = []
     for l in range(layer_total):

time: 311 us -> 322 us (1.035)
  starting transfers between devices: 58.1 us -> 76.3 us
  waiting for transfers between devices: 109 us -> 92 us
  Pallas kernels: 107 us -> 113 us
    ppermute x18 -> x21, starting transfers between devices: 23.6 us -> 38.8 us  [xor_z(): return lax.ppermute(x, 'z', [(i, i ^ s) for i in range(n_z)])]
    ppermute x30 -> x34, waiting for transfers between devices: 62.4 us -> 50.1 us  [swap(): return lax.ppermute(x, axis, [(0, 1), (1, 0)])]
    ppermute x18 -> x21, waiting for transfers between devices: 32.6 us -> 26.2 us  [xor_z(): return lax.ppermute(x, 'z', [(i, i ^ s) for i in range(n_z)])]
    pallas_call x26 -> x28, Pallas kernels: 107 us -> 113 us  [call(): pl.pallas_call(kernel, in_specs=specs, out_shape=[jax.ShapeDtypeStruct(sh...]
    ppermute x30 -> x34, starting transfers between devices: 21.2 us -> 24.8 us  [swap(): return lax.ppermute(x, axis, [(0, 1), (1, 0)])]
    unnamed x124 -> x148, local copies, waits for them, and re-layouts: 10.6 us -> 13.6 us
  transfers between devices with their start and end apart: 55 -> 62, of which waited for: 18 -> 16; matrix products, arithmetic and copies ran while one was open for 8% -> 8% of each run, Pallas kernels for 29% -> 33%
where the time goes in v2:
time: 322 us; the launch traced here: 321 us
  Pallas kernels  113 us (35%)
  waiting for transfers between devices  92 us (29%)
  starting transfers between devices  76.3 us (24%)
  local copies, waits for them, and re-layouts  19.7 us (6%)
  other arithmetic  14.2 us (4%)
    pallas_call x28, Pallas kernels, call(): pl.pallas_call(kernel, in_specs=specs, out_shape=[jax.ShapeDtypeStruct(sh...  113 us
    ppermute x34, waiting for transfers between devices, swap(): return lax.ppermute(x, axis, [(0, 1), (1, 0)])  50.1 us
    ppermute x21, starting transfers between devices, xor_z(): return lax.ppermute(x, 'z', [(i, i ^ s) for i in range(n_z)])  38.8 us
    ppermute x21, waiting for transfers between devices, xor_z(): return lax.ppermute(x, 'z', [(i, i ^ s) for i in range(n_z)])  26.2 us
    ppermute x34, starting transfers between devices, swap(): return lax.ppermute(x, axis, [(0, 1), (1, 0)])  24.8 us
    ppermute x7, waiting for transfers between devices, xor_dp(): return lax.ppermute(x, dp, [(i, i ^ s) for i in range(n_x * n_z)])  15.7 us
    unnamed x148, local copies, waits for them, and re-layouts  13.6 us
    ppermute x7, starting transfers between devices, xor_dp(): return lax.ppermute(x, dp, [(i, i ^ s) for i in range(n_x * n_z)])  12.6 us
  transfers between devices with their start and end apart: 62, of which 16 were waited for; matrix products, arithmetic and copies ran while one was open for 8% of the time, Pallas kernels for 33%

profile of v2, /device:TPU:0, one launch (start us, length us, event | category | flops | bytes accessed | tf_op | source)
XLA Modules:
  0.0 320.5 jit_solution(804629909124517049)
XLA Ops:
  29.3 14.9 %collective-permute-done.5.refs_6_ = bf16[64,512]{1,0:T(8,128)(2,1)S(1)} collective-permute-done((bf16[64,512]{1,0:T(8,128)(2,1)S(1)}, bf16[64,512]{1,0:T(8,128)(2,1)S(1)}, u32[]{:S(2)}, u32[]{:S(2)}) %collective-permute-start.5) | collective-permute-done | bytes 65568 | tf_op jit(solution)/shard_map/ppermute | solution.py:736
  55.1 9.6 %collective-permute-start.19 = (bf16[128,512]{1,0:T(8,128)(2,1)}, bf16[128,512]{1,0:T(8,128)(2,1)S(1)}, u32[]{:S(2)}, u32[]{:S(2)}) collective-permute-start(bf16[128,512]{1,0:T(8,128)(2,1)} %shard_map.632.refs_0_), channel_id=1, source_target_pairs={{0,8},{8,0},{16,24},{24,16},{1,9},{9,1},{17,25},{25,17},{2,10},{10... | collective-permute-start | bytes 393224 | tf_op jit(solution)/shard_map/ppermute | solution.py:733
  70.7 7.9 %shard_map.628 = (f32[400,512]{1,0:T(8,128)}, bf16[400,512]{1,0:T(8,128)(2,1)}, bf16[2,8,64,128]{3,2,1,0:T(8,128)(2,1)}, bf16[2,8,64,128]{3,2,1,0:T(8,128)(2,1)}...) custom-call(f32[2,196,512]{2,1,0:T(8,128)} %copy.82.refs_0_, ...), custom_call_target="tpu_custom_call" | custom-call | tf_op jit(solution)/shard_map/pallas_call | solution.py:122
  87.9 11.3 %collective-permute-done.26.refs_2_ = bf16[128,1024]{1,0:T(8,128)(2,1)S(1)} collective-permute-done((bf16[128,1024]{1,0:T(8,128)(2,1)S(1)}, bf16[128,1024]{1,0:T(8,128)(2,1)S(1)}, u32[]{:S(2)}, u32[]{:S(2)}) %collective-permute-start.26) | collective-permute-done | bytes 262176 | tf_op jit(solution)/shard_map/ppermute | solution.py:733
  104.0 5.0 %shard_map.631 = (f32[400,512]{1,0:T(8,128)}, bf16[400,512]{1,0:T(8,128)(2,1)}, bf16[400,1024]{1,0:T(8,128)(2,1)}, bf16[400,1024]{1,0:T(8,128)(2,1)}, bf16[400,512]{1,0:T(8,128)(2,1)}) custom-call(f32[400,512]{1,0:T(8,128)} %get-tuple-element.156.h_ref, bf16[400,512]{1,0:T(8,128)(2,1)} %get-tuple-element.157.own_ref, bf16[400,512]{1,0:T(8,128)(2,1)} %copy-done.14, ...), custom_call_target="tpu_custom_call" | custom-call | tf_op jit(solution)/shard_map/pallas_call | solution.py:122
  111.8 9.3 %collective-permute-done.17.refs_2_ = bf16[400,512]{1,0:T(8,128)(2,1)S(1)} collective-permute-done((bf16[400,512]{1,0:T(8,128)(2,1)}, bf16[400,512]{1,0:T(8,128)(2,1)S(1)}, u32[]{:S(2)}, u32[]{:S(2)}) %collective-permute-start.17) | collective-permute-done | bytes 409632 | tf_op jit(solution)/shard_map/ppermute | solution.py:724
  121.8 8.6 %shard_map.634 = (f32[400,512]{1,0:T(8,128)}, bf16[400,512]{1,0:T(8,128)(2,1)}, bf16[2,8,64,128]{3,2,1,0:T(8,128)(2,1)}, bf16[2,8,64,128]{3,2,1,0:T(8,128)(2,1)}...) custom-call(f32[400,512]{1,0:T(8,128)} %get-tuple-element.159.refs_0, ...), custom_call_target="tpu_custom_call" | custom-call | tf_op jit(solution)/shard_map/pallas_call | solution.py:122
  132.4 6.1 %collective-permute-done.23.recv_ref = bf16[200,512]{1,0:T(8,128)(2,1)S(1)} collective-permute-done((bf16[200,512]{1,0:T(8,128)(2,1)}, bf16[200,512]{1,0:T(8,128)(2,1)S(1)}, u32[]{:S(2)}, u32[]{:S(2)}) %collective-permute-start.23) | collective-permute-done | bytes 204832 | tf_op jit(solution)/shard_map/ppermute | solution.py:724
  139.2 3.9 %shard_map.637 = (f32[200,512]{1,0:T(8,128)}, bf16[200,512]{1,0:T(8,128)(2,1)}, bf16[200,1024]{1,0:T(8,128)(2,1)}, bf16[200,1024]{1,0:T(8,128)(2,1)}, bf16[200,512]{1,0:T(8,128)(2,1)}) custom-call(f32[400,512]{1,0:T(8,128)} %get-tuple-element.162.h_ref.refs_3_, bf16[200,512]{1,0:T(8,128)(2,1)} %get-tuple-element.163.own_ref, bf16[200,512]{1,0:T(8,128)(2,1)} %copy-done.31, ...), custom_call_target="tpu_custom_call" | custom-call | tf_op jit(solution)/shard_map/pallas_call | solution.py:122
  145.4 3.9 %shard_map.639 = (f32[200,512]{1,0:T(8,128)}, bf16[200,512]{1,0:T(8,128)(2,1)}, bf16[200,1024]{1,0:T(8,128)(2,1)}, bf16[200,1024]{1,0:T(8,128)(2,1)}, bf16[200,512]{1,0:T(8,128)(2,1)}) custom-call(f32[400,512]{1,0:T(8,128)} %get-tuple-element.162.h_ref.refs_3_, bf16[200,512]{1,0:T(8,128)(2,1)} %get-tuple-element.169.own_ref, bf16[200,512]{1,0:T(8,128)(2,1)} %copy-done.30, ...), custom_call_target="tpu_custom_call" | custom-call | tf_op jit(solution)/shard_map/pallas_call | solution.py:122
  163.6 4.0 %shard_map.650 = (bf16[256,1024]{1,0:T(8,128)(2,1)}, bf16[256,1024]{1,0:T(8,128)(2,1)}, bf16[2,256,1024]{2,1,0:T(8,128)(2,1)}) custom-call(s32[4]{0:T(128)} %pad_add_fusion.place_ref.refs_0_, bf16[200,512]{1,0:T(8,128)(2,1)} %get-tuple-element.215.refs_0_, bf16[200,512]{1,0:T(8,128)(2,1)} %get-tuple-element.216.refs_1_, ...), custom_call_target="tpu_custom_call" | custom-call | tf_op jit(solution)/shard_map/pallas_call | solution.py:122
  169.3 12.3 %shard_map.642 = (f32[400,512]{1,0:T(8,128)}, bf16[400,512]{1,0:T(8,128)(2,1)}, bf16[400,768]{1,0:T(8,128)(2,1)}, bf16[400,512]{1,0:T(8,128)(2,1)}, f32[8,512]{1,0:T(8,128)}, /*index=5*/f32[2,256,64]{2,1,0:T(8,128)}) custom-call(f32[200,512]{1,0:T(8,128)} %get-tuple-element.174.refs_0_, f32[200,512]{1,0:T(8,128)} %get-tuple-element.175.refs_1_, ...), custom_call_target="tpu_custom_call" | custom-call | tf_op jit(solution)/shard_map/pallas_call | solution.py:122
  188.0 5.4 %collective-permute-done.36.refs_2_ = bf16[400,512]{1,0:T(8,128)(2,1)S(1)} collective-permute-done((bf16[400,512]{1,0:T(8,128)(2,1)}, bf16[400,512]{1,0:T(8,128)(2,1)S(1)}, u32[]{:S(2)}, u32[]{:S(2)}) %collective-permute-start.36) | collective-permute-done | bytes 409632 | tf_op jit(solution)/shard_map/ppermute | solution.py:724
  194.1 5.0 %shard_map.643 = (f32[400,512]{1,0:T(8,128)}, bf16[400,512]{1,0:T(8,128)(2,1)}, bf16[400,1024]{1,0:T(8,128)(2,1)}, bf16[400,512]{1,0:T(8,128)(2,1)}, f32[8,512]{1,0:T(8,128)}) custom-call(f32[400,512]{1,0:T(8,128)} %get-tuple-element.182.refs_0_, bf16[400,512]{1,0:T(8,128)(2,1)} %get-tuple-element.183.refs_1_, bf16[400,512]{1,0:T(8,128)(2,1)} %copy-done.18, ...), custom_call_target="tpu_custom_call" | custom-call | tf_op jit(solution)/shard_map/pallas_call | solution.py:122
  201.2 4.0 %shard_map.648 = (bf16[256,1024]{1,0:T(8,128)(2,1)}, bf16[256,1024]{1,0:T(8,128)(2,1)}, bf16[2,256,1024]{2,1,0:T(8,128)(2,1)}) custom-call(s32[4]{0:T(128)} %pad_add_fusion.place_ref.refs_0_, bf16[400,512]{1,0:T(8,128)(2,1)} %get-tuple-element.201.refs_0_, bf16[400,1024]{1,0:T(8,128)(2,1)} %get-tuple-element.202.refs_1_, ...), custom_call_target="tpu_custom_call" | custom-call | tf_op jit(solution)/shard_map/pallas_call | solution.py:122
  206.0 4.0 %collective-permute-done.37.refs_2_ = bf16[400,512]{1,0:T(8,128)(2,1)S(1)} collective-permute-done((bf16[400,512]{1,0:T(8,128)(2,1)}, bf16[400,512]{1,0:T(8,128)(2,1)S(1)}, u32[]{:S(2)}, u32[]{:S(2)}) %collective-permute-start.37) | collective-permute-done | bytes 409632 | tf_op jit(solution)/shard_map/ppermute | solution.py:724
  210.8 12.3 %shard_map.644 = (f32[400,512]{1,0:T(8,128)}, bf16[400,512]{1,0:T(8,128)(2,1)}, bf16[400,768]{1,0:T(8,128)(2,1)}, bf16[400,512]{1,0:T(8,128)(2,1)}, f32[8,512]{1,0:T(8,128)}, /*index=5*/f32[2,256,64]{2,1,0:T(8,128)}) custom-call(f32[400,512]{1,0:T(8,128)} %get-tuple-element.185.refs_0_, bf16[400,512]{1,0:T(8,128)(2,1)} %get-tuple-element.186.refs_1_, ...), custom_call_target="tpu_custom_call" | custom-call | tf_op jit(solution)/shard_map/pallas_call | solution.py:122
  247.2 8.1 %collective-permute-done.58 = f32[24,512]{1,0:T(8,128)S(1)} collective-permute-done((f32[24,512]{1,0:T(8,128)S(1)}, f32[24,512]{1,0:T(8,128)S(1)}, u32[]{:S(2)}, u32[]{:S(2)}) %collective-permute-start.58) | collective-permute-done | bytes 49184 | tf_op jit(solution)/shard_map/ppermute | solution.py:724
  255.3 4.9 %collective-permute-start.60 = (f32[24,512]{1,0:T(8,128)S(1)}, f32[24,512]{1,0:T(8,128)S(1)}, u32[]{:S(2)}, u32[]{:S(2)}) collective-permute-start(f32[24,512]{1,0:T(8,128)S(1)} %add.188), channel_id=1, source_target_pairs={{0,16},{8,24},{16,0},{24,8},{1,17},{9,25},{17,1},{25,9},{2,18},{10... | collective-permute-start | bytes 147464 | tf_op jit(solution)/shard_map/ppermute | solution.py:733
  267.9 4.8 %collective-permute-done.41 = bf16[256,512]{1,0:T(8,128)(2,1)S(1)} collective-permute-done((bf16[256,512]{1,0:T(8,128)(2,1)S(1)}, bf16[256,512]{1,0:T(8,128)(2,1)S(1)}, u32[]{:S(2)}, u32[]{:S(2)}) %collective-permute-start.41) | collective-permute-done | bytes 262176 | tf_op jit(solution)/shard_map/ppermute | solution.py:724
  274.4 7.3 %collective-permute-done.46 = bf16[256,1024]{1,0:T(8,128)(2,1)S(1)} collective-permute-done((bf16[256,1024]{1,0:T(8,128)(2,1)S(1)}, bf16[256,1024]{1,0:T(8,128)(2,1)S(1)}, u32[]{:S(2)}, u32[]{:S(2)}) %collective-permute-start.46) | collective-permute-done | bytes 524320 | tf_op jit(solution)/shard_map/ppermute | solution.py:724
  287.2 4.0 %collective-permute-done.54.refs_9_ = bf16[64,1536]{1,0:T(8,128)(2,1)S(1)} collective-permute-done((bf16[64,1536]{1,0:T(8,128)(2,1)S(1)}, bf16[64,1536]{1,0:T(8,128)(2,1)S(1)}, u32[]{:S(2)}, u32[]{:S(2)}) %collective-permute-start.54) | collective-permute-done | bytes 196640 | tf_op jit(solution)/shard_map/ppermute | solution.py:733
  291.4 8.9 %collective-permute-done.55.refs_10_ = bf16[64,1536]{1,0:T(8,128)(2,1)S(1)} collective-permute-done((bf16[64,1536]{1,0:T(8,128)(2,1)S(1)}, bf16[64,1536]{1,0:T(8,128)(2,1)S(1)}, u32[]{:S(2)}, u32[]{:S(2)}) %collective-permute-start.55) | collective-permute-done | bytes 196640 | tf_op jit(solution)/shard_map/ppermute | solution.py:733
  316.0 4.3 %shard_map.651 = (f32[2,3,64,128]{3,2,1,0:T(8,128)}, f32[2,3,64,128]{3,2,1,0:T(8,128)}, f32[2,3,64,128]{3,2,1,0:T(8,128)}, f32[2,3,64,128]{3,2,1,0:T(8,128)}, f3...) custom-call(bf16[64,512]{1,0:T(8,128)(2,1)} %get-tuple-element.283.r, ...), custom_call_target="tpu_custom_call" | custom-call | tf_op jit(solution)/shard_map/pallas_call | solution.py:122
  (317 shorter events, 148.4 us)
Async XLA Ops:
  20.4 27.9 %collective-permute-start.12 = (bf16[128,1024]{1,0:T(8,128)(2,1)}, bf16[128,1024]{1,0:T(8,128)(2,1)S(1)}, u32[]{:S(2)}, u32[]{:S(2)}) collective-permute-start(bf16[128,1024]{1,0:T(8,128)(2,1)} %shard_map.629.refs_0_), channel_id=1, source_target_pairs={{0,8},{8,0},{16,24},{24,16},{1,9},{9,1},{17,25},{25,17},{2,10},{10... | collective-permute-start | bytes 786440 | tf_op jit(solution)/shard_map/ppermute | solution.py:733
  21.3 27.8 %collective-permute-start.13 = (bf16[128,1024]{1,0:T(8,128)(2,1)}, bf16[128,1024]{1,0:T(8,128)(2,1)S(1)}, u32[]{:S(2)}, u32[]{:S(2)}) collective-permute-start(bf16[128,1024]{1,0:T(8,128)(2,1)} %shard_map.629.refs_0_), channel_id=1, source_target_pairs={{0,16},{8,24},{16,0},{24,8},{1,17},{9,25},{17,1},{25,9},{2,18},{10... | collective-permute-start | bytes 786440 | tf_op jit(solution)/shard_map/ppermute | solution.py:733
  23.6 25.5 %collective-permute-start.14 = (bf16[128,1024]{1,0:T(8,128)(2,1)}, bf16[128,1024]{1,0:T(8,128)(2,1)S(1)}, u32[]{:S(2)}, u32[]{:S(2)}) collective-permute-start(bf16[128,1024]{1,0:T(8,128)(2,1)} %shard_map.629.refs_0_), channel_id=1, source_target_pairs={{0,24},{8,16},{16,8},{24,0},{1,25},{9,17},{17,9},{25,1},{2,26},{10... | collective-permute-start | bytes 786440 | tf_op jit(solution)/shard_map/ppermute | solution.py:733
  24.8 19.3 %collective-permute-start.5 = (bf16[64,512]{1,0:T(8,128)(2,1)S(1)}, bf16[64,512]{1,0:T(8,128)(2,1)S(1)}, u32[]{:S(2)}, u32[]{:S(2)}) collective-permute-start(bf16[64,512]{1,0:T(8,128)(2,1)S(1)} %copy-done.55), channel_id=1, source_target_pairs={{0,24},{4,28},{8,16},{12,20},{16,8},{20,12},{24,0},{28,4},{1,25},{... | collective-permute-start | bytes 196616 | tf_op jit(solution)/shard_map/ppermute | solution.py:736
  44.2 22.8 %collective-permute-start.8 = (f32[2,2,128]{2,1,0:T(2,128)S(1)}, f32[2,2,128]{2,1,0:T(2,128)S(1)}, u32[]{:S(2)}, u32[]{:S(2)}) collective-permute-start(f32[2,2,128]{2,1,0:T(2,128)S(1)} %copy-done.67), channel_id=1, source_target_pairs={{0,1},{1,0},{2,3},{3,2},{4,5},{5,4},{6,7},{7,6},{8,9},{9,8},{10,11... | collective-permute-start | bytes 6152 | tf_op jit(solution)/shard_map/ppermute | solution.py:724
  49.1 19.8 %collective-permute-start.7 = (bf16[512,512]{1,0:T(8,128)(2,1)}, bf16[512,512]{1,0:T(8,128)(2,1)S(1)}, u32[]{:S(2)}, u32[]{:S(2)}) collective-permute-start(bf16[512,512]{1,0:T(8,128)(2,1)} %shard_map.627.refs_3_.refs_5_), channel_id=1, source_target_pairs={{0,1},{1,0},{2,3},{3,2},{4,5},{5,4},{6,7},{7,6},{8,9},{9,8},{10,11... | collective-permute-start | bytes 1572872 | tf_op jit(solution)/shard_map/ppermute | solution.py:724
  52.7 50.2 %collective-permute-start.15 = (bf16[512,1024]{1,0:T(8,128)(2,1)}, bf16[512,1024]{1,0:T(8,128)(2,1)S(1)}, u32[]{:S(2)}, u32[]{:S(2)}) collective-permute-start(bf16[512,1024]{1,0:T(8,128)(2,1)} %shard_map.630.w0.refs_7_), channel_id=1, source_target_pairs={{0,1},{1,0},{2,3},{3,2},{4,5},{5,4},{6,7},{7,6},{8,9},{9,8},{10,11... | collective-permute-start | bytes 3145736 | tf_op jit(solution)/shard_map/ppermute | solution.py:724
  55.1 23.5 %collective-permute-start.19 = (bf16[128,512]{1,0:T(8,128)(2,1)}, bf16[128,512]{1,0:T(8,128)(2,1)S(1)}, u32[]{:S(2)}, u32[]{:S(2)}) collective-permute-start(bf16[128,512]{1,0:T(8,128)(2,1)} %shard_map.632.refs_0_), channel_id=1, source_target_pairs={{0,8},{8,0},{16,24},{24,16},{1,9},{9,1},{17,25},{25,17},{2,10},{10... | collective-permute-start | bytes 393224 | tf_op jit(solution)/shard_map/ppermute | solution.py:733
  78.6 20.6 %collective-permute-start.26 = (bf16[128,1024]{1,0:T(8,128)(2,1)S(1)}, bf16[128,1024]{1,0:T(8,128)(2,1)S(1)}, u32[]{:S(2)}, u32[]{:S(2)}) collective-permute-start(bf16[128,1024]{1,0:T(8,128)(2,1)S(1)} %copy-done.7), channel_id=1, source_target_pairs={{0,16},{8,24},{16,0},{24,8},{1,17},{9,25},{17,1},{25,9},{2,18},{10... | collective-permute-start | bytes 786440 | tf_op jit(solution)/shard_map/ppermute | solution.py:733
  80.2 19.0 %collective-permute-start.27 = (bf16[128,1024]{1,0:T(8,128)(2,1)S(1)}, bf16[128,1024]{1,0:T(8,128)(2,1)S(1)}, u32[]{:S(2)}, u32[]{:S(2)}) collective-permute-start(bf16[128,1024]{1,0:T(8,128)(2,1)S(1)} %copy-done.7), channel_id=1, source_target_pairs={{0,24},{8,16},{16,8},{24,0},{1,25},{9,17},{17,9},{25,1},{2,26},{10... | collective-permute-start | bytes 786440 | tf_op jit(solution)/shard_map/ppermute | solution.py:733
  82.0 20.8 %collective-permute-start.10 = (bf16[400,512]{1,0:T(8,128)(2,1)}, bf16[400,512]{1,0:T(8,128)(2,1)S(1)}, u32[]{:S(2)}, u32[]{:S(2)}) collective-permute-start(bf16[400,512]{1,0:T(8,128)(2,1)} %get-tuple-element.157.own_ref), channel_id=1, source_target_pairs={{0,2},{2,0},{1,3},{3,1},{4,6},{6,4},{5,7},{7,5},{8,10},{10,8},{9,1... | collective-permute-start | bytes 1228808 | tf_op jit(solution)/shard_map/ppermute | solution.py:724
  84.5 18.3 %collective-permute-start.16 = (f32[2,512]{1,0:T(2,128)S(1)}, f32[2,512]{1,0:T(2,128)S(1)}, u32[]{:S(2)}, u32[]{:S(2)}) collective-permute-start(f32[2,512]{1,0:T(2,128)S(1)} %copy-done.52), channel_id=1, source_target_pairs={{0,1},{1,0},{2,3},{3,2},{4,5},{5,4},{6,7},{7,6},{8,9},{9,8},{10,11... | collective-permute-start | bytes 12296 | tf_op jit(solution)/shard_map/ppermute | solution.py:724
  102.8 29.6 %collective-permute-start.28 = (bf16[512,1024]{1,0:T(8,128)(2,1)}, bf16[512,1024]{1,0:T(8,128)(2,1)S(1)}, u32[]{:S(2)}, u32[]{:S(2)}) collective-permute-start(bf16[512,1024]{1,0:T(8,128)(2,1)} %shard_map.636.w0.refs_9_), channel_id=1, source_target_pairs={{0,1},{1,0},{2,3},{3,2},{4,5},{5,4},{6,7},{7,6},{8,9},{9,8},{10,11... | collective-permute-start | bytes 3145736 | tf_op jit(solution)/shard_map/ppermute | solution.py:724
  163.1 76.4 %collective-permute-start.32 = (f32[1,196,512]{2,1,0:T(8,128)}, f32[1,196,512]{2,1,0:T(8,128)}, u32[]{:S(2)}, u32[]{:S(2)}) collective-permute-start(f32[1,196,512]{2,1,0:T(8,128)} %get-tuple-element.168.refs_0_), channel_id=1, source_target_pairs={{0,1},{1,0},{2,3},{3,2},{4,5},{5,4},{6,7},{7,6},{8,9},{9,8},{10,11... | collective-permute-start | bytes 1204232 | tf_op jit(solution)/shard_map/ppermute | solution.py:724
  163.1 77.2 %collective-permute-start.33 = (f32[1,196,512]{2,1,0:T(8,128)}, f32[1,196,512]{2,1,0:T(8,128)}, u32[]{:S(2)}, u32[]{:S(2)}) collective-permute-start(f32[1,196,512]{2,1,0:T(8,128)} %get-tuple-element.173.refs_1_), channel_id=1, source_target_pairs={{0,1},{1,0},{2,3},{3,2},{4,5},{5,4},{6,7},{7,6},{8,9},{9,8},{10,11... | collective-permute-start | bytes 1204232 | tf_op jit(solution)/shard_map/ppermute | solution.py:724
  167.6 71.9 %collective-permute-start.52 = (bf16[2,256,1024]{2,1,0:T(8,128)(2,1)}, bf16[2,256,1024]{2,1,0:T(8,128)(2,1)S(1)}, u32[]{:S(2)}, u32[]{:S(2)}) collective-permute-start(bf16[2,256,1024]{2,1,0:T(8,128)(2,1)} %get-tuple-element.224), channel_id=1, source_target_pairs={{0,1},{1,0},{2,3},{3,2},{4,5},{5,4},{6,7},{7,6},{8,9},{9,8},{10,11... | collective-permute-start | bytes 3145736 | tf_op jit(solution)/shard_map/ppermute | solution.py:724
  186.1 19.1 %collective-permute-start.50 = (bf16[2,256,512]{2,1,0:T(8,128)(2,1)}, bf16[2,256,512]{2,1,0:T(8,128)(2,1)S(1)}, u32[]{:S(2)}, u32[]{:S(2)}) collective-permute-start(bf16[2,256,512]{2,1,0:T(8,128)(2,1)} %get-tuple-element.213), channel_id=1, source_target_pairs={{0,1},{1,0},{2,3},{3,2},{4,5},{5,4},{6,7},{7,6},{8,9},{9,8},{10,11... | collective-permute-start | bytes 1572872 | tf_op jit(solution)/shard_map/ppermute | solution.py:724
  205.2 60.5 %collective-permute-start.45 = (bf16[2,256,1024]{2,1,0:T(8,128)(2,1)}, bf16[2,256,1024]{2,1,0:T(8,128)(2,1)S(1)}, u32[]{:S(2)}, u32[]{:S(2)}) collective-permute-start(bf16[2,256,1024]{2,1,0:T(8,128)(2,1)} %get-tuple-element.206), channel_id=1, source_target_pairs={{0,1},{1,0},{2,3},{3,2},{4,5},{5,4},{6,7},{7,6},{8,9},{9,8},{10,11... | collective-permute-start | bytes 3145736 | tf_op jit(solution)/shard_map/ppermute | solution.py:724
  239.5 20.7 %collective-permute-start.40 = (bf16[2,256,512]{2,1,0:T(8,128)(2,1)}, bf16[2,256,512]{2,1,0:T(8,128)(2,1)}, u32[]{:S(2)}, u32[]{:S(2)}) collective-permute-start(bf16[2,256,512]{2,1,0:T(8,128)(2,1)} %get-tuple-element.199), channel_id=1, source_target_pairs={{0,1},{1,0},{2,3},{3,2},{4,5},{5,4},{6,7},{7,6},{8,9},{9,8},{10,11... | collective-permute-start | bytes 1572872 | tf_op jit(solution)/shard_map/ppermute | solution.py:724
  240.3 23.2 %collective-permute-start.53 = (bf16[256,1024]{1,0:T(8,128)(2,1)S(1)}, bf16[256,1024]{1,0:T(8,128)(2,1)}, u32[]{:S(2)}, u32[]{:S(2)}) collective-permute-start(bf16[256,1024]{1,0:T(8,128)(2,1)S(1)} %fusion.8), channel_id=1, source_target_pairs={{0,4},{4,0},{1,5},{5,1},{2,6},{6,2},{3,7},{7,3},{8,12},{12,8},{9,1... | collective-permute-start | bytes 1572872 | tf_op jit(solution)/shard_map/ppermute | solution.py:724
  247.2 57.6 %collective-permute-start.39 = (f32[2,196,512]{2,0,1:T(2,128)S(1)}, f32[2,196,512]{2,0,1:T(2,128)S(1)}, u32[]{:S(2)}, u32[]{:S(2)}) collective-permute-start(f32[2,196,512]{2,0,1:T(2,128)S(1)} %copy.79), channel_id=1, source_target_pairs={{0,1},{1,0},{2,3},{3,2},{4,5},{5,4},{6,7},{7,6},{8,9},{9,8},{10,11... | collective-permute-start | bytes 2408456 | tf_op jit(solution)/shard_map/ppermute | solution.py:724
  255.3 26.7 %collective-permute-start.60 = (f32[24,512]{1,0:T(8,128)S(1)}, f32[24,512]{1,0:T(8,128)S(1)}, u32[]{:S(2)}, u32[]{:S(2)}) collective-permute-start(f32[24,512]{1,0:T(8,128)S(1)} %add.188), channel_id=1, source_target_pairs={{0,16},{8,24},{16,0},{24,8},{1,17},{9,25},{17,1},{25,9},{2,18},{10... | collective-permute-start | bytes 147464 | tf_op jit(solution)/shard_map/ppermute | solution.py:733
  260.3 24.1 %collective-permute-start.61 = (f32[24,512]{1,0:T(8,128)S(1)}, f32[24,512]{1,0:T(8,128)S(1)}, u32[]{:S(2)}, u32[]{:S(2)}) collective-permute-start(f32[24,512]{1,0:T(8,128)S(1)} %add.188), channel_id=1, source_target_pairs={{0,24},{8,16},{16,8},{24,0},{1,25},{9,17},{17,9},{25,1},{2,26},{10... | collective-permute-start | bytes 147464 | tf_op jit(solution)/shard_map/ppermute | solution.py:733
  291.2 22.1 %collective-permute-start.43 = (bf16[64,512]{1,0:T(8,128)(2,1)S(1)}, bf16[64,512]{1,0:T(8,128)(2,1)S(1)}, u32[]{:S(2)}, u32[]{:S(2)}) collective-permute-start(bf16[64,512]{1,0:T(8,128)(2,1)S(1)} %get-tuple-element.281), channel_id=1, source_target_pairs={{0,16},{8,24},{16,0},{24,8},{1,17},{9,25},{17,1},{25,9},{2,18},{10... | collective-permute-start | bytes 196616 | tf_op jit(solution)/shard_map/ppermute | solution.py:733
  (111 other events, 1131.7 us)

commit v3 on v2

--- a/solution.py
+++ b/solution.py
@@ -41,12 +41,26 @@
     return grid.reshape(side_panes, WIN, side_panes, WIN).transpose(0, 2, 1, 3).reshape(-1, CELLS)
 
 
-def selection(shifted, images):
-    source = np.full((images, PANES, SLOT), -1, np.int32)
-    for i in range(images):
-        source[i, :, :CELLS] = window_order(shifted) + i * ROWS
-    wanted = jnp.asarray(source.reshape(-1, 1))
-    return (wanted == jnp.arange(images * ROWS, dtype=jnp.int32)[None, :]).astype(bf16)
+def selection(shifted):
+    source = np.full((PANES, SLOT), -1, np.int32)
+    source[:, :CELLS] = window_order(shifted)
+    wanted = jnp.asarray(source.reshape(1, -1))
+    return (wanted == jnp.arange(ROWS, dtype=jnp.int32)[:, None]).astype(bf16)
+
+
+def to_panes(pick, rows):
+    images = rows.shape[0] // ROWS
+    parts = [dot(pick, rows[i * ROWS : (i + 1) * ROWS].astype(bf16), 0, 0) for i in range(images)]
+    return jnp.concatenate(parts, axis=0).astype(bf16)
+
+
+def from_panes(pick, panes_ref):
+    panes, _, cols = panes_ref.shape
+    parts = [
+        dot(pick, panes_ref[i : i + PANES].reshape(PANES * SLOT, cols), 1, 0)
+        for i in range(0, panes, PANES)
+    ]
+    return jnp.concatenate(parts, axis=0).astype(bf16)
 
 
 def lookup_onehot():
@@ -143,10 +157,10 @@
 
 def attn_fwd(layer, gains, offsets, source, weights, biases, pos, pick, cuts):
     first = layer == 0
-    win_rows, rows = pick.shape
+    images = source[0].shape[0] if first else source[0].shape[0] // ROWS
+    rows, panes = images * ROWS, images * PANES
     *weights, at = weights
     width = weights[0].shape[0]
-    panes = win_rows // SLOT
     local = biases[0].shape[2]
     heads = local // HEAD_DIM
     masks_n = pos.shape[0]
@@ -167,9 +181,9 @@
             )
             h_ref[...] = hidden
         normed, _ = unit_norm(hidden)
-        a = (normed * gain_ref[layer, 0:1] + off_ref[layer, 0:1]).astype(bf16)
-        a_ref[...] = a
-        a_win = dot(pick_ref[...], a, 1, 0).astype(bf16)
+        a = normed * gain_ref[layer, 0:1] + off_ref[layer, 0:1]
+        a_ref[...] = a.astype(bf16)
+        a_win = to_panes(pick_ref[...], a)
         for g, (w, bias_ref) in enumerate(((w0, b0), (w1, b1))):
             proj = dot(a_win, w[:, at : at + 3 * local], 1, 0)
             q = ((proj[:, :local] + bias_ref[layer, 0:1]) * factor).astype(bf16)
@@ -193,7 +207,7 @@
             return carry
 
         lax.fori_loop(0, panes, step, 0, unroll=UNROLL)
-        mixed = dot(pick_ref[...], mw_ref[...].reshape(win_rows, GROUPS * local), 0, 0).astype(bf16)
+        mixed = from_panes(pick_ref[...], mw_ref)
         mixed_ref[...] = mixed
         part = None
         for g, w in enumerate((w0, w1)):
@@ -374,10 +388,10 @@
 
 
 def attn_bwd(layer, grad, own, recv, h1, gains, weights, q, k, v, prob, pick):
-    win_rows, rows = pick.shape
     width = grad[0].shape[1]
     cuts = len(grad)
-    panes = win_rows // SLOT
+    rows = cuts * grad[0].shape[0]
+    panes = rows // ROWS * PANES
     *weights, at = weights
     local = q.shape[3]
     heads = local // HEAD_DIM
@@ -407,9 +421,8 @@
         dh_b = dh1.astype(bf16)
         dhb_ref[...] = dh_b
         for g, w in enumerate((w0, w1)):
-            d_mixed = dot(dh_b, w[:, at + 3 * local : at + 4 * local], 1, 0).astype(bf16)
-            d_win = dot(pick_ref[...], d_mixed, 1, 0).astype(bf16)
-            dm_ref[g] = d_win.reshape(panes, SLOT, local)
+            d_mixed = dot(dh_b, w[:, at + 3 * local : at + 4 * local], 1, 0)
+            dm_ref[g] = to_panes(pick_ref[...], d_mixed).reshape(panes, SLOT, local)
         ds_ref[...] = jnp.zeros_like(ds_ref)
         bias_ref[...] = jnp.zeros_like(bias_ref)
         masks = head_masks(local)
@@ -438,9 +451,7 @@
         lax.fori_loop(0, panes, step, 0)
         sum_ref[3:4, : GROUPS * local] = bias_ref[0:1, :]
         sum_ref[4:5, : GROUPS * local] = bias_ref[1:2, :]
-        d_proj = dot(
-            pick_ref[...], dw_ref[...].reshape(win_rows, GROUPS * 3 * local), 0, 0
-        ).astype(bf16)
+        d_proj = from_panes(pick_ref[...], dw_ref)
         dp_ref[...] = d_proj
         part = None
         for g, w in enumerate((w0, w1)):
@@ -794,7 +805,7 @@
         pos.append(full.reshape(mask.shape[0], GROUPS, heads * SLOT, SLOT))
     picks = []
     for l in range(min(layer_total, 2)):
-        picks.append(selection(l % 2 == 1, images))
+        picks.append(selection(l % 2 == 1))
 
     saved = []
     source = (lax.dynamic_slice_in_dim(tokens, c_index * images, images, 0),)

time: 322 us -> 321 us (level)
  no operation moved by 1% of the time
where the time goes in v3:
time: 321 us; the launch traced here: 320 us
  Pallas kernels  112 us (35%)
  waiting for transfers between devices  92.4 us (29%)
  starting transfers between devices  76.4 us (24%)
  local copies, waits for them, and re-layouts  19.8 us (6%)
  other arithmetic  13.7 us (4%)
    pallas_call x28, Pallas kernels, call(): pl.pallas_call(kernel, in_specs=specs, out_shape=[jax.ShapeDtypeStruct(sh...  112 us
    ppermute x34, waiting for transfers between devices, swap(): return lax.ppermute(x, axis, [(0, 1), (1, 0)])  50.3 us
    ppermute x21, starting transfers between devices, xor_z(): return lax.ppermute(x, 'z', [(i, i ^ s) for i in range(n_z)])  38.9 us
    ppermute x21, waiting for transfers between devices, xor_z(): return lax.ppermute(x, 'z', [(i, i ^ s) for i in range(n_z)])  26.4 us
    ppermute x34, starting transfers between devices, swap(): return lax.ppermute(x, axis, [(0, 1), (1, 0)])  24.8 us
    ppermute x7, waiting for transfers between devices, xor_dp(): return lax.ppermute(x, dp, [(i, i ^ s) for i in range(n_x * n_z)])  15.7 us
    unnamed x148, local copies, waits for them, and re-layouts  13.7 us
    ppermute x7, starting transfers between devices, xor_dp(): return lax.ppermute(x, dp, [(i, i ^ s) for i in range(n_x * n_z)])  12.7 us
  transfers between devices with their start and end apart: 62, of which 16 were waited for; matrix products, arithmetic and copies ran while one was open for 8% of the time, Pallas kernels for 33%

profile of v3, /device:TPU:0, one launch (start us, length us, event | category | flops | bytes accessed | tf_op | source)
XLA Modules:
  0.0 319.7 jit_solution(8499451814537552158)
XLA Ops:
  29.3 14.9 %collective-permute-done.5.refs_6_ = bf16[64,512]{1,0:T(8,128)(2,1)S(1)} collective-permute-done((bf16[64,512]{1,0:T(8,128)(2,1)S(1)}, bf16[64,512]{1,0:T(8,128)(2,1)S(1)}, u32[]{:S(2)}, u32[]{:S(2)}) %collective-permute-start.5) | collective-permute-done | bytes 65568 | tf_op jit(solution)/shard_map/ppermute | solution.py:747
  55.2 9.6 %collective-permute-start.19 = (bf16[128,512]{1,0:T(8,128)(2,1)}, bf16[128,512]{1,0:T(8,128)(2,1)S(1)}, u32[]{:S(2)}, u32[]{:S(2)}) collective-permute-start(bf16[128,512]{1,0:T(8,128)(2,1)} %shard_map.632.refs_0_), channel_id=1, source_target_pairs={{0,8},{8,0},{16,24},{24,16},{1,9},{9,1},{17,25},{25,17},{2,10},{10... | collective-permute-start | bytes 393224 | tf_op jit(solution)/shard_map/ppermute | solution.py:744
  70.8 7.7 %shard_map.628 = (f32[400,512]{1,0:T(8,128)}, bf16[400,512]{1,0:T(8,128)(2,1)}, bf16[2,8,64,128]{3,2,1,0:T(8,128)(2,1)}, bf16[2,8,64,128]{3,2,1,0:T(8,128)(2,1)}...) custom-call(f32[2,196,512]{2,1,0:T(8,128)} %copy.82.refs_0_, ...), custom_call_target="tpu_custom_call" | custom-call | tf_op jit(solution)/shard_map/pallas_call | solution.py:136
  87.5 11.6 %collective-permute-done.26.refs_2_ = bf16[128,1024]{1,0:T(8,128)(2,1)S(1)} collective-permute-done((bf16[128,1024]{1,0:T(8,128)(2,1)S(1)}, bf16[128,1024]{1,0:T(8,128)(2,1)S(1)}, u32[]{:S(2)}, u32[]{:S(2)}) %collective-permute-start.26) | collective-permute-done | bytes 262176 | tf_op jit(solution)/shard_map/ppermute | solution.py:744
  103.9 5.0 %shard_map.631 = (f32[400,512]{1,0:T(8,128)}, bf16[400,512]{1,0:T(8,128)(2,1)}, bf16[400,1024]{1,0:T(8,128)(2,1)}, bf16[400,1024]{1,0:T(8,128)(2,1)}, bf16[400,512]{1,0:T(8,128)(2,1)}) custom-call(f32[400,512]{1,0:T(8,128)} %get-tuple-element.156.h_ref, bf16[400,512]{1,0:T(8,128)(2,1)} %get-tuple-element.157.own_ref, bf16[400,512]{1,0:T(8,128)(2,1)} %copy-done.14, ...), custom_call_target="tpu_custom_call" | custom-call | tf_op jit(solution)/shard_map/pallas_call | solution.py:136
  111.7 9.2 %collective-permute-done.17.refs_2_ = bf16[400,512]{1,0:T(8,128)(2,1)S(1)} collective-permute-done((bf16[400,512]{1,0:T(8,128)(2,1)}, bf16[400,512]{1,0:T(8,128)(2,1)S(1)}, u32[]{:S(2)}, u32[]{:S(2)}) %collective-permute-start.17) | collective-permute-done | bytes 409632 | tf_op jit(solution)/shard_map/ppermute | solution.py:735
  121.7 8.3 %shard_map.634 = (f32[400,512]{1,0:T(8,128)}, bf16[400,512]{1,0:T(8,128)(2,1)}, bf16[2,8,64,128]{3,2,1,0:T(8,128)(2,1)}, bf16[2,8,64,128]{3,2,1,0:T(8,128)(2,1)}...) custom-call(f32[400,512]{1,0:T(8,128)} %get-tuple-element.159.refs_0, ...), custom_call_target="tpu_custom_call" | custom-call | tf_op jit(solution)/shard_map/pallas_call | solution.py:136
  132.1 6.1 %collective-permute-done.23.recv_ref = bf16[200,512]{1,0:T(8,128)(2,1)S(1)} collective-permute-done((bf16[200,512]{1,0:T(8,128)(2,1)}, bf16[200,512]{1,0:T(8,128)(2,1)S(1)}, u32[]{:S(2)}, u32[]{:S(2)}) %collective-permute-start.23) | collective-permute-done | bytes 204832 | tf_op jit(solution)/shard_map/ppermute | solution.py:735
  138.9 3.9 %shard_map.637 = (f32[200,512]{1,0:T(8,128)}, bf16[200,512]{1,0:T(8,128)(2,1)}, bf16[200,1024]{1,0:T(8,128)(2,1)}, bf16[200,1024]{1,0:T(8,128)(2,1)}, bf16[200,512]{1,0:T(8,128)(2,1)}) custom-call(f32[400,512]{1,0:T(8,128)} %get-tuple-element.162.h_ref.refs_3_, bf16[200,512]{1,0:T(8,128)(2,1)} %get-tuple-element.163.own_ref, bf16[200,512]{1,0:T(8,128)(2,1)} %copy-done.31, ...), custom_call_target="tpu_custom_call" | custom-call | tf_op jit(solution)/shard_map/pallas_call | solution.py:136
  158.3 3.9 %shard_map.640 = (f32[200,512]{1,0:T(8,128)}, bf16[200,512]{1,0:T(8,128)(2,1)}, bf16[200,1024]{1,0:T(8,128)(2,1)}, bf16[200,512]{1,0:T(8,128)(2,1)}, f32[8,512]{1,0:T(8,128)}, /*index=5*/f32[1,196,512]{2,1,0:T(8,128)}) custom-call(s32[4]{0:T(128)} %pad_add_fusion.place_ref.refs_0_, s32[1]{0:T(128)S(6)} %copy.83.refs_1_, f32[2,196,512]{2,1,0:T(8,128)} %copy.81.refs_2_, ...), custom_call_target="tpu_custom_call" | custom-call | tf_op jit(solution)/shard_map/pallas_call | solution.py:136
  163.3 4.1 %shard_map.650 = (bf16[256,1024]{1,0:T(8,128)(2,1)}, bf16[256,1024]{1,0:T(8,128)(2,1)}, bf16[2,256,1024]{2,1,0:T(8,128)(2,1)}) custom-call(s32[4]{0:T(128)} %pad_add_fusion.place_ref.refs_0_, bf16[200,512]{1,0:T(8,128)(2,1)} %get-tuple-element.215.refs_0_, bf16[200,512]{1,0:T(8,128)(2,1)} %get-tuple-element.216.refs_1_, ...), custom_call_target="tpu_custom_call" | custom-call | tf_op jit(solution)/shard_map/pallas_call | solution.py:136
  168.9 12.0 %shard_map.642 = (f32[400,512]{1,0:T(8,128)}, bf16[400,512]{1,0:T(8,128)(2,1)}, bf16[400,768]{1,0:T(8,128)(2,1)}, bf16[400,512]{1,0:T(8,128)(2,1)}, f32[8,512]{1,0:T(8,128)}, /*index=5*/f32[2,256,64]{2,1,0:T(8,128)}) custom-call(f32[200,512]{1,0:T(8,128)} %get-tuple-element.174.refs_0_, f32[200,512]{1,0:T(8,128)} %get-tuple-element.175.refs_1_, ...), custom_call_target="tpu_custom_call" | custom-call | tf_op jit(solution)/shard_map/pallas_call | solution.py:136
  187.4 5.4 %collective-permute-done.36.refs_2_ = bf16[400,512]{1,0:T(8,128)(2,1)S(1)} collective-permute-done((bf16[400,512]{1,0:T(8,128)(2,1)}, bf16[400,512]{1,0:T(8,128)(2,1)S(1)}, u32[]{:S(2)}, u32[]{:S(2)}) %collective-permute-start.36) | collective-permute-done | bytes 409632 | tf_op jit(solution)/shard_map/ppermute | solution.py:735
  193.6 5.0 %shard_map.643 = (f32[400,512]{1,0:T(8,128)}, bf16[400,512]{1,0:T(8,128)(2,1)}, bf16[400,1024]{1,0:T(8,128)(2,1)}, bf16[400,512]{1,0:T(8,128)(2,1)}, f32[8,512]{1,0:T(8,128)}) custom-call(f32[400,512]{1,0:T(8,128)} %get-tuple-element.182.refs_0_, bf16[400,512]{1,0:T(8,128)(2,1)} %get-tuple-element.183.refs_1_, bf16[400,512]{1,0:T(8,128)(2,1)} %copy-done.17, ...), custom_call_target="tpu_custom_call" | custom-call | tf_op jit(solution)/shard_map/pallas_call | solution.py:136
  200.7 4.0 %shard_map.648 = (bf16[256,1024]{1,0:T(8,128)(2,1)}, bf16[256,1024]{1,0:T(8,128)(2,1)}, bf16[2,256,1024]{2,1,0:T(8,128)(2,1)}) custom-call(s32[4]{0:T(128)} %pad_add_fusion.place_ref.refs_0_, bf16[400,512]{1,0:T(8,128)(2,1)} %get-tuple-element.201.refs_0_, bf16[400,1024]{1,0:T(8,128)(2,1)} %get-tuple-element.202.refs_1_, ...), custom_call_target="tpu_custom_call" | custom-call | tf_op jit(solution)/shard_map/pallas_call | solution.py:136
  205.5 4.1 %collective-permute-done.37.refs_2_ = bf16[400,512]{1,0:T(8,128)(2,1)S(1)} collective-permute-done((bf16[400,512]{1,0:T(8,128)(2,1)}, bf16[400,512]{1,0:T(8,128)(2,1)S(1)}, u32[]{:S(2)}, u32[]{:S(2)}) %collective-permute-start.37) | collective-permute-done | bytes 409632 | tf_op jit(solution)/shard_map/ppermute | solution.py:735
  210.4 12.0 %shard_map.644 = (f32[400,512]{1,0:T(8,128)}, bf16[400,512]{1,0:T(8,128)(2,1)}, bf16[400,768]{1,0:T(8,128)(2,1)}, bf16[400,512]{1,0:T(8,128)(2,1)}, f32[8,512]{1,0:T(8,128)}, /*index=5*/f32[2,256,64]{2,1,0:T(8,128)}) custom-call(f32[400,512]{1,0:T(8,128)} %get-tuple-element.185.refs_0_, bf16[400,512]{1,0:T(8,128)(2,1)} %get-tuple-element.186.refs_1_, ...), custom_call_target="tpu_custom_call" | custom-call | tf_op jit(solution)/shard_map/pallas_call | solution.py:136
  246.4 8.1 %collective-permute-done.58 = f32[24,512]{1,0:T(8,128)S(1)} collective-permute-done((f32[24,512]{1,0:T(8,128)S(1)}, f32[24,512]{1,0:T(8,128)S(1)}, u32[]{:S(2)}, u32[]{:S(2)}) %collective-permute-start.58) | collective-permute-done | bytes 49184 | tf_op jit(solution)/shard_map/ppermute | solution.py:735
  254.5 5.0 %collective-permute-start.60 = (f32[24,512]{1,0:T(8,128)S(1)}, f32[24,512]{1,0:T(8,128)S(1)}, u32[]{:S(2)}, u32[]{:S(2)}) collective-permute-start(f32[24,512]{1,0:T(8,128)S(1)} %add.188), channel_id=1, source_target_pairs={{0,16},{8,24},{16,0},{24,8},{1,17},{9,25},{17,1},{25,9},{2,18},{10... | collective-permute-start | bytes 147464 | tf_op jit(solution)/shard_map/ppermute | solution.py:744
  267.1 4.8 %collective-permute-done.41 = bf16[256,512]{1,0:T(8,128)(2,1)S(1)} collective-permute-done((bf16[256,512]{1,0:T(8,128)(2,1)S(1)}, bf16[256,512]{1,0:T(8,128)(2,1)S(1)}, u32[]{:S(2)}, u32[]{:S(2)}) %collective-permute-start.41) | collective-permute-done | bytes 262176 | tf_op jit(solution)/shard_map/ppermute | solution.py:735
  273.6 7.3 %collective-permute-done.46 = bf16[256,1024]{1,0:T(8,128)(2,1)S(1)} collective-permute-done((bf16[256,1024]{1,0:T(8,128)(2,1)S(1)}, bf16[256,1024]{1,0:T(8,128)(2,1)S(1)}, u32[]{:S(2)}, u32[]{:S(2)}) %collective-permute-start.46) | collective-permute-done | bytes 524320 | tf_op jit(solution)/shard_map/ppermute | solution.py:735
  286.4 4.1 %collective-permute-done.54.refs_9_ = bf16[64,1536]{1,0:T(8,128)(2,1)S(1)} collective-permute-done((bf16[64,1536]{1,0:T(8,128)(2,1)S(1)}, bf16[64,1536]{1,0:T(8,128)(2,1)S(1)}, u32[]{:S(2)}, u32[]{:S(2)}) %collective-permute-start.54) | collective-permute-done | bytes 196640 | tf_op jit(solution)/shard_map/ppermute | solution.py:744
  290.7 8.7 %collective-permute-done.55.refs_10_ = bf16[64,1536]{1,0:T(8,128)(2,1)S(1)} collective-permute-done((bf16[64,1536]{1,0:T(8,128)(2,1)S(1)}, bf16[64,1536]{1,0:T(8,128)(2,1)S(1)}, u32[]{:S(2)}, u32[]{:S(2)}) %collective-permute-start.55) | collective-permute-done | bytes 196640 | tf_op jit(solution)/shard_map/ppermute | solution.py:744
  315.2 4.3 %shard_map.651 = (f32[2,3,64,128]{3,2,1,0:T(8,128)}, f32[2,3,64,128]{3,2,1,0:T(8,128)}, f32[2,3,64,128]{3,2,1,0:T(8,128)}, f32[2,3,64,128]{3,2,1,0:T(8,128)}, f3...) custom-call(bf16[64,512]{1,0:T(8,128)(2,1)} %get-tuple-element.283.r, ...), custom_call_target="tpu_custom_call" | custom-call | tf_op jit(solution)/shard_map/pallas_call | solution.py:136
  (317 shorter events, 148.3 us)
Async XLA Ops:
  20.5 27.9 %collective-permute-start.12 = (bf16[128,1024]{1,0:T(8,128)(2,1)}, bf16[128,1024]{1,0:T(8,128)(2,1)S(1)}, u32[]{:S(2)}, u32[]{:S(2)}) collective-permute-start(bf16[128,1024]{1,0:T(8,128)(2,1)} %shard_map.629.refs_0_), channel_id=1, source_target_pairs={{0,8},{8,0},{16,24},{24,16},{1,9},{9,1},{17,25},{25,17},{2,10},{10... | collective-permute-start | bytes 786440 | tf_op jit(solution)/shard_map/ppermute | solution.py:744
  21.4 27.8 %collective-permute-start.13 = (bf16[128,1024]{1,0:T(8,128)(2,1)}, bf16[128,1024]{1,0:T(8,128)(2,1)S(1)}, u32[]{:S(2)}, u32[]{:S(2)}) collective-permute-start(bf16[128,1024]{1,0:T(8,128)(2,1)} %shard_map.629.refs_0_), channel_id=1, source_target_pairs={{0,16},{8,24},{16,0},{24,8},{1,17},{9,25},{17,1},{25,9},{2,18},{10... | collective-permute-start | bytes 786440 | tf_op jit(solution)/shard_map/ppermute | solution.py:744
  23.6 25.5 %collective-permute-start.14 = (bf16[128,1024]{1,0:T(8,128)(2,1)}, bf16[128,1024]{1,0:T(8,128)(2,1)S(1)}, u32[]{:S(2)}, u32[]{:S(2)}) collective-permute-start(bf16[128,1024]{1,0:T(8,128)(2,1)} %shard_map.629.refs_0_), channel_id=1, source_target_pairs={{0,24},{8,16},{16,8},{24,0},{1,25},{9,17},{17,9},{25,1},{2,26},{10... | collective-permute-start | bytes 786440 | tf_op jit(solution)/shard_map/ppermute | solution.py:744
  24.9 19.3 %collective-permute-start.5 = (bf16[64,512]{1,0:T(8,128)(2,1)S(1)}, bf16[64,512]{1,0:T(8,128)(2,1)S(1)}, u32[]{:S(2)}, u32[]{:S(2)}) collective-permute-start(bf16[64,512]{1,0:T(8,128)(2,1)S(1)} %copy-done.55), channel_id=1, source_target_pairs={{0,24},{4,28},{8,16},{12,20},{16,8},{20,12},{24,0},{28,4},{1,25},{... | collective-permute-start | bytes 196616 | tf_op jit(solution)/shard_map/ppermute | solution.py:747
  44.3 22.9 %collective-permute-start.8 = (f32[2,2,128]{2,1,0:T(2,128)S(1)}, f32[2,2,128]{2,1,0:T(2,128)S(1)}, u32[]{:S(2)}, u32[]{:S(2)}) collective-permute-start(f32[2,2,128]{2,1,0:T(2,128)S(1)} %copy-done.67), channel_id=1, source_target_pairs={{0,1},{1,0},{2,3},{3,2},{4,5},{5,4},{6,7},{7,6},{8,9},{9,8},{10,11... | collective-permute-start | bytes 6152 | tf_op jit(solution)/shard_map/ppermute | solution.py:735
  49.2 19.8 %collective-permute-start.7 = (bf16[512,512]{1,0:T(8,128)(2,1)}, bf16[512,512]{1,0:T(8,128)(2,1)S(1)}, u32[]{:S(2)}, u32[]{:S(2)}) collective-permute-start(bf16[512,512]{1,0:T(8,128)(2,1)} %shard_map.627.refs_3_.refs_5_), channel_id=1, source_target_pairs={{0,1},{1,0},{2,3},{3,2},{4,5},{5,4},{6,7},{7,6},{8,9},{9,8},{10,11... | collective-permute-start | bytes 1572872 | tf_op jit(solution)/shard_map/ppermute | solution.py:735
  52.8 50.0 %collective-permute-start.15 = (bf16[512,1024]{1,0:T(8,128)(2,1)}, bf16[512,1024]{1,0:T(8,128)(2,1)S(1)}, u32[]{:S(2)}, u32[]{:S(2)}) collective-permute-start(bf16[512,1024]{1,0:T(8,128)(2,1)} %shard_map.630.w0.refs_7_), channel_id=1, source_target_pairs={{0,1},{1,0},{2,3},{3,2},{4,5},{5,4},{6,7},{7,6},{8,9},{9,8},{10,11... | collective-permute-start | bytes 3145736 | tf_op jit(solution)/shard_map/ppermute | solution.py:735
  55.2 23.3 %collective-permute-start.19 = (bf16[128,512]{1,0:T(8,128)(2,1)}, bf16[128,512]{1,0:T(8,128)(2,1)S(1)}, u32[]{:S(2)}, u32[]{:S(2)}) collective-permute-start(bf16[128,512]{1,0:T(8,128)(2,1)} %shard_map.632.refs_0_), channel_id=1, source_target_pairs={{0,8},{8,0},{16,24},{24,16},{1,9},{9,1},{17,25},{25,17},{2,10},{10... | collective-permute-start | bytes 393224 | tf_op jit(solution)/shard_map/ppermute | solution.py:744
  78.5 20.6 %collective-permute-start.26 = (bf16[128,1024]{1,0:T(8,128)(2,1)S(1)}, bf16[128,1024]{1,0:T(8,128)(2,1)S(1)}, u32[]{:S(2)}, u32[]{:S(2)}) collective-permute-start(bf16[128,1024]{1,0:T(8,128)(2,1)S(1)} %copy-done.7), channel_id=1, source_target_pairs={{0,16},{8,24},{16,0},{24,8},{1,17},{9,25},{17,1},{25,9},{2,18},{10... | collective-permute-start | bytes 786440 | tf_op jit(solution)/shard_map/ppermute | solution.py:744
  80.1 19.0 %collective-permute-start.27 = (bf16[128,1024]{1,0:T(8,128)(2,1)S(1)}, bf16[128,1024]{1,0:T(8,128)(2,1)S(1)}, u32[]{:S(2)}, u32[]{:S(2)}) collective-permute-start(bf16[128,1024]{1,0:T(8,128)(2,1)S(1)} %copy-done.7), channel_id=1, source_target_pairs={{0,24},{8,16},{16,8},{24,0},{1,25},{9,17},{17,9},{25,1},{2,26},{10... | collective-permute-start | bytes 786440 | tf_op jit(solution)/shard_map/ppermute | solution.py:744
  81.9 20.8 %collective-permute-start.10 = (bf16[400,512]{1,0:T(8,128)(2,1)}, bf16[400,512]{1,0:T(8,128)(2,1)S(1)}, u32[]{:S(2)}, u32[]{:S(2)}) collective-permute-start(bf16[400,512]{1,0:T(8,128)(2,1)} %get-tuple-element.157.own_ref), channel_id=1, source_target_pairs={{0,2},{2,0},{1,3},{3,1},{4,6},{6,4},{5,7},{7,5},{8,10},{10,8},{9,1... | collective-permute-start | bytes 1228808 | tf_op jit(solution)/shard_map/ppermute | solution.py:735
  84.1 18.6 %collective-permute-start.16 = (f32[2,512]{1,0:T(2,128)S(1)}, f32[2,512]{1,0:T(2,128)S(1)}, u32[]{:S(2)}, u32[]{:S(2)}) collective-permute-start(f32[2,512]{1,0:T(2,128)S(1)} %copy-done.52), channel_id=1, source_target_pairs={{0,1},{1,0},{2,3},{3,2},{4,5},{5,4},{6,7},{7,6},{8,9},{9,8},{10,11... | collective-permute-start | bytes 12296 | tf_op jit(solution)/shard_map/ppermute | solution.py:735
  102.7 29.4 %collective-permute-start.28 = (bf16[512,1024]{1,0:T(8,128)(2,1)}, bf16[512,1024]{1,0:T(8,128)(2,1)S(1)}, u32[]{:S(2)}, u32[]{:S(2)}) collective-permute-start(bf16[512,1024]{1,0:T(8,128)(2,1)} %shard_map.636.w0.refs_9_), channel_id=1, source_target_pairs={{0,1},{1,0},{2,3},{3,2},{4,5},{5,4},{6,7},{7,6},{8,9},{9,8},{10,11... | collective-permute-start | bytes 3145736 | tf_op jit(solution)/shard_map/ppermute | solution.py:735
  162.8 75.9 %collective-permute-start.32 = (f32[1,196,512]{2,1,0:T(8,128)}, f32[1,196,512]{2,1,0:T(8,128)}, u32[]{:S(2)}, u32[]{:S(2)}) collective-permute-start(f32[1,196,512]{2,1,0:T(8,128)} %get-tuple-element.168.refs_0_), channel_id=1, source_target_pairs={{0,1},{1,0},{2,3},{3,2},{4,5},{5,4},{6,7},{7,6},{8,9},{9,8},{10,11... | collective-permute-start | bytes 1204232 | tf_op jit(solution)/shard_map/ppermute | solution.py:735
  162.8 76.6 %collective-permute-start.33 = (f32[1,196,512]{2,1,0:T(8,128)}, f32[1,196,512]{2,1,0:T(8,128)}, u32[]{:S(2)}, u32[]{:S(2)}) collective-permute-start(f32[1,196,512]{2,1,0:T(8,128)} %get-tuple-element.173.refs_1_), channel_id=1, source_target_pairs={{0,1},{1,0},{2,3},{3,2},{4,5},{5,4},{6,7},{7,6},{8,9},{9,8},{10,11... | collective-permute-start | bytes 1204232 | tf_op jit(solution)/shard_map/ppermute | solution.py:735
  167.4 71.3 %collective-permute-start.52 = (bf16[2,256,1024]{2,1,0:T(8,128)(2,1)}, bf16[2,256,1024]{2,1,0:T(8,128)(2,1)S(1)}, u32[]{:S(2)}, u32[]{:S(2)}) collective-permute-start(bf16[2,256,1024]{2,1,0:T(8,128)(2,1)} %get-tuple-element.224), channel_id=1, source_target_pairs={{0,1},{1,0},{2,3},{3,2},{4,5},{5,4},{6,7},{7,6},{8,9},{9,8},{10,11... | collective-permute-start | bytes 3145736 | tf_op jit(solution)/shard_map/ppermute | solution.py:735
  185.5 19.1 %collective-permute-start.50 = (bf16[2,256,512]{2,1,0:T(8,128)(2,1)}, bf16[2,256,512]{2,1,0:T(8,128)(2,1)S(1)}, u32[]{:S(2)}, u32[]{:S(2)}) collective-permute-start(bf16[2,256,512]{2,1,0:T(8,128)(2,1)} %get-tuple-element.213), channel_id=1, source_target_pairs={{0,1},{1,0},{2,3},{3,2},{4,5},{5,4},{6,7},{7,6},{8,9},{9,8},{10,11... | collective-permute-start | bytes 1572872 | tf_op jit(solution)/shard_map/ppermute | solution.py:735
  204.6 60.2 %collective-permute-start.45 = (bf16[2,256,1024]{2,1,0:T(8,128)(2,1)}, bf16[2,256,1024]{2,1,0:T(8,128)(2,1)S(1)}, u32[]{:S(2)}, u32[]{:S(2)}) collective-permute-start(bf16[2,256,1024]{2,1,0:T(8,128)(2,1)} %get-tuple-element.206), channel_id=1, source_target_pairs={{0,1},{1,0},{2,3},{3,2},{4,5},{5,4},{6,7},{7,6},{8,9},{9,8},{10,11... | collective-permute-start | bytes 3145736 | tf_op jit(solution)/shard_map/ppermute | solution.py:735
  238.7 20.8 %collective-permute-start.40 = (bf16[2,256,512]{2,1,0:T(8,128)(2,1)}, bf16[2,256,512]{2,1,0:T(8,128)(2,1)}, u32[]{:S(2)}, u32[]{:S(2)}) collective-permute-start(bf16[2,256,512]{2,1,0:T(8,128)(2,1)} %get-tuple-element.199), channel_id=1, source_target_pairs={{0,1},{1,0},{2,3},{3,2},{4,5},{5,4},{6,7},{7,6},{8,9},{9,8},{10,11... | collective-permute-start | bytes 1572872 | tf_op jit(solution)/shard_map/ppermute | solution.py:735
  239.5 23.2 %collective-permute-start.53 = (bf16[256,1024]{1,0:T(8,128)(2,1)S(1)}, bf16[256,1024]{1,0:T(8,128)(2,1)}, u32[]{:S(2)}, u32[]{:S(2)}) collective-permute-start(bf16[256,1024]{1,0:T(8,128)(2,1)S(1)} %fusion.8), channel_id=1, source_target_pairs={{0,4},{4,0},{1,5},{5,1},{2,6},{6,2},{3,7},{7,3},{8,12},{12,8},{9,1... | collective-permute-start | bytes 1572872 | tf_op jit(solution)/shard_map/ppermute | solution.py:735
  246.4 57.7 %collective-permute-start.39 = (f32[2,196,512]{2,0,1:T(2,128)S(1)}, f32[2,196,512]{2,0,1:T(2,128)S(1)}, u32[]{:S(2)}, u32[]{:S(2)}) collective-permute-start(f32[2,196,512]{2,0,1:T(2,128)S(1)} %copy.79), channel_id=1, source_target_pairs={{0,1},{1,0},{2,3},{3,2},{4,5},{5,4},{6,7},{7,6},{8,9},{9,8},{10,11... | collective-permute-start | bytes 2408456 | tf_op jit(solution)/shard_map/ppermute | solution.py:735
  254.5 26.7 %collective-permute-start.60 = (f32[24,512]{1,0:T(8,128)S(1)}, f32[24,512]{1,0:T(8,128)S(1)}, u32[]{:S(2)}, u32[]{:S(2)}) collective-permute-start(f32[24,512]{1,0:T(8,128)S(1)} %add.188), channel_id=1, source_target_pairs={{0,16},{8,24},{16,0},{24,8},{1,17},{9,25},{17,1},{25,9},{2,18},{10... | collective-permute-start | bytes 147464 | tf_op jit(solution)/shard_map/ppermute | solution.py:744
  259.5 24.1 %collective-permute-start.61 = (f32[24,512]{1,0:T(8,128)S(1)}, f32[24,512]{1,0:T(8,128)S(1)}, u32[]{:S(2)}, u32[]{:S(2)}) collective-permute-start(f32[24,512]{1,0:T(8,128)S(1)} %add.188), channel_id=1, source_target_pairs={{0,24},{8,16},{16,8},{24,0},{1,25},{9,17},{17,9},{25,1},{2,26},{10... | collective-permute-start | bytes 147464 | tf_op jit(solution)/shard_map/ppermute | solution.py:744
  290.5 22.0 %collective-permute-start.43 = (bf16[64,512]{1,0:T(8,128)(2,1)S(1)}, bf16[64,512]{1,0:T(8,128)(2,1)S(1)}, u32[]{:S(2)}, u32[]{:S(2)}) collective-permute-start(bf16[64,512]{1,0:T(8,128)(2,1)S(1)} %get-tuple-element.281), channel_id=1, source_target_pairs={{0,16},{8,24},{16,0},{24,8},{1,17},{9,25},{17,1},{25,9},{2,18},{10... | collective-permute-start | bytes 196616 | tf_op jit(solution)/shard_map/ppermute | solution.py:744
  (111 other events, 1157.5 us)
